TPU v7x, 1024 devices: a whole 4x4x32 slice. The times are simulated.
1024 devices in a mesh: depth: 32 (over z), rows: 32 (over x, y, core).
Axes of the slice: x: 4, y: 4, z: 32, core: 2. Of those that a mesh axis runs over, the one named last changes fastest.
Arguments:
- fuel: float32 [128, 256, 512], P('depth', 'rows'), may hold values from -6 to 6
- heat: float32 [128, 256, 512], P('depth', 'rows'), may hold values from -6 to 6
- kappa: float32 [128, 256, 512], P('depth', 'rows'), may hold values from 0.02 to 0.15
- vel_z: float32 [128, 256, 512], P('depth', 'rows'), may hold values from -0.4 to 0.4
- vel_y: float32 [128, 256, 512], P('depth', 'rows'), may hold values from -0.4 to 0.4
- tf_centre: float32 [8], replicated, may hold values from -1.5 to 1.5
- tf_width: float32 [8], replicated, may hold values from 0.4 to 1.5
- tf_density: float32 [8], replicated, may hold values from 0.5 to 4
- tf_tint: float32 [8, 3], replicated, may hold values from -2 to 2
Outputs:
- picture: float32 [8, 4, 256, 512], P(None, None, 'rows', 'depth')
All inputs are finite; a program needn't handle non-finite values.
Results may differ from a plain program's by a relative error of at most 0.000022.
Values sent between devices are 32-bit elements; how exact they have to be, the bound alone decides.
No kernel may reach another device: no remote copies, remote signals or barrier semaphores. Data moves between devices by JAX's collectives and lax.ppermute only.
A program may use at most 32 MiB of HBM per device.

v0:
```python
import jax
import jax.numpy as jnp
from jax import lax
from jax.sharding import PartitionSpec as P

time_step = 1.0
lewis_ratio = 0.8
heat_release = 0.6
burn_rate = 0.5


def with_halo(block, sides, width):
    for axis, dim in sides:
        count = lax.axis_size(axis)
        forward = [(i, i + 1) for i in range(count - 1)]
        backward = [(target, source) for source, target in forward]
        low = lax.ppermute(
            lax.slice_in_dim(block, block.shape[dim] - width, None, axis=dim), axis, forward
        )
        high = lax.ppermute(lax.slice_in_dim(block, 0, width, axis=dim), axis, backward)
        block = jnp.concatenate([low, block, high], axis=dim)
    return block


def stencil_core(padded, vel_z, vel_y):
    centre = padded[1:-1, 1:-1, 1:-1]
    neighbours = padded[2:, 1:-1, 1:-1] + padded[:-2, 1:-1, 1:-1]
    neighbours = neighbours + padded[1:-1, 2:, 1:-1] + padded[1:-1, :-2, 1:-1]
    neighbours = neighbours + padded[1:-1, 1:-1, 2:] + padded[1:-1, 1:-1, :-2]
    transport = vel_z * (padded[2:, 1:-1, 1:-1] - padded[:-2, 1:-1, 1:-1]) * 0.5
    transport = transport + vel_y * (padded[1:-1, 2:, 1:-1] - padded[1:-1, :-2, 1:-1]) * 0.5
    return (centre, neighbours - 6.0 * centre, transport)


def stencil_parts(field, vel_z, vel_y):
    return stencil_core(jnp.pad(field, ((0, 0), (0, 0), (1, 1))), vel_z, vel_y)


def combine_rates(fuel_parts, heat_parts, kappa):
    fuel_mid, fuel_lap, fuel_adv = fuel_parts
    heat_mid, heat_lap, heat_adv = heat_parts
    burning = burn_rate * fuel_mid * heat_mid * heat_mid / (1.0 + heat_mid * heat_mid)
    return (
        lewis_ratio * kappa * fuel_lap - fuel_adv - burning,
        kappa * heat_lap - heat_adv + heat_release * burning,
    )


def tendency(fuel_wide, heat_wide, kappa, vel_z, vel_y):
    return combine_rates(
        stencil_parts(fuel_wide, vel_z, vel_y), stencil_parts(heat_wide, vel_z, vel_y), kappa
    )


def shade_core(padded):
    grad_z = (padded[2:, 1:-1, 1:-1] - padded[:-2, 1:-1, 1:-1]) * 0.5
    grad_y = (padded[1:-1, 2:, 1:-1] - padded[1:-1, :-2, 1:-1]) * 0.5
    grad_x = (padded[1:-1, 1:-1, 2:] - padded[1:-1, 1:-1, :-2]) * 0.5
    norm_sq = grad_z * grad_z + grad_y * grad_y + grad_x * grad_x + 1.0
    facing = (0.48 * grad_z + 0.6 * grad_y + 0.64 * grad_x) / jnp.sqrt(norm_sq)
    return 0.35 + 0.65 * facing * facing


def shading(framed):
    return shade_core(jnp.pad(framed, ((0, 0), (0, 0), (1, 1))))


def march(level, fuel_now, lighting, tf_centre, tf_width, tf_density, tf_tint, opacity_scale):
    functions = tf_centre.shape[0]
    start_state = (
        jnp.zeros((functions, 3) + level.shape[1:], jnp.float32),
        jnp.ones((functions,) + level.shape[1:], jnp.float32),
    )

    def plane(state_pair, plane_data):
        colour, passing = state_pair
        level_plane, fuel_plane, light_plane = plane_data
        offset = (level_plane[None] - tf_centre[:, None, None]) / tf_width[:, None, None]
        extinct = tf_density[:, None, None] * jnp.exp(-offset * offset) * opacity_scale
        survive = jnp.exp(-extinct)
        tinted = jax.nn.sigmoid(tf_tint[:, :, None, None] * fuel_plane[None, None])
        emitted = ((1.0 - survive) * light_plane[None])[:, None] * tinted
        return ((colour + passing[:, None] * emitted, passing * survive), None)

    (colour, passing), unused = lax.scan(plane, start_state, (level, fuel_now, lighting))
    return (colour, passing)


def margin(stacked):
    return with_halo(stacked, (("depth", 1), ("rows", 2)), 1)


def fold_front(pieces):
    shades, passes = pieces
    while shades.shape[0] > 1:
        pieces_now = shades.shape[0]
        half_count = pieces_now // 2
        front_c = shades[0 : 2 * half_count : 2]
        back_c = shades[1 : 2 * half_count : 2]
        front_t = passes[0 : 2 * half_count : 2]
        back_t = passes[1 : 2 * half_count : 2]
        new_shades = front_c + front_t * back_c
        new_passes = front_t * back_t
        shades, passes = (new_shades, new_passes)
    return jnp.concatenate([shades[0], passes[0]], axis=1)


def native_layout(fuel, heat, kappa, vel_z, vel_y, tf_centre, tf_width, tf_density, tf_tint):
    depth_count = lax.axis_size("depth")
    planes = fuel.shape[0]
    nz_total = planes * depth_count
    padded = margin(jnp.stack([fuel, heat]))
    rate_u, rate_v = tendency(padded[0], padded[1], kappa, vel_z, vel_y)
    first_u = fuel + time_step * rate_u
    first_v = heat + time_step * rate_v
    padded = margin(jnp.stack([first_u, first_v]))
    rate_u, rate_v = tendency(padded[0], padded[1], kappa, vel_z, vel_y)
    final_u = 0.5 * (fuel + first_u + time_step * rate_u)
    final_v = 0.5 * (heat + first_v + time_step * rate_v)
    framed = with_halo(final_v, (("depth", 0), ("rows", 1)), 1)
    lighting = shading(framed)
    colour, passing = march(
        framed[1:-1, 1:-1],
        final_u,
        lighting,
        tf_centre,
        tf_width,
        tf_density,
        tf_tint,
        4.0 / nz_total,
    )
    passing = passing[:, None]
    picture = fold_front(
        (
            lax.all_to_all(colour[None], "depth", split_axis=4, concat_axis=0, tiled=True),
            lax.all_to_all(passing[None], "depth", split_axis=4, concat_axis=0, tiled=True),
        )
    )
    return picture


def body(fuel, heat, kappa, vel_z, vel_y, tf_centre, tf_width, tf_density, tf_tint):
    picture = native_layout(
        fuel, heat, kappa, vel_z, vel_y, tf_centre, tf_width, tf_density, tf_tint
    )
    return picture


def solution(mesh):
    placed = (
        P("depth", "rows", None),
        P("depth", "rows", None),
        P("depth", "rows", None),
        P("depth", "rows", None),
        P("depth", "rows", None),
        P(),
        P(),
        P(),
        P(),
    )
    return jax.shard_map(
        body, mesh=mesh, in_specs=placed, out_specs=P(None, None, "rows", "depth"), check_vma=False
    )
```

profile of v0, /device:TPU:6, one launch (start us, length us, event | category | flops | bytes accessed | tf_op | source)
XLA Modules:
  0.0 225.1 jit_solution(10075458054266632198)
XLA Ops:
  0.8 3.8 %collective-permute-start = (f32[2,1,8,512]{3,2,1,0:T(8,128)S(1)}, f32[2,1,8,512]{3,2,1,0:T(8,128)S(1)}, u32[]{:S(2)}, u32[]{:S(2)}) collective-permute-start(f32[2,1,8,512]{3,2,1,0:T(8,128)S(1)} %get-tuple-element.178), channel_id=1, source_target_pairs={{0,32},{32,64},{64,96},{96,128},{128,160},{160,192},{192,224},{224... | collective-permute-start | bytes 98312 | tf_op jit(solution)/shard_map/ppermute | solution.py:17
  6.2 4.2 %collective-permute-done.1 = f32[2,1,8,512]{3,2,1,0:T(8,128)S(1)} collective-permute-done((f32[2,1,8,512]{3,2,1,0:T(8,128)S(1)}, f32[2,1,8,512]{3,2,1,0:T(8,128)S(1)}, u32[]{:S(2)}, u32[]{:S(2)}) %collective-permute-start.1) | collective-permute-done | bytes 32800 | tf_op jit(solution)/shard_map/ppermute | solution.py:20
  13.3 5.8 %collective-permute-start.3 = (f32[2,6,1,512]{3,2,1,0:T(1,128)S(1)}, f32[2,6,1,512]{3,2,1,0:T(1,128)S(1)}, u32[]{:S(2)}, u32[]{:S(2)}) collective-permute-start(f32[2,6,1,512]{3,2,1,0:T(1,128)S(1)} %get-tuple-element.173), channel_id=1, source_target_pairs={{1,0},{2,1},{3,2},{4,3},{5,4},{6,5},{7,6},{8,7},{9,8},{10,9},{11,1... | collective-permute-start | bytes 73736 | tf_op jit(solution)/shard_map/ppermute | solution.py:20
  22.8 3.8 %collective-permute-start.4 = (f32[2,1,8,512]{3,2,1,0:T(8,128)S(1)}, f32[2,1,8,512]{3,2,1,0:T(8,128)S(1)}, u32[]{:S(2)}, u32[]{:S(2)}) collective-permute-start(f32[2,1,8,512]{3,2,1,0:T(8,128)S(1)} %get-tuple-element.176), channel_id=1, source_target_pairs={{0,32},{32,64},{64,96},{96,128},{128,160},{160,192},{192,224},{224... | collective-permute-start | bytes 98312 | tf_op jit(solution)/shard_map/ppermute | solution.py:17
  28.2 5.2 %collective-permute-done.5 = f32[2,1,8,512]{3,2,1,0:T(8,128)S(1)} collective-permute-done((f32[2,1,8,512]{3,2,1,0:T(8,128)S(1)}, f32[2,1,8,512]{3,2,1,0:T(8,128)S(1)}, u32[]{:S(2)}, u32[]{:S(2)}) %collective-permute-start.5) | collective-permute-done | bytes 32800 | tf_op jit(solution)/shard_map/ppermute | solution.py:20
  35.5 5.9 %collective-permute-start.7 = (f32[2,6,1,512]{3,2,1,0:T(1,128)S(1)}, f32[2,6,1,512]{3,2,1,0:T(1,128)S(1)}, u32[]{:S(2)}, u32[]{:S(2)}) collective-permute-start(f32[2,6,1,512]{3,2,1,0:T(1,128)S(1)} %get-tuple-element.171), channel_id=1, source_target_pairs={{1,0},{2,1},{3,2},{4,3},{5,4},{6,5},{7,6},{8,7},{9,8},{10,9},{11,1... | collective-permute-start | bytes 73736 | tf_op jit(solution)/shard_map/ppermute | solution.py:20
  44.5 5.8 %collective-permute-start.9 = (f32[1,8,512]{2,1,0:T(8,128)S(1)}, f32[1,8,512]{2,1,0:T(8,128)S(1)}, u32[]{:S(2)}, u32[]{:S(2)}) collective-permute-start(f32[1,8,512]{2,1,0:T(8,128)S(1)} %get-tuple-element.184), channel_id=1, source_target_pairs={{0,32},{32,64},{64,96},{96,128},{128,160},{160,192},{192,224},{224... | collective-permute-start | bytes 49160 | tf_op jit(solution)/shard_map/ppermute | solution.py:17
  51.7 4.9 %collective-permute-start.10 = (f32[6,1,512]{2,1,0:T(1,128)S(1)}, f32[6,1,512]{2,1,0:T(1,128)S(1)}, u32[]{:S(2)}, u32[]{:S(2)}) collective-permute-start(f32[6,1,512]{2,1,0:T(1,128)S(1)} %get-tuple-element.181), channel_id=1, source_target_pairs={{1,0},{2,1},{3,2},{4,3},{5,4},{6,5},{7,6},{8,7},{9,8},{10,9},{11,1... | collective-permute-start | bytes 36872 | tf_op jit(solution)/shard_map/ppermute | solution.py:20
  56.6 1.9 collective-permute-start.11
  58.6 5.0 %collective-permute-done.11 = f32[6,1,512]{2,1,0:T(1,128)S(1)} collective-permute-done((f32[6,1,512]{2,1,0:T(1,128)S(1)}, f32[6,1,512]{2,1,0:T(1,128)S(1)}, u32[]{:S(2)}, u32[]{:S(2)}) %collective-permute-start.11) | collective-permute-done | bytes 12320 | tf_op jit(solution)/shard_map/ppermute | solution.py:17
  68.0 3.3 %reshape.20 = f32[32,1,1024]{2,1,0:T(1,128)} reshape(f32[512,1,1,8,8]{4,3,2,1,0:T(8,128)} %bitcast_bitcast_fusion.1) | data formatting | bytes 262144
  71.4 29.2 %all-to-all-start.1 = ((f32[32,1,1024]{2,1,0:T(1,128)}), f32[32,1,1024]{2,1,0:T(1,128)S(1)}, u32[]{:S(2)}, u32[]{:S(2)}) async-start(f32[32,1,1024]{2,1,0:T(1,128)} %reshape.20), calls=%async_computation.1 | async-start | bytes 262144 | tf_op jit(solution)/shard_map/all_to_all | solution.py:136
  100.6 4.1 %copy.28 = f32[8,3,8,512]{2,0,1,3:T(8,128)} copy(f32[8,3,8,512]{3,2,1,0:T(8,128)S(1)} %get-tuple-element.58) | data formatting | bytes 786432 | tf_op jit(solution)/shard_map/while | solution.py:85
  104.7 5.8 %bitcast_bitcast_fusion = f32[512,1,3,8,8]{4,3,2,1,0:T(8,128)} fusion(f32[8,3,8,512]{2,0,1,3:T(8,128)} %copy.28), kind=kLoop, calls=%fused_computation.115 | loop fusion | bytes 786432
  110.6 6.1 %reshape.22 = f32[32,1,3072]{2,1,0:T(1,128)} reshape(f32[512,1,3,8,8]{4,3,2,1,0:T(8,128)} %bitcast_bitcast_fusion) | data formatting | bytes 786432
  116.7 11.4 %all-to-all-done.1 = f32[32,1,1024]{2,1,0:T(1,128)S(1)} async-done(((f32[32,1,1024]{2,1,0:T(1,128)}), f32[32,1,1024]{2,1,0:T(1,128)S(1)}, u32[]{:S(2)}, u32[]{:S(2)}) %all-to-all-start.1) | async-done | bytes 131104 | tf_op jit(solution)/shard_map/all_to_all | solution.py:136
  128.1 10.7 %all-to-all-start = ((f32[32,1,3072]{2,1,0:T(1,128)}), f32[32,1,3072]{2,1,0:T(1,128)}, u32[]{:S(2)}, u32[]{:S(2)}) async-start(f32[32,1,3072]{2,1,0:T(1,128)} %reshape.22), calls=%async_computation | async-start | bytes 786432 | tf_op jit(solution)/shard_map/all_to_all | solution.py:135
  146.1 41.9 %all-to-all-done = f32[32,1,3072]{2,1,0:T(1,128)} async-done(((f32[32,1,3072]{2,1,0:T(1,128)}), f32[32,1,3072]{2,1,0:T(1,128)}, u32[]{:S(2)}, u32[]{:S(2)}) %all-to-all-start) | async-done | bytes 393248 | tf_op jit(solution)/shard_map/all_to_all | solution.py:135
  188.1 2.5 %reduce.1 = f32[32,3072]{1,0:T(8,128)S(1)} reduce(f32[32,1,3072]{2,1,0:T(1,128)} %all-to-all-done, f32[]{:T(128)} %broadcast.156), dimensions={1}, to_apply=%all_to_all.26.reduce_sub_computation | reduce | bytes 786436 | tf_op jit(solution)/shard_map/all_to_all | solution.py:135
  190.5 5.1 %reshape.23 = f32[512,1,3,8,8]{4,3,2,1,0:T(8,128)} reshape(f32[32,3072]{1,0:T(8,128)S(1)} %reduce.1) | data formatting | bytes 786432
  195.7 5.2 %copy.37 = f32[1,8,3,8,32,16]{5,4,3,2,1,0:T(8,128)S(1)} copy(f32[1,8,3,8,32,16]{3,1,2,5,4,0:T(8,128)} %bitcast.61) | data formatting | bytes 786432 | tf_op jit(solution)/shard_map/all_to_all | solution.py:135
  200.8 7.7 %slice.310 = f32[16,8,3,8,16]{4,0,3,2,1:T(8,128)} slice(f32[32,8,3,8,16]{4,0,3,2,1:T(8,128)S(1)} %bitcast.62), slice={[0:32:2], [0:8:1], [0:3:1], [0:8:1], [0:16:1]} | slice | bytes 393216 | tf_op jit(solution)/shard_map/slice | solution.py:98
  208.6 7.7 %slice.312 = f32[16,8,3,8,16]{4,0,3,2,1:T(8,128)} slice(f32[32,8,3,8,16]{4,0,3,2,1:T(8,128)S(1)} %bitcast.63), slice={[1:32:2], [0:8:1], [0:3:1], [0:8:1], [0:16:1]} | slice | bytes 393216 | tf_op jit(solution)/shard_map/slice | solution.py:99
  216.3 2.3 %multiply_add_fusion = f32[16,8,3,8,16]{4,0,3,2,1:T(8,128)S(1)} fusion(f32[16,8,3,8,16]{4,0,3,2,1:T(8,128)} %slice.310, f32[16,8,3,8,16]{4,0,3,2,1:T(8,128)} %slice.312, f32[16,8,8,16]{3,0,2,1:T(8,128)} %copy.33), kind=kLoop, calls=%fused_computation.13 | loop fusion | flops 98304 | bytes 655360 | tf_op jit(solution)/shard_map/add | solution.py:102
  (101 shorter events, 36.4 us)
Async XLA Ops:
  0.8 5.4 %collective-permute-start = (f32[2,1,8,512]{3,2,1,0:T(8,128)S(1)}, f32[2,1,8,512]{3,2,1,0:T(8,128)S(1)}, u32[]{:S(2)}, u32[]{:S(2)}) collective-permute-start(f32[2,1,8,512]{3,2,1,0:T(8,128)S(1)} %get-tuple-element.178), channel_id=1, source_target_pairs={{0,32},{32,64},{64,96},{96,128},{128,160},{160,192},{192,224},{224... | collective-permute-start | bytes 98312 | tf_op jit(solution)/shard_map/ppermute | solution.py:17
  4.6 5.8 %collective-permute-start.1 = (f32[2,1,8,512]{3,2,1,0:T(8,128)S(1)}, f32[2,1,8,512]{3,2,1,0:T(8,128)S(1)}, u32[]{:S(2)}, u32[]{:S(2)}) collective-permute-start(f32[2,1,8,512]{3,2,1,0:T(8,128)S(1)} %get-tuple-element.179), channel_id=1, source_target_pairs={{32,0},{64,32},{96,64},{128,96},{160,128},{192,160},{224,192},{256... | collective-permute-start | bytes 98312 | tf_op jit(solution)/shard_map/ppermute | solution.py:20
  11.4 7.7 %collective-permute-start.2 = (f32[2,6,1,512]{3,2,1,0:T(1,128)S(1)}, f32[2,6,1,512]{3,2,1,0:T(1,128)S(1)}, u32[]{:S(2)}, u32[]{:S(2)}) collective-permute-start(f32[2,6,1,512]{3,2,1,0:T(1,128)S(1)} %get-tuple-element.172), channel_id=1, source_target_pairs={{0,1},{1,2},{2,3},{3,4},{4,5},{5,6},{6,7},{7,8},{8,9},{9,10},{10,1... | collective-permute-start | bytes 73736 | tf_op jit(solution)/shard_map/ppermute | solution.py:17
  13.3 7.3 %collective-permute-start.3 = (f32[2,6,1,512]{3,2,1,0:T(1,128)S(1)}, f32[2,6,1,512]{3,2,1,0:T(1,128)S(1)}, u32[]{:S(2)}, u32[]{:S(2)}) collective-permute-start(f32[2,6,1,512]{3,2,1,0:T(1,128)S(1)} %get-tuple-element.173), channel_id=1, source_target_pairs={{1,0},{2,1},{3,2},{4,3},{5,4},{6,5},{7,6},{8,7},{9,8},{10,9},{11,1... | collective-permute-start | bytes 73736 | tf_op jit(solution)/shard_map/ppermute | solution.py:20
  21.5 21.5 %copy-start = (f32[4,8,512]{2,1,0:T(8,128)S(1)}, f32[4,8,512]{2,1,0:T(8,128)}, u32[]{:S(2)}) copy-start(f32[4,8,512]{2,1,0:T(8,128)} %param.12) | copy-start | bytes 196612
  21.5 21.5 %copy-start.3 = (f32[4,8,512]{2,1,0:T(8,128)S(1)}, f32[4,8,512]{2,1,0:T(8,128)}, u32[]{:S(2)}) copy-start(f32[4,8,512]{2,1,0:T(8,128)} %param.13) | copy-start | bytes 196612
  21.5 21.5 %copy-start.4 = (f32[4,8,512]{2,1,0:T(8,128)S(1)}, f32[4,8,512]{2,1,0:T(8,128)}, u32[]{:S(2)}) copy-start(f32[4,8,512]{2,1,0:T(8,128)} %param.15) | copy-start | bytes 196612
  21.5 21.5 %copy-start.5 = (f32[4,8,512]{2,1,0:T(8,128)S(1)}, f32[4,8,512]{2,1,0:T(8,128)}, u32[]{:S(2)}) copy-start(f32[4,8,512]{2,1,0:T(8,128)} %param.14) | copy-start | bytes 196612
  21.6 28.7 %copy-start.12 = (f32[8,3]{0,1:T(4,128)S(1)}, f32[8,3]{0,1:T(4,128)}, u32[]{:S(2)}) copy-start(f32[8,3]{0,1:T(4,128)} %param.19) | copy-start | bytes 292
  21.6 36.9 %copy-start.1 = (f32[4,8,512]{2,1,0:T(8,128)S(1)}, f32[4,8,512]{2,1,0:T(8,128)}, u32[]{:S(2)}) copy-start(f32[4,8,512]{2,1,0:T(8,128)} %param.11) | copy-start | bytes 196612
  22.8 5.4 %collective-permute-start.4 = (f32[2,1,8,512]{3,2,1,0:T(8,128)S(1)}, f32[2,1,8,512]{3,2,1,0:T(8,128)S(1)}, u32[]{:S(2)}, u32[]{:S(2)}) collective-permute-start(f32[2,1,8,512]{3,2,1,0:T(8,128)S(1)} %get-tuple-element.176), channel_id=1, source_target_pairs={{0,32},{32,64},{64,96},{96,128},{128,160},{160,192},{192,224},{224... | collective-permute-start | bytes 98312 | tf_op jit(solution)/shard_map/ppermute | solution.py:17
  26.7 6.8 %collective-permute-start.5 = (f32[2,1,8,512]{3,2,1,0:T(8,128)S(1)}, f32[2,1,8,512]{3,2,1,0:T(8,128)S(1)}, u32[]{:S(2)}, u32[]{:S(2)}) collective-permute-start(f32[2,1,8,512]{3,2,1,0:T(8,128)S(1)} %get-tuple-element.177), channel_id=1, source_target_pairs={{32,0},{64,32},{96,64},{128,96},{160,128},{192,160},{224,192},{256... | collective-permute-start | bytes 98312 | tf_op jit(solution)/shard_map/ppermute | solution.py:20
  33.5 7.9 %collective-permute-start.6 = (f32[2,6,1,512]{3,2,1,0:T(1,128)S(1)}, f32[2,6,1,512]{3,2,1,0:T(1,128)S(1)}, u32[]{:S(2)}, u32[]{:S(2)}) collective-permute-start(f32[2,6,1,512]{3,2,1,0:T(1,128)S(1)} %get-tuple-element.170), channel_id=1, source_target_pairs={{0,1},{1,2},{2,3},{3,4},{4,5},{5,6},{6,7},{7,8},{8,9},{9,10},{10,1... | collective-permute-start | bytes 73736 | tf_op jit(solution)/shard_map/ppermute | solution.py:17
  35.4 28.6 %copy-start.9 = (f32[8]{0:T(128)S(1)}, f32[8]{0:T(128)}, u32[]{:S(2)}) copy-start(f32[8]{0:T(128)} %param.18) | copy-start | bytes 100
  35.5 28.6 %copy-start.10 = (f32[8]{0:T(128)S(1)}, f32[8]{0:T(128)}, u32[]{:S(2)}) copy-start(f32[8]{0:T(128)} %param.16) | copy-start | bytes 100
  35.5 28.6 %copy-start.11 = (f32[8]{0:T(128)S(1)}, f32[8]{0:T(128)}, u32[]{:S(2)}) copy-start(f32[8]{0:T(128)} %param.17) | copy-start | bytes 100
  35.5 7.4 %collective-permute-start.7 = (f32[2,6,1,512]{3,2,1,0:T(1,128)S(1)}, f32[2,6,1,512]{3,2,1,0:T(1,128)S(1)}, u32[]{:S(2)}, u32[]{:S(2)}) collective-permute-start(f32[2,6,1,512]{3,2,1,0:T(1,128)S(1)} %get-tuple-element.171), channel_id=1, source_target_pairs={{1,0},{2,1},{3,2},{4,3},{5,4},{6,5},{7,6},{8,7},{9,8},{10,9},{11,1... | collective-permute-start | bytes 73736 | tf_op jit(solution)/shard_map/ppermute | solution.py:20
  43.2 7.2 %collective-permute-start.8 = (f32[1,8,512]{2,1,0:T(8,128)S(1)}, f32[1,8,512]{2,1,0:T(8,128)S(1)}, u32[]{:S(2)}, u32[]{:S(2)}) collective-permute-start(f32[1,8,512]{2,1,0:T(8,128)S(1)} %get-tuple-element.185), channel_id=1, source_target_pairs={{32,0},{64,32},{96,64},{128,96},{160,128},{192,160},{224,192},{256... | collective-permute-start | bytes 49160 | tf_op jit(solution)/shard_map/ppermute | solution.py:20
  44.5 7.2 %collective-permute-start.9 = (f32[1,8,512]{2,1,0:T(8,128)S(1)}, f32[1,8,512]{2,1,0:T(8,128)S(1)}, u32[]{:S(2)}, u32[]{:S(2)}) collective-permute-start(f32[1,8,512]{2,1,0:T(8,128)S(1)} %get-tuple-element.184), channel_id=1, source_target_pairs={{0,32},{32,64},{64,96},{96,128},{128,160},{160,192},{192,224},{224... | collective-permute-start | bytes 49160 | tf_op jit(solution)/shard_map/ppermute | solution.py:17
  51.7 7.0 %collective-permute-start.10 = (f32[6,1,512]{2,1,0:T(1,128)S(1)}, f32[6,1,512]{2,1,0:T(1,128)S(1)}, u32[]{:S(2)}, u32[]{:S(2)}) collective-permute-start(f32[6,1,512]{2,1,0:T(1,128)S(1)} %get-tuple-element.181), channel_id=1, source_target_pairs={{1,0},{2,1},{3,2},{4,3},{5,4},{6,5},{7,6},{8,7},{9,8},{10,9},{11,1... | collective-permute-start | bytes 36872 | tf_op jit(solution)/shard_map/ppermute | solution.py:20
  56.6 7.1 %collective-permute-start.11 = (f32[6,1,512]{2,1,0:T(1,128)S(1)}, f32[6,1,512]{2,1,0:T(1,128)S(1)}, u32[]{:S(2)}, u32[]{:S(2)}) collective-permute-start(f32[6,1,512]{2,1,0:T(1,128)S(1)} %get-tuple-element.180), channel_id=1, source_target_pairs={{0,1},{1,2},{2,3},{3,4},{4,5},{5,6},{6,7},{7,8},{8,9},{9,10},{10,1... | collective-permute-start | bytes 36872 | tf_op jit(solution)/shard_map/ppermute | solution.py:17
  71.4 56.8 %all-to-all-start.1 = ((f32[32,1,1024]{2,1,0:T(1,128)}), f32[32,1,1024]{2,1,0:T(1,128)S(1)}, u32[]{:S(2)}, u32[]{:S(2)}) async-start(f32[32,1,1024]{2,1,0:T(1,128)} %reshape.20), calls=%async_computation.1 | async-start | bytes 262144 | tf_op jit(solution)/shard_map/all_to_all | solution.py:136
  128.1 59.9 %all-to-all-start = ((f32[32,1,3072]{2,1,0:T(1,128)}), f32[32,1,3072]{2,1,0:T(1,128)}, u32[]{:S(2)}, u32[]{:S(2)}) async-start(f32[32,1,3072]{2,1,0:T(1,128)} %reshape.22), calls=%async_computation | async-start | bytes 786432 | tf_op jit(solution)/shard_map/all_to_all | solution.py:135
  220.0 4.2 %copy-start.7 = (f32[8,8,16]{2,1,0:T(8,128)S(1)}, f32[8,8,16]{2,1,0:T(8,128)}, u32[]{:S(2)}) copy-start(f32[8,8,16]{2,1,0:T(8,128)} %get-tuple-element.182) | copy-start | bytes 12292
  (3 other events, 9.0 us)
where the time goes:
time: 226 us; the launch traced here: 225 us
  starting transfers between devices  79.5 us (35%)
  waiting for transfers between devices  72.7 us (32%)
  local copies, waits for them, and re-layouts  57.8 us (26%)
  other arithmetic  14.3 us (6%)
    all_to_all x1, waiting for transfers between devices, native_layout(): lax.all_to_all(colour[None], 'depth', split_axis=4, concat_axis=0, tiled=...  41.9 us
    all_to_all x1, starting transfers between devices, native_layout(): lax.all_to_all(passing[None], 'depth', split_axis=4, concat_axis=0, tiled...  29.2 us
    unnamed x33, local copies, waits for them, and re-layouts  23.2 us
    ppermute x6, starting transfers between devices, with_halo(): lax.ppermute(lax.slice_in_dim(block, 0, width, axis=dim), axis, backward)  20.4 us
    ppermute x6, starting transfers between devices, with_halo(): lax.ppermute(lax.slice_in_dim(block, block.shape[dim] - width, None, axis...  19.2 us
    ppermute x6, waiting for transfers between devices, with_halo(): lax.ppermute(lax.slice_in_dim(block, 0, width, axis=dim), axis, backward)  12.5 us
    all_to_all x1, waiting for transfers between devices, native_layout(): lax.all_to_all(passing[None], 'depth', split_axis=4, concat_axis=0, tiled...  11.4 us
    all_to_all x1, starting transfers between devices, native_layout(): lax.all_to_all(colour[None], 'depth', split_axis=4, concat_axis=0, tiled=...  10.7 us
  transfers between devices with their start and end apart: 14, of which 10 were waited for; matrix products, arithmetic and copies ran while one was open for 10% of the time, Pallas kernels for 0%

commit v1 on v0

v1 whole, which is shorter than its diff:
```python
import functools

import jax
import jax.numpy as jnp
from jax import lax
from jax.experimental import pallas as pl
from jax.experimental.pallas import tpu as pltpu
from jax.sharding import PartitionSpec as P

time_step = 1.0
lewis_ratio = 0.8
heat_release = 0.6
burn_rate = 0.5

WF = 3
WC = 2

vmem = pl.BlockSpec(memory_space=pltpu.VMEM)
smem = pl.BlockSpec(memory_space=pltpu.SMEM)


def pairs(axis):
    count = lax.axis_size(axis)
    forward = [(i, i + 1) for i in range(count - 1)]
    return forward, [(target, source) for source, target in forward]


def exchange(to_next, to_prev, axis):
    forward, backward = pairs(axis)
    return lax.ppermute(to_next, axis, forward), lax.ppermute(to_prev, axis, backward)


def planes_kernel(fuel, heat, kappa, vel_z, vel_y, to_next, to_prev):
    planes = fuel.shape[0]
    at = 0
    for field, width in ((fuel, WF), (heat, WF), (kappa, WC), (vel_z, WC), (vel_y, WC)):
        to_next[at : at + width] = field[planes - width : planes]
        to_prev[at : at + width] = field[0:width]
        at += width


def deep_planes(fields, low, high):
    planes = fields[0].shape[0]
    at = 0
    columns = []
    for field, width in zip(fields, (WF, WF, WC, WC, WC)):
        column = [(low, at + i) for i in range(width)]
        column += [(field, i) for i in range(planes)]
        column += [(high, at + i) for i in range(width)]
        columns.append((column, width))
        at += width
    return columns


def rows_kernel(fuel, heat, kappa, vel_z, vel_y, low, high, to_next, to_prev):
    rows = fuel.shape[1]
    at = 0
    for column, width in deep_planes((fuel, heat, kappa, vel_z, vel_y), low, high):
        for source, i in column:
            to_next[at : at + width] = source[i, rows - width : rows]
            to_prev[at : at + width] = source[i, 0:width]
            at += width


def side(value, step):
    size = value.shape[1]
    lane = lax.broadcasted_iota(jnp.int32, value.shape, 1)
    if step > 0:
        return jnp.where(lane < size - 1, pltpu.roll(value, size - 1, 1), 0.0)
    return jnp.where(lane > 0, pltpu.roll(value, 1, 1), 0.0)


def above(value):
    return pltpu.roll(value, value.shape[0] - 1, 0)


def below(value):
    return pltpu.roll(value, 1, 0)


def parts(ref, i, vel_z, vel_y):
    centre = ref[i]
    ahead, behind = ref[i + 1], ref[i - 1]
    up, down = above(centre), below(centre)
    near = (ahead + behind) + (up + down) + (side(centre, 1) + side(centre, -1))
    transport = 0.5 * (vel_z * (ahead - behind) + vel_y * (up - down))
    return centre, near - 6.0 * centre, transport


def rates(fuel_ref, heat_ref, i, kappa, vel_z, vel_y, both):
    heat_mid, heat_lap, heat_adv = parts(heat_ref, i, vel_z, vel_y)
    square = heat_mid * heat_mid
    if both:
        fuel_mid, fuel_lap, fuel_adv = parts(fuel_ref, i, vel_z, vel_y)
    else:
        fuel_mid = fuel_ref[i]
    burning = burn_rate * fuel_mid * square / (1.0 + square)
    rate_heat = kappa * heat_lap - heat_adv + heat_release * burning
    if not both:
        return None, rate_heat
    return lewis_ratio * kappa * fuel_lap - fuel_adv - burning, rate_heat


def block_transpose(tile):
    row = lax.broadcasted_iota(jnp.int32, tile.shape, 0)
    block = lax.broadcasted_iota(jnp.int32, tile.shape, 1) // 16
    for bit in (1, 2, 4):
        later = pltpu.roll(pltpu.roll(tile, 8 - bit, 0), 16 * bit, 1)
        earlier = pltpu.roll(pltpu.roll(tile, bit, 0), 128 - 16 * bit, 1)
        row_bit, block_bit = (row & bit) != 0, (block & bit) != 0
        swapped = jnp.where(block_bit, later, earlier)
        tile = jnp.where(row_bit == block_bit, tile, swapped)
    return tile


def step_kernel(
    fuel, heat, kappa, vel_z, vel_y, low, high, row_low, row_high, out,
    fuel_s, heat_s, kappa_s, vel_z_s, vel_y_s, fuel_one, heat_one, heat_two, fuel_two,
):
    planes, rows = fuel.shape[0], fuel.shape[1]
    own = slice(WF, WF + rows)
    at = 0
    whole = (fuel_s, heat_s, kappa_s, vel_z_s, vel_y_s)
    columns = deep_planes((fuel, heat, kappa, vel_z, vel_y), low, high)
    for target, (column, width) in zip(whole, columns):
        for j, (source, i) in enumerate(column):
            target[j, own] = source[i]
            target[j, WF - width : WF] = row_low[at : at + width]
            target[j, WF + rows : WF + rows + width] = row_high[at : at + width]
            at += width

    def first(j, carry):
        rate_fuel, rate_heat = rates(
            fuel_s, heat_s, j + 1, kappa_s[j], vel_z_s[j], vel_y_s[j], True
        )
        fuel_one[j] = fuel_s[j + 1] + time_step * rate_fuel
        heat_one[j] = heat_s[j + 1] + time_step * rate_heat
        return carry

    lax.fori_loop(0, planes + 4, first, 0)

    def second(j, both):
        rate_fuel, rate_heat = rates(
            fuel_one, heat_one, j + 1, kappa_s[j + 1], vel_z_s[j + 1], vel_y_s[j + 1], both
        )
        heat_two[j] = 0.5 * (heat_s[j + 2] + heat_one[j + 1] + time_step * rate_heat)
        if both:
            fuel_two[j] = 0.5 * (fuel_s[j + 2] + fuel_one[j + 1] + time_step * rate_fuel)

    def inner(j, carry):
        second(j, True)
        return carry

    second(0, False)
    lax.fori_loop(1, planes + 1, inner, 0)
    second(planes + 1, False)

    groups = fuel.shape[2] // 128

    def shade(p):
        centre = heat_two[p + 1]
        grad_z = (heat_two[p + 2] - heat_two[p]) * 0.5
        grad_y = (above(centre) - below(centre)) * 0.5
        grad_x = (side(centre, 1) - side(centre, -1)) * 0.5
        norm_sq = grad_z * grad_z + grad_y * grad_y + grad_x * grad_x + 1.0
        facing = 0.48 * grad_z + 0.6 * grad_y + 0.64 * grad_x
        return 0.35 + 0.65 * (facing * facing) / norm_sq

    for p in range(planes):
        light = shade(p)
        for f, value in enumerate((heat_two[p + 1], fuel_two[p + 1], light)):
            value = value[own]
            lanes = slice((f * planes + p) * 128, (f * planes + p + 1) * 128)
            for m in range(groups):
                tile = block_transpose(value[:, m * 128 : (m + 1) * 128])
                for l in range(8):
                    out[8 * m + l, :, lanes] = tile[l : l + 1]


def per_function(ref, *index):
    row = lax.broadcasted_iota(jnp.int32, (8, 128), 0)
    value = jnp.full((8, 128), ref[(0,) + index], jnp.float32)
    for k in range(1, 8):
        value = jnp.where(row == k, ref[(k,) + index], value)
    return value


def march_kernel(opacity_scale, planes, centre, width, density, tint, fields, out):
    mid = per_function(centre)
    inverse = 1.0 / per_function(width)
    thick = per_function(density) * opacity_scale
    half = [0.5 * per_function(tint, c) for c in range(3)]

    def segment(s, state):
        passing, colour = state[0], list(state[1:])
        for p in range(planes):
            level, fuel, light = (
                fields[s, :, (f * planes + p) * 128 : (f * planes + p + 1) * 128]
                for f in range(3)
            )
            offset = (level - mid) * inverse
            survive = jnp.exp(-thick * jnp.exp(-offset * offset))
            weight = passing * (1.0 - survive) * (0.5 * light)
            for c in range(3):
                colour[c] = colour[c] + weight * (1.0 + jnp.tanh(half[c] * fuel))
            passing = passing * survive
        return (passing, *colour)

    zero = jnp.zeros((8, 128), jnp.float32)
    state = lax.fori_loop(0, fields.shape[0], segment, (zero + 1.0, zero, zero, zero))
    for c, value in enumerate((state[1], state[2], state[3], state[0])):
        tile = block_transpose(value)
        for k in range(8):
            out[k, c] = tile[:, 16 * k : 16 * k + 16]


def body(fuel, heat, kappa, vel_z, vel_y, tf_centre, tf_width, tf_density, tf_tint):
    planes, rows, columns = fuel.shape
    depth_count = lax.axis_size("depth")
    fields = (fuel, heat, kappa, vel_z, vel_y)
    f32 = functools.partial(jax.ShapeDtypeStruct, dtype=jnp.float32)
    sent_planes = 2 * WF + 3 * WC
    sent_rows = 2 * WF * (planes + 2 * WF) + 3 * WC * (planes + 2 * WC)

    to_next, to_prev = pl.pallas_call(
        planes_kernel,
        out_shape=[f32((sent_planes, rows, columns))] * 2,
        in_specs=[vmem] * 5,
        out_specs=[vmem] * 2,
        name="pack_planes",
    )(*fields)
    low, high = exchange(to_next, to_prev, "depth")
    to_next, to_prev = pl.pallas_call(
        rows_kernel,
        out_shape=[f32((sent_rows, columns))] * 2,
        in_specs=[vmem] * 7,
        out_specs=[vmem] * 2,
        name="pack_rows",
    )(*fields, low, high)
    row_low, row_high = exchange(to_next, to_prev, "rows")

    tall = rows + 8
    segment = f32((depth_count, 1, 3 * planes * 128))
    scratch = [pltpu.VMEM((planes + 2 * w, tall, columns), jnp.float32) for w in (WF, WF, WC, WC, WC)]
    scratch += [pltpu.VMEM((planes + 4, tall, columns), jnp.float32)] * 2
    scratch += [pltpu.VMEM((planes + 2, tall, columns), jnp.float32)] * 2
    stepped = pl.pallas_call(
        step_kernel,
        out_shape=segment,
        in_specs=[vmem] * 9,
        out_specs=vmem,
        scratch_shapes=scratch,
        name="step",
    )(*fields, low, high, row_low, row_high)

    gathered = lax.all_to_all(stepped, "depth", split_axis=0, concat_axis=0, tiled=True)

    return pl.pallas_call(
        functools.partial(march_kernel, 4.0 / (planes * depth_count), planes),
        out_shape=f32((8, 4, rows, columns // depth_count)),
        in_specs=[smem] * 4 + [vmem],
        out_specs=vmem,
        name="march",
    )(tf_centre, tf_width, tf_density, tf_tint, gathered)


def solution(mesh):
    placed = (P("depth", "rows", None),) * 5 + (P(),) * 4
    return jax.shard_map(
        body, mesh=mesh, in_specs=placed, out_specs=P(None, None, "rows", "depth"), check_vma=False
    )
```

time: 226 us -> 104 us (0.46)
  local copies, waits for them, and re-layouts: 57.8 us -> 2.72 us
  starting transfers between devices: 79.5 us -> 41.3 us
  waiting for transfers between devices: 72.7 us -> 47.3 us
  other arithmetic: 14.3 us -> 0 us
  Pallas kernels: 0 us -> 12.3 us
    ppermute x12 -> x4, starting transfers between devices: 39.6 us -> 12.8 us  [the longest x2 7.04 us: exchange(): lax.ppermute(to_prev, axis, backward)]
    unnamed x33 -> x13, local copies, waits for them, and re-layouts: 23.2 us -> 2.72 us
    slice x9 -> x0, local copies, waits for them, and re-layouts: 19.9 us -> none  [the longest x4 9.93 us: fold_front(): back_c = shades[1:2 * half_count:2]]
    all_to_all x2 -> x1, waiting for transfers between devices: 53.4 us -> 36.2 us  [body(): lax.all_to_all(stepped, 'depth', split_axis=0, concat_axis=0, tiled=True)]
    pallas_call x0 -> x4, Pallas kernels: none -> 12.3 us  [the longest x1 5.47 us: body(): pl.pallas_call(step_kernel, out_shape=segment, in_specs=[vmem] * 9, out_s...]
    all_to_all x2 -> x1, starting transfers between devices: 39.9 us -> 28.5 us  [body(): lax.all_to_all(stepped, 'depth', split_axis=0, concat_axis=0, tiled=True)]
    ppermute x12 -> x4, waiting for transfers between devices: 19.4 us -> 11.2 us  [the longest x2 6.05 us: exchange(): lax.ppermute(to_prev, axis, backward)]
    all_to_all x3 -> x0, local copies, waits for them, and re-layouts: 6.28 us -> none  [the longest x1 5.17 us: native_layout(): lax.all_to_all(colour[None], 'depth', split_axis=4, concat_axis=0, tiled=...]
  transfers between devices with their start and end apart: 14 -> 5, of which waited for: 10 -> 5; matrix products, arithmetic and copies ran while one was open for 10% -> 1% of each run, Pallas kernels for 0% -> 0%
where the time goes in v1:
time: 104 us
  waiting for transfers between devices  47.3 us (45%)
  starting transfers between devices  41.3 us (40%)
  Pallas kernels  12.3 us (12%)
  local copies, waits for them, and re-layouts  2.72 us (3%)
    all_to_all x1, waiting for transfers between devices, body(): lax.all_to_all(stepped, 'depth', split_axis=0, concat_axis=0, tiled=True)  36.2 us
    all_to_all x1, starting transfers between devices, body(): lax.all_to_all(stepped, 'depth', split_axis=0, concat_axis=0, tiled=True)  28.5 us
    ppermute x2, starting transfers between devices, exchange(): lax.ppermute(to_prev, axis, backward)  7.04 us
    ppermute x2, waiting for transfers between devices, exchange(): lax.ppermute(to_prev, axis, backward)  6.05 us
    ppermute x2, starting transfers between devices, exchange(): lax.ppermute(to_next, axis, forward)  5.73 us
    pallas_call x1, Pallas kernels, body(): pl.pallas_call(step_kernel, out_shape=segment, in_specs=[vmem] * 9, out_s...  5.47 us
    ppermute x2, waiting for transfers between devices, exchange(): lax.ppermute(to_next, axis, forward)  5.12 us
    pallas_call x1, Pallas kernels, body(): pl.pallas_call(functools.partial(march_kernel, 4.0 / (planes * depth_coun...  2.94 us
  transfers between devices with their start and end apart: 5, of which 5 were waited for; matrix products, arithmetic and copies ran while one was open for 1% of the time, Pallas kernels for 0%

profile of v1, /device:TPU:6, one launch (start us, length us, event | category | flops | bytes accessed | tf_op | source)
XLA Modules:
  0.0 103.7 jit_solution(17147556683578021979)
XLA Ops:
  0.0 1.7 %pack_planes.1 = (f32[12,8,512]{2,1,0:T(8,128)}, f32[12,8,512]{2,1,0:T(8,128)}) custom-call(f32[4,8,512]{2,1,0:T(8,128)} %fuel.5, f32[4,8,512]{2,1,0:T(8,128)} %heat.5, f32[4,8,512]{2,1,0:T(8,128)} %kappa.5, f32[4,8,512]{2,1,0:T(8,128)} %vel_z.5, f32[4,8,512]{2,1,0:T(8,128)} %vel_y.5), custom_call_target="tpu_custom_call" | custom-call | tf_op jit(solution)/shard_map/pack_planes/pallas_call | solution.py:225
  1.7 3.8 %collective-permute-start = (f32[12,8,512]{2,1,0:T(8,128)}, f32[12,8,512]{2,1,0:T(8,128)S(1)}, u32[]{:S(2)}, u32[]{:S(2)}) collective-permute-start(f32[12,8,512]{2,1,0:T(8,128)} %get-tuple-element.9), channel_id=1, source_target_pairs={{0,32},{32,64},{64,96},{96,128},{128,160},{160,192},{192,224},{224... | collective-permute-start | bytes 589832 | tf_op jit(solution)/shard_map/ppermute | solution.py:30
  5.6 1.3 %collective-permute-start.1 = (f32[12,8,512]{2,1,0:T(8,128)}, f32[12,8,512]{2,1,0:T(8,128)S(1)}, u32[]{:S(2)}, u32[]{:S(2)}) collective-permute-start(f32[12,8,512]{2,1,0:T(8,128)} %get-tuple-element.10), channel_id=1, source_target_pairs={{32,0},{64,32},{96,64},{128,96},{160,128},{192,160},{224,192},{256... | collective-permute-start | bytes 589832 | tf_op jit(solution)/shard_map/ppermute | solution.py:30
  6.9 3.1 %collective-permute-done.low = f32[12,8,512]{2,1,0:T(8,128)S(1)} collective-permute-done((f32[12,8,512]{2,1,0:T(8,128)}, f32[12,8,512]{2,1,0:T(8,128)S(1)}, u32[]{:S(2)}, u32[]{:S(2)}) %collective-permute-start) | collective-permute-done | bytes 196640 | tf_op jit(solution)/shard_map/ppermute | solution.py:30
  10.0 0.0 copy-start.1
  10.0 4.2 %collective-permute-done.1.high = f32[12,8,512]{2,1,0:T(8,128)S(1)} collective-permute-done((f32[12,8,512]{2,1,0:T(8,128)}, f32[12,8,512]{2,1,0:T(8,128)S(1)}, u32[]{:S(2)}, u32[]{:S(2)}) %collective-permute-start.1) | collective-permute-done | bytes 196640 | tf_op jit(solution)/shard_map/ppermute | solution.py:30
  14.2 0.0 copy-done.1
  14.2 0.0 copy-start.2
  14.2 0.7 copy-done.2
  14.9 2.1 %pack_rows.1 = (f32[108,512]{1,0:T(8,128)}, f32[108,512]{1,0:T(8,128)}) custom-call(f32[4,8,512]{2,1,0:T(8,128)} %fuel.5, f32[4,8,512]{2,1,0:T(8,128)} %heat.5, f32[4,8,512]{2,1,0:T(8,128)} %kappa.5, f32[4,8,512]{2,1,0:T(8,128)} %vel_z.5, f32[4,8,512]{2,1,0:T(8,128)} %vel_y.5, f32[12,8,512]{2,1,0:T(8,128)} %copy-done.1, f32[12,8,512]{2,1,0:T(8,128)} %copy-done.2), custom_call_target="tpu_custom_call" | custom-call | tf_op jit(solution)/shard_map/pack_rows/pallas_call | solution.py:233
  17.0 1.9 %collective-permute-start.2 = (f32[108,512]{1,0:T(8,128)}, f32[108,512]{1,0:T(8,128)S(1)}, u32[]{:S(2)}, u32[]{:S(2)}) collective-permute-start(f32[108,512]{1,0:T(8,128)} %get-tuple-element.11), channel_id=1, source_target_pairs={{0,1},{1,2},{2,3},{3,4},{4,5},{5,6},{6,7},{7,8},{8,9},{9,10},{10,1... | collective-permute-start | bytes 663560 | tf_op jit(solution)/shard_map/ppermute | solution.py:30
  18.9 5.8 %collective-permute-start.3 = (f32[108,512]{1,0:T(8,128)}, f32[108,512]{1,0:T(8,128)S(1)}, u32[]{:S(2)}, u32[]{:S(2)}) collective-permute-start(f32[108,512]{1,0:T(8,128)} %get-tuple-element.12), channel_id=1, source_target_pairs={{1,0},{2,1},{3,2},{4,3},{5,4},{6,5},{7,6},{8,7},{9,8},{10,9},{11,1... | collective-permute-start | bytes 663560 | tf_op jit(solution)/shard_map/ppermute | solution.py:30
  24.7 2.0 %collective-permute-done.2.row_low = f32[108,512]{1,0:T(8,128)S(1)} collective-permute-done((f32[108,512]{1,0:T(8,128)}, f32[108,512]{1,0:T(8,128)S(1)}, u32[]{:S(2)}, u32[]{:S(2)}) %collective-permute-start.2) | collective-permute-done | bytes 221216 | tf_op jit(solution)/shard_map/ppermute | solution.py:30
  26.7 0.0 copy-start.3
  26.7 1.9 %collective-permute-done.3.row_high = f32[108,512]{1,0:T(8,128)S(1)} collective-permute-done((f32[108,512]{1,0:T(8,128)}, f32[108,512]{1,0:T(8,128)S(1)}, u32[]{:S(2)}, u32[]{:S(2)}) %collective-permute-start.3) | collective-permute-done | bytes 221216 | tf_op jit(solution)/shard_map/ppermute | solution.py:30
  28.5 0.0 copy-done.3
  28.5 0.7 copy-done.4
  29.2 5.5 %step.1 = f32[32,1,1536]{2,1,0:T(1,128)} custom-call(f32[4,8,512]{2,1,0:T(8,128)} %fuel.5, f32[4,8,512]{2,1,0:T(8,128)} %heat.5, f32[4,8,512]{2,1,0:T(8,128)} %kappa.5, f32[4,8,512]{2,1,0:T(8,128)} %vel_z.5, f32[4,8,512]{2,1,0:T(8,128)} %vel_y.5, f32[12,8,512]{2,1,0:T(8,128)} %copy-done.1, f32[12,8,512]{2,1,0:T(8,128)} %copy-done.2, f32[108,512]{1,0:T(8,128)} %copy-done.3, ...), custom_call_target="tpu_custom_call" | custom-call | tf_op jit(solution)/shard_map/step/pallas_call | solution.py:247
  34.7 28.5 %all-to-all-start = ((f32[32,1,1536]{2,1,0:T(1,128)}), f32[32,1,1536]{2,1,0:T(1,128)S(1)}, u32[]{:S(2)}, u32[]{:S(2)}) async-start(f32[32,1,1536]{2,1,0:T(1,128)} %step.1), calls=%async_computation | async-start | bytes 393216 | tf_op jit(solution)/shard_map/all_to_all | solution.py:256
  63.2 0.0 copy-done.5
  63.2 0.7 copy.10.tint
  63.9 36.2 %all-to-all-done.fields = f32[32,1,1536]{2,1,0:T(1,128)S(1)} async-done(((f32[32,1,1536]{2,1,0:T(1,128)}), f32[32,1,1536]{2,1,0:T(1,128)S(1)}, u32[]{:S(2)}, u32[]{:S(2)}) %all-to-all-start) | async-done | bytes 196640 | tf_op jit(solution)/shard_map/all_to_all | solution.py:256
  100.1 0.7 copy-done
  100.8 2.9 %march.1 = f32[8,4,8,16]{3,2,1,0:T(8,128)} custom-call(f32[8]{0:T(128)} %centre.1, f32[8]{0:T(128)} %width.1, f32[8]{0:T(128)} %density.1, f32[8,3]{1,0:T(8,128)} %copy.10.tint, f32[32,1,1536]{2,1,0:T(1,128)} %copy-done), custom_call_target="tpu_custom_call" | custom-call | tf_op jit(solution)/shard_map/march/pallas_call | solution.py:258
  (3 shorter events, 0.0 us)
Async XLA Ops:
  1.7 8.3 %collective-permute-start = (f32[12,8,512]{2,1,0:T(8,128)}, f32[12,8,512]{2,1,0:T(8,128)S(1)}, u32[]{:S(2)}, u32[]{:S(2)}) collective-permute-start(f32[12,8,512]{2,1,0:T(8,128)} %get-tuple-element.9), channel_id=1, source_target_pairs={{0,32},{32,64},{64,96},{96,128},{128,160},{160,192},{192,224},{224... | collective-permute-start | bytes 589832 | tf_op jit(solution)/shard_map/ppermute | solution.py:30
  5.6 8.6 %collective-permute-start.1 = (f32[12,8,512]{2,1,0:T(8,128)}, f32[12,8,512]{2,1,0:T(8,128)S(1)}, u32[]{:S(2)}, u32[]{:S(2)}) collective-permute-start(f32[12,8,512]{2,1,0:T(8,128)} %get-tuple-element.10), channel_id=1, source_target_pairs={{32,0},{64,32},{96,64},{128,96},{160,128},{192,160},{224,192},{256... | collective-permute-start | bytes 589832 | tf_op jit(solution)/shard_map/ppermute | solution.py:30
  10.0 4.2 %copy-start.1 = (f32[12,8,512]{2,1,0:T(8,128)}, f32[12,8,512]{2,1,0:T(8,128)S(1)}, u32[]{:S(2)}) copy-start(f32[12,8,512]{2,1,0:T(8,128)S(1)} %collective-permute-done.low) | copy-start | bytes 589828
  14.2 0.7 copy-start.2
  17.0 9.6 %collective-permute-start.2 = (f32[108,512]{1,0:T(8,128)}, f32[108,512]{1,0:T(8,128)S(1)}, u32[]{:S(2)}, u32[]{:S(2)}) collective-permute-start(f32[108,512]{1,0:T(8,128)} %get-tuple-element.11), channel_id=1, source_target_pairs={{0,1},{1,2},{2,3},{3,4},{4,5},{5,6},{6,7},{7,8},{8,9},{9,10},{10,1... | collective-permute-start | bytes 663560 | tf_op jit(solution)/shard_map/ppermute | solution.py:30
  18.9 9.6 %collective-permute-start.3 = (f32[108,512]{1,0:T(8,128)}, f32[108,512]{1,0:T(8,128)S(1)}, u32[]{:S(2)}, u32[]{:S(2)}) collective-permute-start(f32[108,512]{1,0:T(8,128)} %get-tuple-element.12), channel_id=1, source_target_pairs={{1,0},{2,1},{3,2},{4,3},{5,4},{6,5},{7,6},{8,7},{9,8},{10,9},{11,1... | collective-permute-start | bytes 663560 | tf_op jit(solution)/shard_map/ppermute | solution.py:30
  26.7 1.9 %copy-start.3 = (f32[108,512]{1,0:T(8,128)}, f32[108,512]{1,0:T(8,128)S(1)}, u32[]{:S(2)}) copy-start(f32[108,512]{1,0:T(8,128)S(1)} %collective-permute-done.2.row_low) | copy-start | bytes 663556
  28.5 0.7 copy-start.4
  34.7 28.5 %copy-start.5 = (f32[8,3]{0,1:T(4,128)S(1)}, f32[8,3]{0,1:T(4,128)}, u32[]{:S(2)}) copy-start(f32[8,3]{0,1:T(4,128)} %param.17) | copy-start | bytes 292
  34.7 65.4 %all-to-all-start = ((f32[32,1,1536]{2,1,0:T(1,128)}), f32[32,1,1536]{2,1,0:T(1,128)S(1)}, u32[]{:S(2)}, u32[]{:S(2)}) async-start(f32[32,1,1536]{2,1,0:T(1,128)} %step.1), calls=%async_computation | async-start | bytes 393216 | tf_op jit(solution)/shard_map/all_to_all | solution.py:256
  100.1 0.7 copy-start

commit v2 on v1

v2 whole, which is shorter than its diff:
```python
import functools

import jax
import jax.numpy as jnp
from jax import lax
from jax.experimental import pallas as pl
from jax.experimental.pallas import tpu as pltpu
from jax.sharding import PartitionSpec as P

time_step = 1.0
lewis_ratio = 0.8
heat_release = 0.6
burn_rate = 0.5

DF = 2
DC = 1
WF = 3
depths = (DF, DF, DC, DC, DC)

vmem = pl.BlockSpec(memory_space=pltpu.VMEM)
smem = pl.BlockSpec(memory_space=pltpu.SMEM)


def pairs(axis):
    count = lax.axis_size(axis)
    forward = [(i, i + 1) for i in range(count - 1)]
    return forward, [(target, source) for source, target in forward]


def exchange(to_next, to_prev, axis):
    forward, backward = pairs(axis)
    return lax.ppermute(to_next, axis, forward), lax.ppermute(to_prev, axis, backward)


def params(**more):
    return pltpu.CompilerParams(vmem_limit_bytes=8 << 20, **more)


def planes_kernel(fuel, heat, kappa, vel_z, vel_y, to_next, to_prev):
    planes = fuel.shape[0]
    at = 0
    for field, width in zip((fuel, heat, kappa, vel_z, vel_y), depths):
        to_next[at : at + width] = field[planes - width : planes]
        to_prev[at : at + width] = field[0:width]
        at += width


def deep_planes(fields, low, high):
    planes = fields[0].shape[0]
    at = 0
    columns = []
    for field, deep in zip(fields, depths):
        column = [(low, at + i, 1 + i) for i in range(deep)]
        column += [(field, i, 1 + deep) for i in range(planes)]
        column += [(high, at + i, deep - i) for i in range(deep)]
        columns.append(column)
        at += deep
    return columns


def rows_kernel(fuel, heat, kappa, vel_z, vel_y, low, high, to_next, to_prev):
    rows = fuel.shape[1]
    at = 0
    for column in deep_planes((fuel, heat, kappa, vel_z, vel_y), low, high):
        for source, i, width in column:
            to_next[at : at + width] = source[i, rows - width : rows]
            to_prev[at : at + width] = source[i, 0:width]
            at += width


def side(value, step):
    size = value.shape[1]
    lane = lax.broadcasted_iota(jnp.int32, value.shape, 1)
    if step > 0:
        return jnp.where(lane < size - 1, pltpu.roll(value, size - 1, 1), 0.0)
    return jnp.where(lane > 0, pltpu.roll(value, 1, 1), 0.0)


def above(value):
    return pltpu.roll(value, value.shape[0] - 1, 0)


def below(value):
    return pltpu.roll(value, 1, 0)


def parts(ref, i, vel_z, vel_y):
    centre = ref[i]
    ahead, behind = ref[i + 1], ref[i - 1]
    up, down = above(centre), below(centre)
    near = (ahead + behind) + (up + down) + (side(centre, 1) + side(centre, -1))
    transport = 0.5 * (vel_z * (ahead - behind) + vel_y * (up - down))
    return centre, near - 6.0 * centre, transport


def rates(fuel_ref, heat_ref, i, kappa, vel_z, vel_y):
    fuel_mid, fuel_lap, fuel_adv = parts(fuel_ref, i, vel_z, vel_y)
    heat_mid, heat_lap, heat_adv = parts(heat_ref, i, vel_z, vel_y)
    square = heat_mid * heat_mid
    burning = burn_rate * fuel_mid * square / (1.0 + square)
    return (
        lewis_ratio * kappa * fuel_lap - fuel_adv - burning,
        kappa * heat_lap - heat_adv + heat_release * burning,
    )


def block_transpose(tile):
    row = lax.broadcasted_iota(jnp.int32, tile.shape, 0)
    block = lax.broadcasted_iota(jnp.int32, tile.shape, 1) // 16
    for bit in (1, 2, 4):
        later = pltpu.roll(pltpu.roll(tile, 8 - bit, 0), 16 * bit, 1)
        earlier = pltpu.roll(pltpu.roll(tile, bit, 0), 128 - 16 * bit, 1)
        row_bit, block_bit = (row & bit) != 0, (block & bit) != 0
        swapped = jnp.where(block_bit, later, earlier)
        tile = jnp.where(row_bit == block_bit, tile, swapped)
    return tile


def step_kernel(
    fuel, heat, kappa, vel_z, vel_y, low, high, row_low, row_high, out,
    fuel_s, heat_s, kappa_s, vel_z_s, vel_y_s, fuel_one, heat_one, heat_two, fuel_two, edge,
):
    planes, rows, size = fuel.shape
    own = slice(WF, WF + rows)
    at = 0
    whole = (fuel_s, heat_s, kappa_s, vel_z_s, vel_y_s)
    columns = deep_planes((fuel, heat, kappa, vel_z, vel_y), low, high)
    for target, column in zip(whole, columns):
        for j, (source, i, width) in enumerate(column):
            target[j, own] = source[i]
            target[j, WF - width : WF] = row_low[at : at + width]
            target[j, WF + rows : WF + rows + width] = row_high[at : at + width]
            at += width

    def first(j, carry):
        rate_fuel, rate_heat = rates(
            fuel_s, heat_s, j + 1, kappa_s[j], vel_z_s[j], vel_y_s[j]
        )
        fuel_one[j] = fuel_s[j + 1] + time_step * rate_fuel
        heat_one[j] = heat_s[j + 1] + time_step * rate_heat
        return carry

    lax.fori_loop(0, planes + 2, first, 0)

    def second(j, carry):
        rate_fuel, rate_heat = rates(
            fuel_one, heat_one, j + 1, kappa_s[j + 1], vel_z_s[j + 1], vel_y_s[j + 1]
        )
        fuel_two[j] = 0.5 * (fuel_s[j + 2] + fuel_one[j + 1] + time_step * rate_fuel)
        heat_two[j] = 0.5 * (heat_s[j + 2] + heat_one[j + 1] + time_step * rate_heat)
        return carry

    lax.fori_loop(0, planes, second, 0)

    def send(value, at):
        lanes = slice(at * 128, (at + 1) * 128)
        for m in range(size // 128):
            tile = block_transpose(value[:, m * 128 : (m + 1) * 128])
            for l in range(8):
                out[8 * m + l, :, lanes] = tile[l : l + 1]

    lane = lax.broadcasted_iota(jnp.int32, (rows, size), 1)
    place = lane % 16
    borders = jnp.zeros((rows, size), jnp.float32)
    for p in range(planes):
        level = heat_two[p, own]
        send(level, p)
        send(fuel_two[p, own], planes + p)
        edge[p : p + 1] = heat_two[p, WF - 1 : WF]
        edge[planes + p : planes + p + 1] = heat_two[p, WF + rows : WF + rows + 1]
        left = (place == p) & (lane >= 16)
        right = (place == planes + p) & (lane < size - 16)
        borders = jnp.where(left, pltpu.roll(level, p + 1, 1), borders)
        borders = jnp.where(right, pltpu.roll(level, size - 16 + planes + p, 1), borders)
    send(edge[...], 2 * planes)
    send(borders, 2 * planes + 1)


def per_function(ref, *index):
    row = lax.broadcasted_iota(jnp.int32, (8, 128), 0)
    value = jnp.full((8, 128), ref[(0,) + index], jnp.float32)
    for k in range(1, 8):
        value = jnp.where(row == k, ref[(k,) + index], value)
    return value


def shift_rows(value, step):
    size = value.shape[0]
    row = lax.broadcasted_iota(jnp.int32, value.shape, 0)
    if step > 0:
        return jnp.where(row < size - 1, pltpu.roll(value, size - 1, 0), 0.0)
    return jnp.where(row > 0, pltpu.roll(value, 1, 0), 0.0)


def march_kernel(opacity_scale, planes, centre, width, density, tint, fields, out, lights):
    count = fields.shape[0]
    columns = [fields[:, 0, i * 128 : (i + 1) * 128] for i in range(planes)]
    edge, borders = (
        fields[:, 0, i * 128 : (i + 1) * 128] for i in (2 * planes, 2 * planes + 1)
    )
    lane = lax.broadcasted_iota(jnp.int32, (count, 128), 1)
    place = lane % 16
    for p in range(planes):
        level = columns[p]
        ahead = columns[p + 1] if p + 1 < planes else shift_rows(columns[0], 1)
        behind = columns[p - 1] if p > 0 else shift_rows(columns[planes - 1], -1)

        def moved(value, by):
            by = by % 128
            return pltpu.roll(value, by, 1) if by else value

        up = jnp.where(lane < 112, moved(level, -16), moved(edge, 112 - 16 * (planes + p)))
        down = jnp.where(lane >= 16, moved(level, 16), moved(edge, -16 * p))
        right = jnp.where(place < 15, moved(level, -1), moved(borders, 15 - planes - p))
        left = jnp.where(place > 0, moved(level, 1), moved(borders, -p))
        grad_z, grad_y, grad_x = 0.5 * (ahead - behind), 0.5 * (up - down), 0.5 * (right - left)
        norm_sq = grad_z * grad_z + grad_y * grad_y + grad_x * grad_x + 1.0
        facing = 0.48 * grad_z + 0.6 * grad_y + 0.64 * grad_x
        lights[p] = 0.5 * (0.35 + 0.65 * (facing * facing) / norm_sq)

    mid = per_function(centre)
    inverse = 1.0 / per_function(width)
    thick = per_function(density) * opacity_scale
    half = [0.5 * per_function(tint, c) for c in range(3)]

    def segment(s, state):
        passing, colour = state[0], list(state[1:])
        for p in range(planes):
            level = fields[s, :, p * 128 : (p + 1) * 128]
            fuel = fields[s, :, (planes + p) * 128 : (planes + p + 1) * 128]
            light = lights[p, pl.ds(s, 1)]
            offset = (level - mid) * inverse
            survive = jnp.exp(-thick * jnp.exp(-offset * offset))
            weight = passing * (1.0 - survive) * light
            for c in range(3):
                colour[c] = colour[c] + weight * (1.0 + jnp.tanh(half[c] * fuel))
            passing = passing * survive
        return (passing, *colour)

    zero = jnp.zeros((8, 128), jnp.float32)
    state = lax.fori_loop(0, count, segment, (zero + 1.0, zero, zero, zero))
    for c, value in enumerate((state[1], state[2], state[3], state[0])):
        tile = block_transpose(value)
        for k in range(8):
            out[k, c] = tile[:, 16 * k : 16 * k + 16]


def body(fuel, heat, kappa, vel_z, vel_y, tf_centre, tf_width, tf_density, tf_tint):
    planes, rows, columns = fuel.shape
    depth_count = lax.axis_size("depth")
    fields = (fuel, heat, kappa, vel_z, vel_y)
    f32 = functools.partial(jax.ShapeDtypeStruct, dtype=jnp.float32)
    sent_planes = sum(depths)
    sent_rows = sum(planes * (1 + deep) + deep * (1 + deep) for deep in depths)

    to_next, to_prev = pl.pallas_call(
        planes_kernel,
        out_shape=[f32((sent_planes, rows, columns))] * 2,
        in_specs=[vmem] * 5,
        out_specs=[vmem] * 2,
        compiler_params=params(),
        name="pack_planes",
    )(*fields)
    low, high = exchange(to_next, to_prev, "depth")
    to_next, to_prev = pl.pallas_call(
        rows_kernel,
        out_shape=[f32((sent_rows, columns))] * 2,
        in_specs=[vmem] * 7,
        out_specs=[vmem] * 2,
        compiler_params=params(),
        name="pack_rows",
    )(*fields, low, high)
    row_low, row_high = exchange(to_next, to_prev, "rows")

    tall = rows + 8
    segment = f32((depth_count, 1, (2 * planes + 2) * 128))
    scratch = [pltpu.VMEM((planes + 2 * deep, tall, columns), jnp.float32) for deep in depths]
    scratch += [pltpu.VMEM((planes + 2, tall, columns), jnp.float32)] * 2
    scratch += [pltpu.VMEM((planes, tall, columns), jnp.float32)] * 2
    scratch += [pltpu.VMEM((2 * planes, columns), jnp.float32)]
    stepped = pl.pallas_call(
        step_kernel,
        out_shape=segment,
        in_specs=[vmem] * 9,
        out_specs=vmem,
        scratch_shapes=scratch,
        compiler_params=params(),
        name="step",
    )(*fields, low, high, row_low, row_high)

    gathered = lax.all_to_all(stepped, "depth", split_axis=0, concat_axis=0, tiled=True)

    return pl.pallas_call(
        functools.partial(march_kernel, 4.0 / (planes * depth_count), planes),
        out_shape=f32((8, 4, rows, columns // depth_count)),
        in_specs=[smem] * 4 + [vmem],
        out_specs=vmem,
        scratch_shapes=[pltpu.VMEM((planes, depth_count, 128), jnp.float32)],
        compiler_params=params(),
        name="march",
    )(tf_centre, tf_width, tf_density, tf_tint, gathered)


def solution(mesh):
    placed = (P("depth", "rows", None),) * 5 + (P(),) * 4
    return jax.shard_map(
        body, mesh=mesh, in_specs=placed, out_specs=P(None, None, "rows", "depth"), check_vma=False
    )
```

time: 104 us -> 94 us (0.904)
  Pallas kernels: 12.3 us -> 5.55 us
  waiting for transfers between devices: 47.3 us -> 42.1 us
  local copies, waits for them, and re-layouts: 2.72 us -> 4.3 us
    ppermute x2, waiting for transfers between devices: 5.12 us -> 1.96 us  [exchange(): lax.ppermute(to_next, axis, forward)]
    pallas_call x1, Pallas kernels: 5.47 us -> 2.64 us  [body(): pl.pallas_call(step_kernel, out_shape=segment, in_specs=[vmem] * 9, out_s...]
    all_to_all x1, waiting for transfers between devices: 36.2 us -> 34 us  [body(): lax.all_to_all(stepped, 'depth', split_axis=0, concat_axis=0, tiled=True)]
    pallas_call x1, Pallas kernels: 2.13 us -> 0.1 us  [body(): pl.pallas_call(rows_kernel, out_shape=[f32((sent_rows, columns))] * 2, in...]
    pallas_call x1, Pallas kernels: 1.74 us -> 0.02 us  [body(): pl.pallas_call(planes_kernel, out_shape=[f32((sent_planes, rows, columns)...]
    unnamed x13 -> x19, local copies, waits for them, and re-layouts: 2.72 us -> 4.3 us
  transfers between devices with their start and end apart: 5 -> 5, of which waited for: 5 -> 5; matrix products, arithmetic and copies ran while one was open for 1% -> 0% of each run, Pallas kernels for 0% -> 0%
where the time goes in v2:
time: 94 us; the launch traced here: 93.5 us
  waiting for transfers between devices  42.1 us (45%)
  starting transfers between devices  41.5 us (44%)
  Pallas kernels  5.55 us (6%)
  local copies, waits for them, and re-layouts  4.3 us (5%)
    all_to_all x1, waiting for transfers between devices, body(): lax.all_to_all(stepped, 'depth', split_axis=0, concat_axis=0, tiled=True)  34 us
    all_to_all x1, starting transfers between devices, body(): lax.all_to_all(stepped, 'depth', split_axis=0, concat_axis=0, tiled=True)  28.7 us
    ppermute x2, starting transfers between devices, exchange(): lax.ppermute(to_prev, axis, backward)  7.04 us
    ppermute x2, waiting for transfers between devices, exchange(): lax.ppermute(to_prev, axis, backward)  6.07 us
    ppermute x2, starting transfers between devices, exchange(): lax.ppermute(to_next, axis, forward)  5.75 us
    unnamed x19, local copies, waits for them, and re-layouts  4.3 us
    pallas_call x1, Pallas kernels, body(): pl.pallas_call(functools.partial(march_kernel, 4.0 / (planes * depth_coun...  2.78 us
    pallas_call x1, Pallas kernels, body(): pl.pallas_call(step_kernel, out_shape=segment, in_specs=[vmem] * 9, out_s...  2.64 us
  transfers between devices with their start and end apart: 5, of which 5 were waited for; matrix products, arithmetic and copies ran while one was open for 0% of the time, Pallas kernels for 0%

profile of v2, /device:TPU:6, one launch (start us, length us, event | category | flops | bytes accessed | tf_op | source)
XLA Modules:
  0.0 93.5 jit_solution(3026910830413353972)
XLA Ops:
  0.0 0.8 copy-done
  0.8 0.8 copy-done.1
  1.7 0.8 copy-done.2
  2.5 0.8 copy-done.3
  3.4 0.8 copy-done.4
  4.2 3.8 %collective-permute-start = (f32[7,8,512]{2,1,0:T(8,128)S(1)}, f32[7,8,512]{2,1,0:T(8,128)S(1)}, u32[]{:S(2)}, u32[]{:S(2)}) collective-permute-start(f32[7,8,512]{2,1,0:T(8,128)S(1)} %get-tuple-element.9), channel_id=1, source_target_pairs={{0,32},{32,64},{64,96},{96,128},{128,160},{160,192},{192,224},{224... | collective-permute-start | bytes 344072 | tf_op jit(solution)/shard_map/ppermute | solution.py:32
  8.1 1.3 %collective-permute-start.1 = (f32[7,8,512]{2,1,0:T(8,128)S(1)}, f32[7,8,512]{2,1,0:T(8,128)S(1)}, u32[]{:S(2)}, u32[]{:S(2)}) collective-permute-start(f32[7,8,512]{2,1,0:T(8,128)S(1)} %get-tuple-element.10), channel_id=1, source_target_pairs={{32,0},{64,32},{96,64},{128,96},{160,128},{192,160},{224,192},{256... | collective-permute-start | bytes 344072 | tf_op jit(solution)/shard_map/ppermute | solution.py:32
  9.4 1.1 %collective-permute-done.low = f32[7,8,512]{2,1,0:T(8,128)S(1)} collective-permute-done((f32[7,8,512]{2,1,0:T(8,128)S(1)}, f32[7,8,512]{2,1,0:T(8,128)S(1)}, u32[]{:S(2)}, u32[]{:S(2)}) %collective-permute-start) | collective-permute-done | bytes 114720 | tf_op jit(solution)/shard_map/ppermute | solution.py:32
  10.4 4.3 %collective-permute-done.1.high = f32[7,8,512]{2,1,0:T(8,128)S(1)} collective-permute-done((f32[7,8,512]{2,1,0:T(8,128)S(1)}, f32[7,8,512]{2,1,0:T(8,128)S(1)}, u32[]{:S(2)}, u32[]{:S(2)}) %collective-permute-start.1) | collective-permute-done | bytes 114720 | tf_op jit(solution)/shard_map/ppermute | solution.py:32
  14.7 0.1 pack_rows.1
  14.8 1.9 %collective-permute-start.2 = (f32[66,512]{1,0:T(8,128)S(1)}, f32[66,512]{1,0:T(8,128)S(1)}, u32[]{:S(2)}, u32[]{:S(2)}) collective-permute-start(f32[66,512]{1,0:T(8,128)S(1)} %get-tuple-element.11), channel_id=1, source_target_pairs={{0,1},{1,2},{2,3},{3,4},{4,5},{5,6},{6,7},{7,8},{8,9},{9,10},{10,1... | collective-permute-start | bytes 405512 | tf_op jit(solution)/shard_map/ppermute | solution.py:32
  16.8 5.8 %collective-permute-start.3 = (f32[66,512]{1,0:T(8,128)S(1)}, f32[66,512]{1,0:T(8,128)S(1)}, u32[]{:S(2)}, u32[]{:S(2)}) collective-permute-start(f32[66,512]{1,0:T(8,128)S(1)} %get-tuple-element.12), channel_id=1, source_target_pairs={{1,0},{2,1},{3,2},{4,3},{5,4},{6,5},{7,6},{8,7},{9,8},{10,9},{11,1... | collective-permute-start | bytes 405512 | tf_op jit(solution)/shard_map/ppermute | solution.py:32
  22.5 0.9 collective-permute-done.2.row_low
  23.4 1.8 %collective-permute-done.3.row_high = f32[66,512]{1,0:T(8,128)S(1)} collective-permute-done((f32[66,512]{1,0:T(8,128)S(1)}, f32[66,512]{1,0:T(8,128)S(1)}, u32[]{:S(2)}, u32[]{:S(2)}) %collective-permute-start.3) | collective-permute-done | bytes 135200 | tf_op jit(solution)/shard_map/ppermute | solution.py:32
  25.2 2.6 %step.1 = f32[32,1,1280]{2,1,0:T(1,128)} custom-call(f32[4,8,512]{2,1,0:T(8,128)S(1)} %copy-done, f32[4,8,512]{2,1,0:T(8,128)S(1)} %copy-done.1, f32[4,8,512]{2,1,0:T(8,128)S(1)} %copy-done.2, f32[4,8,512]{2,1,0:T(8,128)S(1)} %copy-done.3, f32[4,8,512]{2,1,0:T(8,128)S(1)} %copy-done.4, f32[7,8,512]{2,1,0:T(8,128)S(1)} %collective-permute-done.low, ...), custom_call_target="tpu_custom_call" | custom-call | tf_op jit(solution)/shard_map/step/pallas_call | solution.py:281
  27.8 28.7 %all-to-all-start = ((f32[32,1,1280]{2,1,0:T(1,128)}), f32[32,1,1280]{2,1,0:T(1,128)S(1)}, u32[]{:S(2)}, u32[]{:S(2)}) async-start(f32[32,1,1280]{2,1,0:T(1,128)} %step.1), calls=%async_computation | async-start | bytes 327680 | tf_op jit(solution)/shard_map/all_to_all | solution.py:291
  56.6 0.0 copy-done.8
  56.6 0.0 copy-start.5
  56.6 0.0 copy-start.6
  56.6 0.0 copy-start.7
  56.6 0.1 copy.10.tint
  56.7 34.0 %all-to-all-done.fields = f32[32,1,1280]{2,1,0:T(1,128)S(1)} async-done(((f32[32,1,1280]{2,1,0:T(1,128)}), f32[32,1,1280]{2,1,0:T(1,128)S(1)}, u32[]{:S(2)}, u32[]{:S(2)}) %all-to-all-start) | async-done | bytes 163872 | tf_op jit(solution)/shard_map/all_to_all | solution.py:291
  90.7 0.0 copy-done.5
  90.7 2.8 %march.1 = f32[8,4,8,16]{3,2,1,0:T(8,128)} custom-call(f32[8]{0:T(128)S(1)} %copy-done.5, f32[8]{0:T(128)S(1)} %copy-done.6, f32[8]{0:T(128)S(1)} %copy-done.7, f32[8,3]{1,0:T(8,128)S(1)} %copy.10.tint, f32[32,1,1280]{2,1,0:T(1,128)S(1)} %all-to-all-done.fields), custom_call_target="tpu_custom_call" | custom-call | tf_op jit(solution)/shard_map/march/pallas_call | solution.py:293
  (9 shorter events, 0.0 us)
Async XLA Ops:
  0.0 0.8 copy-start
  0.8 0.8 copy-start.1
  1.7 0.8 copy-start.2
  2.5 0.8 copy-start.3
  3.4 0.8 copy-start.4
  4.2 6.2 %collective-permute-start = (f32[7,8,512]{2,1,0:T(8,128)S(1)}, f32[7,8,512]{2,1,0:T(8,128)S(1)}, u32[]{:S(2)}, u32[]{:S(2)}) collective-permute-start(f32[7,8,512]{2,1,0:T(8,128)S(1)} %get-tuple-element.9), channel_id=1, source_target_pairs={{0,32},{32,64},{64,96},{96,128},{128,160},{160,192},{192,224},{224... | collective-permute-start | bytes 344072 | tf_op jit(solution)/shard_map/ppermute | solution.py:32
  8.1 6.7 %collective-permute-start.1 = (f32[7,8,512]{2,1,0:T(8,128)S(1)}, f32[7,8,512]{2,1,0:T(8,128)S(1)}, u32[]{:S(2)}, u32[]{:S(2)}) collective-permute-start(f32[7,8,512]{2,1,0:T(8,128)S(1)} %get-tuple-element.10), channel_id=1, source_target_pairs={{32,0},{64,32},{96,64},{128,96},{160,128},{192,160},{224,192},{256... | collective-permute-start | bytes 344072 | tf_op jit(solution)/shard_map/ppermute | solution.py:32
  14.8 8.6 %collective-permute-start.2 = (f32[66,512]{1,0:T(8,128)S(1)}, f32[66,512]{1,0:T(8,128)S(1)}, u32[]{:S(2)}, u32[]{:S(2)}) collective-permute-start(f32[66,512]{1,0:T(8,128)S(1)} %get-tuple-element.11), channel_id=1, source_target_pairs={{0,1},{1,2},{2,3},{3,4},{4,5},{5,6},{6,7},{7,8},{8,9},{9,10},{10,1... | collective-permute-start | bytes 405512 | tf_op jit(solution)/shard_map/ppermute | solution.py:32
  16.8 8.4 %collective-permute-start.3 = (f32[66,512]{1,0:T(8,128)S(1)}, f32[66,512]{1,0:T(8,128)S(1)}, u32[]{:S(2)}, u32[]{:S(2)}) collective-permute-start(f32[66,512]{1,0:T(8,128)S(1)} %get-tuple-element.12), channel_id=1, source_target_pairs={{1,0},{2,1},{3,2},{4,3},{5,4},{6,5},{7,6},{8,7},{9,8},{10,9},{11,1... | collective-permute-start | bytes 405512 | tf_op jit(solution)/shard_map/ppermute | solution.py:32
  27.8 28.7 %copy-start.8 = (f32[8,3]{0,1:T(4,128)S(1)}, f32[8,3]{0,1:T(4,128)}, u32[]{:S(2)}) copy-start(f32[8,3]{0,1:T(4,128)} %param.17) | copy-start | bytes 292
  27.8 62.9 %all-to-all-start = ((f32[32,1,1280]{2,1,0:T(1,128)}), f32[32,1,1280]{2,1,0:T(1,128)S(1)}, u32[]{:S(2)}, u32[]{:S(2)}) async-start(f32[32,1,1280]{2,1,0:T(1,128)} %step.1), calls=%async_computation | async-start | bytes 327680 | tf_op jit(solution)/shard_map/all_to_all | solution.py:291
  56.6 34.2 %copy-start.5 = (f32[8]{0:T(128)S(1)}, f32[8]{0:T(128)}, u32[]{:S(2)}) copy-start(f32[8]{0:T(128)} %centre.1) | copy-start | bytes 100
  56.6 34.1 %copy-start.6 = (f32[8]{0:T(128)S(1)}, f32[8]{0:T(128)}, u32[]{:S(2)}) copy-start(f32[8]{0:T(128)} %width.1) | copy-start | bytes 100
  56.6 34.1 %copy-start.7 = (f32[8]{0:T(128)S(1)}, f32[8]{0:T(128)}, u32[]{:S(2)}) copy-start(f32[8]{0:T(128)} %density.1) | copy-start | bytes 100

commit v3 on v2

--- a/solution.py
+++ b/solution.py
@@ -1,4 +1,5 @@
 import functools
+import math
 
 import jax
 import jax.numpy as jnp
@@ -12,13 +13,12 @@
 heat_release = 0.6
 burn_rate = 0.5
 
-DF = 2
-DC = 1
-WF = 3
-depths = (DF, DF, DC, DC, DC)
+depths = (2, 2, 1, 1, 1)
+log2_e = math.log2(math.e)
 
 vmem = pl.BlockSpec(memory_space=pltpu.VMEM)
 smem = pl.BlockSpec(memory_space=pltpu.SMEM)
+hbm = pl.BlockSpec(memory_space=pltpu.HBM)
 
 
 def pairs(axis):
@@ -36,13 +36,23 @@
     return pltpu.CompilerParams(vmem_limit_bytes=8 << 20, **more)
 
 
-def planes_kernel(fuel, heat, kappa, vel_z, vel_y, to_next, to_prev):
+def planes_kernel(fuel, heat, kappa, vel_z, vel_y, to_next, to_prev, arrived):
     planes = fuel.shape[0]
-    at = 0
-    for field, width in zip((fuel, heat, kappa, vel_z, vel_y), depths):
-        to_next[at : at + width] = field[planes - width : planes]
-        to_prev[at : at + width] = field[0:width]
-        at += width
+    at, copies = 0, []
+    for field, deep in zip((fuel, heat, kappa, vel_z, vel_y), depths):
+        for source, target in ((planes - deep, to_next), (0, to_prev)):
+            copies.append(
+                pltpu.make_async_copy(
+                    field.at[pl.ds(source, deep)],
+                    target.at[pl.ds(at, deep)],
+                    arrived.at[len(copies)],
+                )
+            )
+        at += deep
+    for copy in copies:
+        copy.start()
+    for copy in copies:
+        copy.wait()
 
 
 def deep_planes(fields, low, high):
@@ -121,15 +131,16 @@
     fuel_s, heat_s, kappa_s, vel_z_s, vel_y_s, fuel_one, heat_one, heat_two, fuel_two, edge,
 ):
     planes, rows, size = fuel.shape
-    own = slice(WF, WF + rows)
+    tall = fuel_s.shape[1]
+    own = slice(0, rows)
     at = 0
     whole = (fuel_s, heat_s, kappa_s, vel_z_s, vel_y_s)
     columns = deep_planes((fuel, heat, kappa, vel_z, vel_y), low, high)
     for target, column in zip(whole, columns):
         for j, (source, i, width) in enumerate(column):
             target[j, own] = source[i]
-            target[j, WF - width : WF] = row_low[at : at + width]
-            target[j, WF + rows : WF + rows + width] = row_high[at : at + width]
+            target[j, tall - width : tall] = row_low[at : at + width]
+            target[j, rows : rows + width] = row_high[at : at + width]
             at += width
 
     def first(j, carry):
@@ -152,12 +163,12 @@
 
     lax.fori_loop(0, planes, second, 0)
 
+    chunk = 2 * planes + 2
+
     def send(value, at):
-        lanes = slice(at * 128, (at + 1) * 128)
         for m in range(size // 128):
             tile = block_transpose(value[:, m * 128 : (m + 1) * 128])
-            for l in range(8):
-                out[8 * m + l, :, lanes] = tile[l : l + 1]
+            out[pl.ds(8 * m * chunk + at, 8, stride=chunk), :] = tile
 
     lane = lax.broadcasted_iota(jnp.int32, (rows, size), 1)
     place = lane % 16
@@ -166,8 +177,8 @@
         level = heat_two[p, own]
         send(level, p)
         send(fuel_two[p, own], planes + p)
-        edge[p : p + 1] = heat_two[p, WF - 1 : WF]
-        edge[planes + p : planes + p + 1] = heat_two[p, WF + rows : WF + rows + 1]
+        edge[p : p + 1] = heat_two[p, tall - 1 : tall]
+        edge[planes + p : planes + p + 1] = heat_two[p, rows : rows + 1]
         left = (place == p) & (lane >= 16)
         right = (place == planes + p) & (lane < size - 16)
         borders = jnp.where(left, pltpu.roll(level, p + 1, 1), borders)
@@ -193,10 +204,11 @@
 
 
 def march_kernel(opacity_scale, planes, centre, width, density, tint, fields, out, lights):
-    count = fields.shape[0]
-    columns = [fields[:, 0, i * 128 : (i + 1) * 128] for i in range(planes)]
+    chunk = 2 * planes + 2
+    count = fields.shape[0] // chunk
+    columns = [fields[pl.ds(i, count, stride=chunk), :] for i in range(planes)]
     edge, borders = (
-        fields[:, 0, i * 128 : (i + 1) * 128] for i in (2 * planes, 2 * planes + 1)
+        fields[pl.ds(2 * planes + i, count, stride=chunk), :] for i in range(2)
     )
     lane = lax.broadcasted_iota(jnp.int32, (count, 128), 1)
     place = lane % 16
@@ -219,27 +231,33 @@
         lights[p] = 0.5 * (0.35 + 0.65 * (facing * facing) / norm_sq)
 
     mid = per_function(centre)
-    inverse = 1.0 / per_function(width)
-    thick = per_function(density) * opacity_scale
+    spread = per_function(width)
+    narrow = -log2_e / (spread * spread)
+    thick = per_function(density) * (-log2_e * opacity_scale)
     half = [0.5 * per_function(tint, c) for c in range(3)]
 
-    def segment(s, state):
-        passing, colour = state[0], list(state[1:])
-        for p in range(planes):
-            level = fields[s, :, p * 128 : (p + 1) * 128]
-            fuel = fields[s, :, (planes + p) * 128 : (planes + p + 1) * 128]
-            light = lights[p, pl.ds(s, 1)]
-            offset = (level - mid) * inverse
-            survive = jnp.exp(-thick * jnp.exp(-offset * offset))
-            weight = passing * (1.0 - survive) * light
-            for c in range(3):
-                colour[c] = colour[c] + weight * (1.0 + jnp.tanh(half[c] * fuel))
-            passing = passing * survive
-        return (passing, *colour)
+    def one_plane(s, p, state):
+        passing, total, *colour = state
+        at = s * chunk + p
+        level, fuel = fields[pl.ds(at, 1), :], fields[pl.ds(at + planes, 1), :]
+        offset = level - mid
+        survive = jnp.exp2(thick * jnp.exp2(narrow * (offset * offset)))
+        weight = passing * (1.0 - survive) * lights[p, pl.ds(s, 1)]
+        colour = [value + weight * jnp.tanh(half[c] * fuel) for c, value in enumerate(colour)]
+        return (passing * survive, total + weight, *colour)
+
+    joint = 4
+
+    def segments(i, state):
+        for s in range(joint):
+            for p in range(planes):
+                state = one_plane(i * joint + s, p, state)
+        return state
 
     zero = jnp.zeros((8, 128), jnp.float32)
-    state = lax.fori_loop(0, count, segment, (zero + 1.0, zero, zero, zero))
-    for c, value in enumerate((state[1], state[2], state[3], state[0])):
+    state = lax.fori_loop(0, count // joint, segments, (zero + 1.0, zero, zero, zero, zero))
+    passing, total, *colour = state
+    for c, value in enumerate([total + value for value in colour] + [passing]):
         tile = block_transpose(value)
         for k in range(8):
             out[k, c] = tile[:, 16 * k : 16 * k + 16]
@@ -256,11 +274,12 @@
     to_next, to_prev = pl.pallas_call(
         planes_kernel,
         out_shape=[f32((sent_planes, rows, columns))] * 2,
-        in_specs=[vmem] * 5,
+        in_specs=[hbm] * 5,
         out_specs=[vmem] * 2,
+        scratch_shapes=[pltpu.SemaphoreType.DMA((2 * len(depths),))],
         compiler_params=params(),
         name="pack_planes",
-    )(*fields)
+    )(*(pltpu.with_memory_space_constraint(field, pltpu.HBM) for field in fields))
     low, high = exchange(to_next, to_prev, "depth")
     to_next, to_prev = pl.pallas_call(
         rows_kernel,
@@ -273,14 +292,14 @@
     row_low, row_high = exchange(to_next, to_prev, "rows")
 
     tall = rows + 8
-    segment = f32((depth_count, 1, (2 * planes + 2) * 128))
+    chunk = 2 * planes + 2
     scratch = [pltpu.VMEM((planes + 2 * deep, tall, columns), jnp.float32) for deep in depths]
     scratch += [pltpu.VMEM((planes + 2, tall, columns), jnp.float32)] * 2
     scratch += [pltpu.VMEM((planes, tall, columns), jnp.float32)] * 2
     scratch += [pltpu.VMEM((2 * planes, columns), jnp.float32)]
     stepped = pl.pallas_call(
         step_kernel,
-        out_shape=segment,
+        out_shape=f32((depth_count * chunk, 128)),
         in_specs=[vmem] * 9,
         out_specs=vmem,
         scratch_shapes=scratch,
@@ -288,7 +307,9 @@
         name="step",
     )(*fields, low, high, row_low, row_high)
 
-    gathered = lax.all_to_all(stepped, "depth", split_axis=0, concat_axis=0, tiled=True)
+    gathered = lax.all_to_all(
+        stepped.reshape(depth_count, 1, chunk * 128), "depth", split_axis=0, concat_axis=0, tiled=True
+    ).reshape(depth_count * chunk, 128)
 
     return pl.pallas_call(
         functools.partial(march_kernel, 4.0 / (planes * depth_count), planes),

time: 94 us -> 90.4 us (0.962)
  local copies, waits for them, and re-layouts: 4.3 us -> 0.12 us
    unnamed x19, local copies, waits for them, and re-layouts: 4.3 us -> 0.12 us
where the time goes in v3:
time: 90.4 us; the launch traced here: 90 us
  waiting for transfers between devices  42.1 us (47%)
  starting transfers between devices  41.5 us (46%)
  Pallas kernels  6.13 us (7%)
    all_to_all x1, waiting for transfers between devices, body(): lax.all_to_all(stepped.reshape(depth_count, 1, chunk * 128), 'depth', spl...  34.1 us
    all_to_all x1, starting transfers between devices, body(): lax.all_to_all(stepped.reshape(depth_count, 1, chunk * 128), 'depth', spl...  28.7 us
    ppermute x2, starting transfers between devices, exchange(): lax.ppermute(to_prev, axis, backward)  7.04 us
    ppermute x2, waiting for transfers between devices, exchange(): lax.ppermute(to_prev, axis, backward)  6.07 us
    ppermute x2, starting transfers between devices, exchange(): lax.ppermute(to_next, axis, forward)  5.75 us
    pallas_call x1, Pallas kernels, body(): pl.pallas_call(step_kernel, out_shape=f32((depth_count * chunk, 128)), in...  2.72 us
    pallas_call x1, Pallas kernels, body(): pl.pallas_call(functools.partial(march_kernel, 4.0 / (planes * depth_coun...  2.36 us
    ppermute x2, waiting for transfers between devices, exchange(): lax.ppermute(to_next, axis, forward)  1.96 us
  transfers between devices with their start and end apart: 5, of which 5 were waited for; matrix products, arithmetic and copies ran while one was open for 0% of the time, Pallas kernels for 0%

profile of v3, /device:TPU:6, one launch (start us, length us, event | category | flops | bytes accessed | tf_op | source)
XLA Modules:
  0.0 90.0 jit_solution(11518485066676264818)
XLA Ops:
  0.0 0.0 copy-start.4
  0.0 0.0 copy-start
  0.0 0.9 %pack_planes.1 = (f32[7,8,512]{2,1,0:T(8,128)S(1)}, f32[7,8,512]{2,1,0:T(8,128)S(1)}) custom-call(f32[4,8,512]{2,1,0:T(8,128)} %fuel.5, f32[4,8,512]{2,1,0:T(8,128)} %heat.5, f32[4,8,512]{2,1,0:T(8,128)} %kappa.5, f32[4,8,512]{2,1,0:T(8,128)} %vel_z.5, f32[4,8,512]{2,1,0:T(8,128)} %vel_y.5), custom_call_target="tpu_custom_call" | custom-call | tf_op jit(solution)/shard_map/pack_planes/pallas_call | solution.py:274
  1.0 3.8 %collective-permute-start = (f32[7,8,512]{2,1,0:T(8,128)S(1)}, f32[7,8,512]{2,1,0:T(8,128)S(1)}, u32[]{:S(2)}, u32[]{:S(2)}) collective-permute-start(f32[7,8,512]{2,1,0:T(8,128)S(1)} %get-tuple-element.9), channel_id=1, source_target_pairs={{0,32},{32,64},{64,96},{96,128},{128,160},{160,192},{192,224},{224... | collective-permute-start | bytes 344072 | tf_op jit(solution)/shard_map/ppermute | solution.py:32
  4.8 1.3 %collective-permute-start.1 = (f32[7,8,512]{2,1,0:T(8,128)S(1)}, f32[7,8,512]{2,1,0:T(8,128)S(1)}, u32[]{:S(2)}, u32[]{:S(2)}) collective-permute-start(f32[7,8,512]{2,1,0:T(8,128)S(1)} %get-tuple-element.10), channel_id=1, source_target_pairs={{32,0},{64,32},{96,64},{128,96},{160,128},{192,160},{224,192},{256... | collective-permute-start | bytes 344072 | tf_op jit(solution)/shard_map/ppermute | solution.py:32
  6.1 1.1 %collective-permute-done.low = f32[7,8,512]{2,1,0:T(8,128)S(1)} collective-permute-done((f32[7,8,512]{2,1,0:T(8,128)S(1)}, f32[7,8,512]{2,1,0:T(8,128)S(1)}, u32[]{:S(2)}, u32[]{:S(2)}) %collective-permute-start) | collective-permute-done | bytes 114720 | tf_op jit(solution)/shard_map/ppermute | solution.py:32
  7.2 4.3 %collective-permute-done.1.high = f32[7,8,512]{2,1,0:T(8,128)S(1)} collective-permute-done((f32[7,8,512]{2,1,0:T(8,128)S(1)}, f32[7,8,512]{2,1,0:T(8,128)S(1)}, u32[]{:S(2)}, u32[]{:S(2)}) %collective-permute-start.1) | collective-permute-done | bytes 114720 | tf_op jit(solution)/shard_map/ppermute | solution.py:32
  11.5 0.0 copy-done.1
  11.5 0.0 copy-done.2
  11.5 0.0 copy-done.3
  11.5 0.0 copy-done.4
  11.5 0.0 copy-done
  11.5 0.1 pack_rows.1
  11.7 1.9 %collective-permute-start.2 = (f32[66,512]{1,0:T(8,128)S(1)}, f32[66,512]{1,0:T(8,128)S(1)}, u32[]{:S(2)}, u32[]{:S(2)}) collective-permute-start(f32[66,512]{1,0:T(8,128)S(1)} %get-tuple-element.11), channel_id=1, source_target_pairs={{0,1},{1,2},{2,3},{3,4},{4,5},{5,6},{6,7},{7,8},{8,9},{9,10},{10,1... | collective-permute-start | bytes 405512 | tf_op jit(solution)/shard_map/ppermute | solution.py:32
  13.6 5.8 %collective-permute-start.3 = (f32[66,512]{1,0:T(8,128)S(1)}, f32[66,512]{1,0:T(8,128)S(1)}, u32[]{:S(2)}, u32[]{:S(2)}) collective-permute-start(f32[66,512]{1,0:T(8,128)S(1)} %get-tuple-element.12), channel_id=1, source_target_pairs={{1,0},{2,1},{3,2},{4,3},{5,4},{6,5},{7,6},{8,7},{9,8},{10,9},{11,1... | collective-permute-start | bytes 405512 | tf_op jit(solution)/shard_map/ppermute | solution.py:32
  19.3 0.9 collective-permute-done.2.row_low
  20.2 1.8 %collective-permute-done.3.row_high = f32[66,512]{1,0:T(8,128)S(1)} collective-permute-done((f32[66,512]{1,0:T(8,128)S(1)}, f32[66,512]{1,0:T(8,128)S(1)}, u32[]{:S(2)}, u32[]{:S(2)}) %collective-permute-start.3) | collective-permute-done | bytes 135200 | tf_op jit(solution)/shard_map/ppermute | solution.py:32
  22.0 2.7 %step.1 = f32[320,128]{1,0:T(8,128)} custom-call(f32[4,8,512]{2,1,0:T(8,128)S(1)} %copy-done, f32[4,8,512]{2,1,0:T(8,128)S(1)} %copy-done.1, f32[4,8,512]{2,1,0:T(8,128)S(1)} %copy-done.2, f32[4,8,512]{2,1,0:T(8,128)S(1)} %copy-done.3, f32[4,8,512]{2,1,0:T(8,128)S(1)} %copy-done.4, f32[7,8,512]{2,1,0:T(8,128)S(1)} %collective-permute-done.low, ...), custom_call_target="tpu_custom_call" | custom-call | tf_op jit(solution)/shard_map/step/pallas_call | solution.py:300
  24.7 28.7 %all-to-all-start = ((f32[32,1,1280]{2,1,0:T(1,128)}), f32[32,1,1280]{2,1,0:T(1,128)S(1)}, u32[]{:S(2)}, u32[]{:S(2)}) async-start(f32[32,1,1280]{2,1,0:T(1,128)} %bitcast), calls=%async_computation | async-start | bytes 327680 | tf_op jit(solution)/shard_map/all_to_all | solution.py:310
  53.4 0.0 copy-done.8
  53.5 0.1 copy.12.tint
  53.5 34.1 %all-to-all-done = f32[32,1,1280]{2,1,0:T(1,128)S(1)} async-done(((f32[32,1,1280]{2,1,0:T(1,128)}), f32[32,1,1280]{2,1,0:T(1,128)S(1)}, u32[]{:S(2)}, u32[]{:S(2)}) %all-to-all-start) | async-done | bytes 163872 | tf_op jit(solution)/shard_map/all_to_all | solution.py:310
  87.6 0.0 copy-done.5
  87.6 2.4 %march.1 = f32[8,4,8,16]{3,2,1,0:T(8,128)} custom-call(f32[8]{0:T(128)S(1)} %copy-done.5, f32[8]{0:T(128)S(1)} %copy-done.6, f32[8]{0:T(128)S(1)} %copy-done.7, f32[8,3]{1,0:T(8,128)S(1)} %copy.12.tint, f32[320,128]{1,0:T(8,128)S(1)} %bitcast.2), custom_call_target="tpu_custom_call" | custom-call | tf_op jit(solution)/shard_map/march/pallas_call | solution.py:314
  (9 shorter events, 0.0 us)
Async XLA Ops:
  0.0 11.5 %copy-start.1 = (f32[4,8,512]{2,1,0:T(8,128)S(1)}, f32[4,8,512]{2,1,0:T(8,128)}, u32[]{:S(2)}) copy-start(f32[4,8,512]{2,1,0:T(8,128)} %heat.5) | copy-start | bytes 196612
  0.0 11.5 %copy-start.2 = (f32[4,8,512]{2,1,0:T(8,128)S(1)}, f32[4,8,512]{2,1,0:T(8,128)}, u32[]{:S(2)}) copy-start(f32[4,8,512]{2,1,0:T(8,128)} %kappa.5) | copy-start | bytes 196612
  0.0 11.5 %copy-start.3 = (f32[4,8,512]{2,1,0:T(8,128)S(1)}, f32[4,8,512]{2,1,0:T(8,128)}, u32[]{:S(2)}) copy-start(f32[4,8,512]{2,1,0:T(8,128)} %vel_z.5) | copy-start | bytes 196612
  0.0 11.5 %copy-start.4 = (f32[4,8,512]{2,1,0:T(8,128)S(1)}, f32[4,8,512]{2,1,0:T(8,128)}, u32[]{:S(2)}) copy-start(f32[4,8,512]{2,1,0:T(8,128)} %vel_y.5) | copy-start | bytes 196612
  0.0 11.5 %copy-start = (f32[4,8,512]{2,1,0:T(8,128)S(1)}, f32[4,8,512]{2,1,0:T(8,128)}, u32[]{:S(2)}) copy-start(f32[4,8,512]{2,1,0:T(8,128)} %fuel.5) | copy-start | bytes 196612
  1.0 6.2 %collective-permute-start = (f32[7,8,512]{2,1,0:T(8,128)S(1)}, f32[7,8,512]{2,1,0:T(8,128)S(1)}, u32[]{:S(2)}, u32[]{:S(2)}) collective-permute-start(f32[7,8,512]{2,1,0:T(8,128)S(1)} %get-tuple-element.9), channel_id=1, source_target_pairs={{0,32},{32,64},{64,96},{96,128},{128,160},{160,192},{192,224},{224... | collective-permute-start | bytes 344072 | tf_op jit(solution)/shard_map/ppermute | solution.py:32
  4.8 6.7 %collective-permute-start.1 = (f32[7,8,512]{2,1,0:T(8,128)S(1)}, f32[7,8,512]{2,1,0:T(8,128)S(1)}, u32[]{:S(2)}, u32[]{:S(2)}) collective-permute-start(f32[7,8,512]{2,1,0:T(8,128)S(1)} %get-tuple-element.10), channel_id=1, source_target_pairs={{32,0},{64,32},{96,64},{128,96},{160,128},{192,160},{224,192},{256... | collective-permute-start | bytes 344072 | tf_op jit(solution)/shard_map/ppermute | solution.py:32
  11.7 8.6 %collective-permute-start.2 = (f32[66,512]{1,0:T(8,128)S(1)}, f32[66,512]{1,0:T(8,128)S(1)}, u32[]{:S(2)}, u32[]{:S(2)}) collective-permute-start(f32[66,512]{1,0:T(8,128)S(1)} %get-tuple-element.11), channel_id=1, source_target_pairs={{0,1},{1,2},{2,3},{3,4},{4,5},{5,6},{6,7},{7,8},{8,9},{9,10},{10,1... | collective-permute-start | bytes 405512 | tf_op jit(solution)/shard_map/ppermute | solution.py:32
  13.6 8.4 %collective-permute-start.3 = (f32[66,512]{1,0:T(8,128)S(1)}, f32[66,512]{1,0:T(8,128)S(1)}, u32[]{:S(2)}, u32[]{:S(2)}) collective-permute-start(f32[66,512]{1,0:T(8,128)S(1)} %get-tuple-element.12), channel_id=1, source_target_pairs={{1,0},{2,1},{3,2},{4,3},{5,4},{6,5},{7,6},{8,7},{9,8},{10,9},{11,1... | collective-permute-start | bytes 405512 | tf_op jit(solution)/shard_map/ppermute | solution.py:32
  24.7 28.7 %copy-start.8 = (f32[8,3]{0,1:T(4,128)S(1)}, f32[8,3]{0,1:T(4,128)}, u32[]{:S(2)}) copy-start(f32[8,3]{0,1:T(4,128)} %param.17) | copy-start | bytes 292
  24.7 62.9 %all-to-all-start = ((f32[32,1,1280]{2,1,0:T(1,128)}), f32[32,1,1280]{2,1,0:T(1,128)S(1)}, u32[]{:S(2)}, u32[]{:S(2)}) async-start(f32[32,1,1280]{2,1,0:T(1,128)} %bitcast), calls=%async_computation | async-start | bytes 327680 | tf_op jit(solution)/shard_map/all_to_all | solution.py:310
  53.5 34.1 %copy-start.5 = (f32[8]{0:T(128)S(1)}, f32[8]{0:T(128)}, u32[]{:S(2)}) copy-start(f32[8]{0:T(128)} %centre.1) | copy-start | bytes 100
  53.5 34.1 %copy-start.6 = (f32[8]{0:T(128)S(1)}, f32[8]{0:T(128)}, u32[]{:S(2)}) copy-start(f32[8]{0:T(128)} %width.1) | copy-start | bytes 100
  53.5 34.1 %copy-start.7 = (f32[8]{0:T(128)S(1)}, f32[8]{0:T(128)}, u32[]{:S(2)}) copy-start(f32[8]{0:T(128)} %density.1) | copy-start | bytes 100

commit v4 on v3

--- a/solution.py
+++ b/solution.py
@@ -19,6 +19,10 @@
 vmem = pl.BlockSpec(memory_space=pltpu.VMEM)
 smem = pl.BlockSpec(memory_space=pltpu.SMEM)
 hbm = pl.BlockSpec(memory_space=pltpu.HBM)
+
+
+def first_member(count):
+    return 5 * count // 8
 
 
 def pairs(axis):
@@ -164,11 +168,16 @@
     lax.fori_loop(0, planes, second, 0)
 
     chunk = 2 * planes + 2
+    count = size // 16
 
     def send(value, at):
         for m in range(size // 128):
             tile = block_transpose(value[:, m * 128 : (m + 1) * 128])
-            out[pl.ds(8 * m * chunk + at, 8, stride=chunk), :] = tile
+            place = (8 * m - first_member(count)) % count
+            before = min(8, count - place)
+            out[pl.ds(place * chunk + at, before, stride=chunk), :] = tile[:before]
+            if before < 8:
+                out[pl.ds(at, 8 - before, stride=chunk), :] = tile[before:]
 
     lane = lax.broadcasted_iota(jnp.int32, (rows, size), 1)
     place = lane % 16
@@ -198,9 +207,10 @@
 def shift_rows(value, step):
     size = value.shape[0]
     row = lax.broadcasted_iota(jnp.int32, value.shape, 0)
+    start = (size - first_member(size)) % size
     if step > 0:
-        return jnp.where(row < size - 1, pltpu.roll(value, size - 1, 0), 0.0)
-    return jnp.where(row > 0, pltpu.roll(value, 1, 0), 0.0)
+        return jnp.where(row != (start - 1) % size, pltpu.roll(value, size - 1, 0), 0.0)
+    return jnp.where(row != start, pltpu.roll(value, 1, 0), 0.0)
 
 
 def march_kernel(opacity_scale, planes, centre, width, density, tint, fields, out, lights):
@@ -238,6 +248,7 @@
 
     def one_plane(s, p, state):
         passing, total, *colour = state
+        s = lax.rem(s + (count - first_member(count)), count)
         at = s * chunk + p
         level, fuel = fields[pl.ds(at, 1), :], fields[pl.ds(at + planes, 1), :]
         offset = level - mid
@@ -307,8 +318,14 @@
         name="step",
     )(*fields, low, high, row_low, row_high)
 
+    order = [(first_member(depth_count) + i) % depth_count for i in range(depth_count)]
     gathered = lax.all_to_all(
-        stepped.reshape(depth_count, 1, chunk * 128), "depth", split_axis=0, concat_axis=0, tiled=True
+        stepped.reshape(depth_count, 1, chunk * 128),
+        "depth",
+        split_axis=0,
+        concat_axis=0,
+        axis_index_groups=[order],
+        tiled=True,
     ).reshape(depth_count * chunk, 128)
 
     return pl.pallas_call(

time: 90.4 us -> 77.2 us (0.85)
  waiting for transfers between devices: 42.1 us -> 26.5 us
  starting transfers between devices: 41.5 us -> 44 us
    all_to_all x1, waiting for transfers between devices: 34.1 us -> 18.5 us  [body(): lax.all_to_all(stepped.reshape(depth_count, 1, chunk * 128), 'depth', spl...]
    all_to_all x1, starting transfers between devices: 28.7 us -> 31.2 us  [body(): lax.all_to_all(stepped.reshape(depth_count, 1, chunk * 128), 'depth', spl...]
where the time goes in v4:
time: 77.2 us; the launch traced here: 76.8 us
  starting transfers between devices  44 us (57%)
  waiting for transfers between devices  26.5 us (34%)
  Pallas kernels  6.13 us (8%)
    all_to_all x1, starting transfers between devices, body(): lax.all_to_all(stepped.reshape(depth_count, 1, chunk * 128), 'depth', spl...  31.2 us
    all_to_all x1, waiting for transfers between devices, body(): lax.all_to_all(stepped.reshape(depth_count, 1, chunk * 128), 'depth', spl...  18.5 us
    ppermute x2, starting transfers between devices, exchange(): lax.ppermute(to_prev, axis, backward)  7.04 us
    ppermute x2, waiting for transfers between devices, exchange(): lax.ppermute(to_prev, axis, backward)  6.07 us
    ppermute x2, starting transfers between devices, exchange(): lax.ppermute(to_next, axis, forward)  5.75 us
    pallas_call x1, Pallas kernels, body(): pl.pallas_call(step_kernel, out_shape=f32((depth_count * chunk, 128)), in...  2.7 us
    pallas_call x1, Pallas kernels, body(): pl.pallas_call(functools.partial(march_kernel, 4.0 / (planes * depth_coun...  2.38 us
    ppermute x2, waiting for transfers between devices, exchange(): lax.ppermute(to_next, axis, forward)  1.96 us
  transfers between devices with their start and end apart: 5, of which 5 were waited for; matrix products, arithmetic and copies ran while one was open for 0% of the time, Pallas kernels for 0%

profile of v4, /device:TPU:6, one launch (start us, length us, event | category | flops | bytes accessed | tf_op | source)
XLA Modules:
  0.0 76.8 jit_solution(2964224410143303541)
XLA Ops:
  0.0 0.0 copy-start.4
  0.0 0.0 copy-start
  0.0 0.9 %pack_planes.1 = (f32[7,8,512]{2,1,0:T(8,128)S(1)}, f32[7,8,512]{2,1,0:T(8,128)S(1)}) custom-call(f32[4,8,512]{2,1,0:T(8,128)} %fuel.5, f32[4,8,512]{2,1,0:T(8,128)} %heat.5, f32[4,8,512]{2,1,0:T(8,128)} %kappa.5, f32[4,8,512]{2,1,0:T(8,128)} %vel_z.5, f32[4,8,512]{2,1,0:T(8,128)} %vel_y.5), custom_call_target="tpu_custom_call" | custom-call | tf_op jit(solution)/shard_map/pack_planes/pallas_call | solution.py:285
  1.0 3.8 %collective-permute-start = (f32[7,8,512]{2,1,0:T(8,128)S(1)}, f32[7,8,512]{2,1,0:T(8,128)S(1)}, u32[]{:S(2)}, u32[]{:S(2)}) collective-permute-start(f32[7,8,512]{2,1,0:T(8,128)S(1)} %get-tuple-element.9), channel_id=1, source_target_pairs={{0,32},{32,64},{64,96},{96,128},{128,160},{160,192},{192,224},{224... | collective-permute-start | bytes 344072 | tf_op jit(solution)/shard_map/ppermute | solution.py:36
  4.8 1.3 %collective-permute-start.1 = (f32[7,8,512]{2,1,0:T(8,128)S(1)}, f32[7,8,512]{2,1,0:T(8,128)S(1)}, u32[]{:S(2)}, u32[]{:S(2)}) collective-permute-start(f32[7,8,512]{2,1,0:T(8,128)S(1)} %get-tuple-element.10), channel_id=1, source_target_pairs={{32,0},{64,32},{96,64},{128,96},{160,128},{192,160},{224,192},{256... | collective-permute-start | bytes 344072 | tf_op jit(solution)/shard_map/ppermute | solution.py:36
  6.1 1.1 %collective-permute-done.low = f32[7,8,512]{2,1,0:T(8,128)S(1)} collective-permute-done((f32[7,8,512]{2,1,0:T(8,128)S(1)}, f32[7,8,512]{2,1,0:T(8,128)S(1)}, u32[]{:S(2)}, u32[]{:S(2)}) %collective-permute-start) | collective-permute-done | bytes 114720 | tf_op jit(solution)/shard_map/ppermute | solution.py:36
  7.2 4.3 %collective-permute-done.1.high = f32[7,8,512]{2,1,0:T(8,128)S(1)} collective-permute-done((f32[7,8,512]{2,1,0:T(8,128)S(1)}, f32[7,8,512]{2,1,0:T(8,128)S(1)}, u32[]{:S(2)}, u32[]{:S(2)}) %collective-permute-start.1) | collective-permute-done | bytes 114720 | tf_op jit(solution)/shard_map/ppermute | solution.py:36
  11.5 0.0 copy-done.1
  11.5 0.0 copy-done.2
  11.5 0.0 copy-done.3
  11.5 0.0 copy-done.4
  11.5 0.0 copy-done
  11.5 0.1 pack_rows.1
  11.7 1.9 %collective-permute-start.2 = (f32[66,512]{1,0:T(8,128)S(1)}, f32[66,512]{1,0:T(8,128)S(1)}, u32[]{:S(2)}, u32[]{:S(2)}) collective-permute-start(f32[66,512]{1,0:T(8,128)S(1)} %get-tuple-element.11), channel_id=1, source_target_pairs={{0,1},{1,2},{2,3},{3,4},{4,5},{5,6},{6,7},{7,8},{8,9},{9,10},{10,1... | collective-permute-start | bytes 405512 | tf_op jit(solution)/shard_map/ppermute | solution.py:36
  13.6 5.8 %collective-permute-start.3 = (f32[66,512]{1,0:T(8,128)S(1)}, f32[66,512]{1,0:T(8,128)S(1)}, u32[]{:S(2)}, u32[]{:S(2)}) collective-permute-start(f32[66,512]{1,0:T(8,128)S(1)} %get-tuple-element.12), channel_id=1, source_target_pairs={{1,0},{2,1},{3,2},{4,3},{5,4},{6,5},{7,6},{8,7},{9,8},{10,9},{11,1... | collective-permute-start | bytes 405512 | tf_op jit(solution)/shard_map/ppermute | solution.py:36
  19.3 0.9 %collective-permute-done.2.row_low = f32[66,512]{1,0:T(8,128)S(1)} collective-permute-done((f32[66,512]{1,0:T(8,128)S(1)}, f32[66,512]{1,0:T(8,128)S(1)}, u32[]{:S(2)}, u32[]{:S(2)}) %collective-permute-start.2) | collective-permute-done | bytes 135200 | tf_op jit(solution)/shard_map/ppermute | solution.py:36
  20.2 1.8 %collective-permute-done.3.row_high = f32[66,512]{1,0:T(8,128)S(1)} collective-permute-done((f32[66,512]{1,0:T(8,128)S(1)}, f32[66,512]{1,0:T(8,128)S(1)}, u32[]{:S(2)}, u32[]{:S(2)}) %collective-permute-start.3) | collective-permute-done | bytes 135200 | tf_op jit(solution)/shard_map/ppermute | solution.py:36
  22.0 2.7 %step.1 = f32[320,128]{1,0:T(8,128)} custom-call(f32[4,8,512]{2,1,0:T(8,128)S(1)} %copy-done, f32[4,8,512]{2,1,0:T(8,128)S(1)} %copy-done.1, f32[4,8,512]{2,1,0:T(8,128)S(1)} %copy-done.2, f32[4,8,512]{2,1,0:T(8,128)S(1)} %copy-done.3, f32[4,8,512]{2,1,0:T(8,128)S(1)} %copy-done.4, f32[7,8,512]{2,1,0:T(8,128)S(1)} %collective-permute-done.low, ...), custom_call_target="tpu_custom_call" | custom-call | tf_op jit(solution)/shard_map/step/pallas_call | solution.py:311
  24.7 31.2 %all-to-all-start = ((f32[32,1,1280]{2,1,0:T(1,128)}), f32[32,1,1280]{2,1,0:T(1,128)S(1)}, u32[]{:S(2)}, u32[]{:S(2)}) async-start(f32[32,1,1280]{2,1,0:T(1,128)} %bitcast), calls=%async_computation | async-start | bytes 327680 | tf_op jit(solution)/shard_map/all_to_all | solution.py:322
  55.9 0.0 copy-done.8
  55.9 0.1 copy.12.tint
  56.0 18.5 %all-to-all-done = f32[32,1,1280]{2,1,0:T(1,128)S(1)} async-done(((f32[32,1,1280]{2,1,0:T(1,128)}), f32[32,1,1280]{2,1,0:T(1,128)S(1)}, u32[]{:S(2)}, u32[]{:S(2)}) %all-to-all-start) | async-done | bytes 163872 | tf_op jit(solution)/shard_map/all_to_all | solution.py:322
  74.4 0.0 copy-done.5
  74.5 2.4 %march.1 = f32[8,4,8,16]{3,2,1,0:T(8,128)} custom-call(f32[8]{0:T(128)S(1)} %copy-done.5, f32[8]{0:T(128)S(1)} %copy-done.6, f32[8]{0:T(128)S(1)} %copy-done.7, f32[8,3]{1,0:T(8,128)S(1)} %copy.12.tint, f32[320,128]{1,0:T(8,128)S(1)} %bitcast.2), custom_call_target="tpu_custom_call" | custom-call | tf_op jit(solution)/shard_map/march/pallas_call | solution.py:331
  (9 shorter events, 0.0 us)
Async XLA Ops:
  0.0 11.5 %copy-start.1 = (f32[4,8,512]{2,1,0:T(8,128)S(1)}, f32[4,8,512]{2,1,0:T(8,128)}, u32[]{:S(2)}) copy-start(f32[4,8,512]{2,1,0:T(8,128)} %heat.5) | copy-start | bytes 196612
  0.0 11.5 %copy-start.2 = (f32[4,8,512]{2,1,0:T(8,128)S(1)}, f32[4,8,512]{2,1,0:T(8,128)}, u32[]{:S(2)}) copy-start(f32[4,8,512]{2,1,0:T(8,128)} %kappa.5) | copy-start | bytes 196612
  0.0 11.5 %copy-start.3 = (f32[4,8,512]{2,1,0:T(8,128)S(1)}, f32[4,8,512]{2,1,0:T(8,128)}, u32[]{:S(2)}) copy-start(f32[4,8,512]{2,1,0:T(8,128)} %vel_z.5) | copy-start | bytes 196612
  0.0 11.5 %copy-start.4 = (f32[4,8,512]{2,1,0:T(8,128)S(1)}, f32[4,8,512]{2,1,0:T(8,128)}, u32[]{:S(2)}) copy-start(f32[4,8,512]{2,1,0:T(8,128)} %vel_y.5) | copy-start | bytes 196612
  0.0 11.5 %copy-start = (f32[4,8,512]{2,1,0:T(8,128)S(1)}, f32[4,8,512]{2,1,0:T(8,128)}, u32[]{:S(2)}) copy-start(f32[4,8,512]{2,1,0:T(8,128)} %fuel.5) | copy-start | bytes 196612
  1.0 6.2 %collective-permute-start = (f32[7,8,512]{2,1,0:T(8,128)S(1)}, f32[7,8,512]{2,1,0:T(8,128)S(1)}, u32[]{:S(2)}, u32[]{:S(2)}) collective-permute-start(f32[7,8,512]{2,1,0:T(8,128)S(1)} %get-tuple-element.9), channel_id=1, source_target_pairs={{0,32},{32,64},{64,96},{96,128},{128,160},{160,192},{192,224},{224... | collective-permute-start | bytes 344072 | tf_op jit(solution)/shard_map/ppermute | solution.py:36
  4.8 6.7 %collective-permute-start.1 = (f32[7,8,512]{2,1,0:T(8,128)S(1)}, f32[7,8,512]{2,1,0:T(8,128)S(1)}, u32[]{:S(2)}, u32[]{:S(2)}) collective-permute-start(f32[7,8,512]{2,1,0:T(8,128)S(1)} %get-tuple-element.10), channel_id=1, source_target_pairs={{32,0},{64,32},{96,64},{128,96},{160,128},{192,160},{224,192},{256... | collective-permute-start | bytes 344072 | tf_op jit(solution)/shard_map/ppermute | solution.py:36
  11.7 8.6 %collective-permute-start.2 = (f32[66,512]{1,0:T(8,128)S(1)}, f32[66,512]{1,0:T(8,128)S(1)}, u32[]{:S(2)}, u32[]{:S(2)}) collective-permute-start(f32[66,512]{1,0:T(8,128)S(1)} %get-tuple-element.11), channel_id=1, source_target_pairs={{0,1},{1,2},{2,3},{3,4},{4,5},{5,6},{6,7},{7,8},{8,9},{9,10},{10,1... | collective-permute-start | bytes 405512 | tf_op jit(solution)/shard_map/ppermute | solution.py:36
  13.6 8.4 %collective-permute-start.3 = (f32[66,512]{1,0:T(8,128)S(1)}, f32[66,512]{1,0:T(8,128)S(1)}, u32[]{:S(2)}, u32[]{:S(2)}) collective-permute-start(f32[66,512]{1,0:T(8,128)S(1)} %get-tuple-element.12), channel_id=1, source_target_pairs={{1,0},{2,1},{3,2},{4,3},{5,4},{6,5},{7,6},{8,7},{9,8},{10,9},{11,1... | collective-permute-start | bytes 405512 | tf_op jit(solution)/shard_map/ppermute | solution.py:36
  24.7 31.2 %copy-start.8 = (f32[8,3]{0,1:T(4,128)S(1)}, f32[8,3]{0,1:T(4,128)}, u32[]{:S(2)}) copy-start(f32[8,3]{0,1:T(4,128)} %param.17) | copy-start | bytes 292
  24.7 49.7 %all-to-all-start = ((f32[32,1,1280]{2,1,0:T(1,128)}), f32[32,1,1280]{2,1,0:T(1,128)S(1)}, u32[]{:S(2)}, u32[]{:S(2)}) async-start(f32[32,1,1280]{2,1,0:T(1,128)} %bitcast), calls=%async_computation | async-start | bytes 327680 | tf_op jit(solution)/shard_map/all_to_all | solution.py:322
  56.0 18.5 %copy-start.5 = (f32[8]{0:T(128)S(1)}, f32[8]{0:T(128)}, u32[]{:S(2)}) copy-start(f32[8]{0:T(128)} %centre.1) | copy-start | bytes 100
  56.0 18.5 %copy-start.6 = (f32[8]{0:T(128)S(1)}, f32[8]{0:T(128)}, u32[]{:S(2)}) copy-start(f32[8]{0:T(128)} %width.1) | copy-start | bytes 100
  56.0 18.5 %copy-start.7 = (f32[8]{0:T(128)S(1)}, f32[8]{0:T(128)}, u32[]{:S(2)}) copy-start(f32[8]{0:T(128)} %density.1) | copy-start | bytes 100

commit v5 on v4

--- a/solution.py
+++ b/solution.py
@@ -25,15 +25,21 @@
     return 5 * count // 8
 
 
-def pairs(axis):
+def exchange(to_next, to_prev, axis):
     count = lax.axis_size(axis)
     forward = [(i, i + 1) for i in range(count - 1)]
-    return forward, [(target, source) for source, target in forward]
-
-
-def exchange(to_next, to_prev, axis):
-    forward, backward = pairs(axis)
+    backward = [(target, source) for source, target in forward]
     return lax.ppermute(to_next, axis, forward), lax.ppermute(to_prev, axis, backward)
+
+
+def swap(block, axis, first):
+    count = lax.axis_size(axis)
+    forward = [(i, i + 1) for i in range(first, count - 1, 2)]
+    return lax.ppermute(block, axis, forward + [(target, source) for source, target in forward])
+
+
+def second_core():
+    return lax.rem(lax.axis_index("rows"), 2) == 1
 
 
 def params(**more):
@@ -72,14 +78,21 @@
     return columns
 
 
-def rows_kernel(fuel, heat, kappa, vel_z, vel_y, low, high, to_next, to_prev):
+def rows_kernel(fuel, heat, kappa, vel_z, vel_y, low, high, outer, inner):
     rows = fuel.shape[1]
-    at = 0
-    for column in deep_planes((fuel, heat, kappa, vel_z, vel_y), low, high):
-        for source, i, width in column:
-            to_next[at : at + width] = source[i, rows - width : rows]
-            to_prev[at : at + width] = source[i, 0:width]
-            at += width
+    columns = deep_planes((fuel, heat, kappa, vel_z, vel_y), low, high)
+
+    def fill(to_next, to_prev):
+        at = 0
+        for column in columns:
+            for source, i, width in column:
+                to_next[at : at + width] = source[i, rows - width : rows]
+                to_prev[at : at + width] = source[i, 0:width]
+                at += width
+
+    odd = second_core()
+    pl.when(odd)(lambda: fill(outer, inner))
+    pl.when(jnp.logical_not(odd))(lambda: fill(inner, outer))
 
 
 def side(value, step):
@@ -131,21 +144,29 @@
 
 
 def step_kernel(
-    fuel, heat, kappa, vel_z, vel_y, low, high, row_low, row_high, out,
+    fuel, heat, kappa, vel_z, vel_y, low, high, outer, inner, out,
     fuel_s, heat_s, kappa_s, vel_z_s, vel_y_s, fuel_one, heat_one, heat_two, fuel_two, edge,
 ):
     planes, rows, size = fuel.shape
     tall = fuel_s.shape[1]
     own = slice(0, rows)
-    at = 0
     whole = (fuel_s, heat_s, kappa_s, vel_z_s, vel_y_s)
     columns = deep_planes((fuel, heat, kappa, vel_z, vel_y), low, high)
     for target, column in zip(whole, columns):
         for j, (source, i, width) in enumerate(column):
             target[j, own] = source[i]
-            target[j, tall - width : tall] = row_low[at : at + width]
-            target[j, rows : rows + width] = row_high[at : at + width]
-            at += width
+
+    def border(row_low, row_high):
+        at = 0
+        for target, column in zip(whole, columns):
+            for j, (source, i, width) in enumerate(column):
+                target[j, tall - width : tall] = row_low[at : at + width]
+                target[j, rows : rows + width] = row_high[at : at + width]
+                at += width
+
+    odd = second_core()
+    pl.when(odd)(lambda: border(inner, outer))
+    pl.when(jnp.logical_not(odd))(lambda: border(outer, inner))
 
     def first(j, carry):
         rate_fuel, rate_heat = rates(
@@ -292,7 +313,7 @@
         name="pack_planes",
     )(*(pltpu.with_memory_space_constraint(field, pltpu.HBM) for field in fields))
     low, high = exchange(to_next, to_prev, "depth")
-    to_next, to_prev = pl.pallas_call(
+    outer, inner = pl.pallas_call(
         rows_kernel,
         out_shape=[f32((sent_rows, columns))] * 2,
         in_specs=[vmem] * 7,
@@ -300,7 +321,7 @@
         compiler_params=params(),
         name="pack_rows",
     )(*fields, low, high)
-    row_low, row_high = exchange(to_next, to_prev, "rows")
+    outer, inner = swap(outer, "rows", 1), swap(inner, "rows", 0)
 
     tall = rows + 8
     chunk = 2 * planes + 2
@@ -316,7 +337,7 @@
         scratch_shapes=scratch,
         compiler_params=params(),
         name="step",
-    )(*fields, low, high, row_low, row_high)
+    )(*fields, low, high, outer, inner)
 
     order = [(first_member(depth_count) + i) % depth_count for i in range(depth_count)]
     gathered = lax.all_to_all(

time: 77.2 us -> 74.4 us (0.964)
  starting transfers between devices: 44 us -> 41.8 us
    ppermute x2 -> x1, starting transfers between devices: 7.04 us -> 1.29 us  [exchange(): lax.ppermute(to_prev, axis, backward)]
    ppermute x0 -> x2, starting transfers between devices: none -> 5.51 us  [swap(): lax.ppermute(block, axis, forward + [(target, source) for source, target...]
    ppermute x0 -> x2, waiting for transfers between devices: none -> 3.05 us  [swap(): lax.ppermute(block, axis, forward + [(target, source) for source, target...]
    ppermute x2 -> x1, starting transfers between devices: 5.75 us -> 3.83 us  [exchange(): lax.ppermute(to_next, axis, forward)]
    ppermute x2 -> x1, waiting for transfers between devices: 6.07 us -> 4.31 us  [exchange(): lax.ppermute(to_prev, axis, backward)]
    all_to_all x1, waiting for transfers between devices: 18.5 us -> 17.4 us  [body(): lax.all_to_all(stepped.reshape(depth_count, 1, chunk * 128), 'depth', spl...]
    ppermute x2 -> x1, waiting for transfers between devices: 1.96 us -> 1.08 us  [exchange(): lax.ppermute(to_next, axis, forward)]
  transfers between devices with their start and end apart: 5 -> 5, of which waited for: 5 -> 4; matrix products, arithmetic and copies ran while one was open for 0% -> 0% of each run, Pallas kernels for 0% -> 0%
where the time goes in v5:
time: 74.4 us; the launch traced here: 74 us
  starting transfers between devices  41.8 us (56%)
  waiting for transfers between devices  25.8 us (35%)
  Pallas kernels  6.16 us (8%)
    all_to_all x1, starting transfers between devices, body(): lax.all_to_all(stepped.reshape(depth_count, 1, chunk * 128), 'depth', spl...  31.2 us
    all_to_all x1, waiting for transfers between devices, body(): lax.all_to_all(stepped.reshape(depth_count, 1, chunk * 128), 'depth', spl...  17.4 us
    ppermute x2, starting transfers between devices, swap(): lax.ppermute(block, axis, forward + [(target, source) for source, target...  5.51 us
    ppermute x1, waiting for transfers between devices, exchange(): lax.ppermute(to_prev, axis, backward)  4.31 us
    ppermute x1, starting transfers between devices, exchange(): lax.ppermute(to_next, axis, forward)  3.83 us
    ppermute x2, waiting for transfers between devices, swap(): lax.ppermute(block, axis, forward + [(target, source) for source, target...  3.05 us
    pallas_call x1, Pallas kernels, body(): pl.pallas_call(step_kernel, out_shape=f32((depth_count * chunk, 128)), in...  2.72 us
    pallas_call x1, Pallas kernels, body(): pl.pallas_call(functools.partial(march_kernel, 4.0 / (planes * depth_coun...  2.38 us
  transfers between devices with their start and end apart: 5, of which 4 were waited for; matrix products, arithmetic and copies ran while one was open for 0% of the time, Pallas kernels for 0%

profile of v5, /device:TPU:6, one launch (start us, length us, event | category | flops | bytes accessed | tf_op | source)
XLA Modules:
  0.0 74.0 jit_solution(2114488740305477211)
XLA Ops:
  0.0 0.0 copy-start.4
  0.0 0.0 copy-start
  0.0 0.9 %pack_planes.1 = (f32[7,8,512]{2,1,0:T(8,128)S(1)}, f32[7,8,512]{2,1,0:T(8,128)S(1)}) custom-call(f32[4,8,512]{2,1,0:T(8,128)} %fuel.5, f32[4,8,512]{2,1,0:T(8,128)} %heat.5, f32[4,8,512]{2,1,0:T(8,128)} %kappa.5, f32[4,8,512]{2,1,0:T(8,128)} %vel_z.5, f32[4,8,512]{2,1,0:T(8,128)} %vel_y.5), custom_call_target="tpu_custom_call" | custom-call | tf_op jit(solution)/shard_map/pack_planes/pallas_call | solution.py:306
  1.0 3.8 %collective-permute-start = (f32[7,8,512]{2,1,0:T(8,128)S(1)}, f32[7,8,512]{2,1,0:T(8,128)S(1)}, u32[]{:S(2)}, u32[]{:S(2)}) collective-permute-start(f32[7,8,512]{2,1,0:T(8,128)S(1)} %get-tuple-element.9), channel_id=1, source_target_pairs={{0,32},{32,64},{64,96},{96,128},{128,160},{160,192},{192,224},{224... | collective-permute-start | bytes 344072 | tf_op jit(solution)/shard_map/ppermute | solution.py:32
  4.8 1.3 %collective-permute-start.1 = (f32[7,8,512]{2,1,0:T(8,128)S(1)}, f32[7,8,512]{2,1,0:T(8,128)S(1)}, u32[]{:S(2)}, u32[]{:S(2)}) collective-permute-start(f32[7,8,512]{2,1,0:T(8,128)S(1)} %get-tuple-element.10), channel_id=1, source_target_pairs={{32,0},{64,32},{96,64},{128,96},{160,128},{192,160},{224,192},{256... | collective-permute-start | bytes 344072 | tf_op jit(solution)/shard_map/ppermute | solution.py:32
  6.1 1.1 %collective-permute-done.low = f32[7,8,512]{2,1,0:T(8,128)S(1)} collective-permute-done((f32[7,8,512]{2,1,0:T(8,128)S(1)}, f32[7,8,512]{2,1,0:T(8,128)S(1)}, u32[]{:S(2)}, u32[]{:S(2)}) %collective-permute-start) | collective-permute-done | bytes 114720 | tf_op jit(solution)/shard_map/ppermute | solution.py:32
  7.2 4.3 %collective-permute-done.1.high = f32[7,8,512]{2,1,0:T(8,128)S(1)} collective-permute-done((f32[7,8,512]{2,1,0:T(8,128)S(1)}, f32[7,8,512]{2,1,0:T(8,128)S(1)}, u32[]{:S(2)}, u32[]{:S(2)}) %collective-permute-start.1) | collective-permute-done | bytes 114720 | tf_op jit(solution)/shard_map/ppermute | solution.py:32
  11.5 0.0 copy-done.1
  11.5 0.0 copy-done.2
  11.5 0.0 copy-done.3
  11.5 0.0 copy-done.4
  11.5 0.0 copy-done
  11.5 0.1 pack_rows.1
  11.7 3.4 %collective-permute-start.2 = (f32[66,512]{1,0:T(8,128)S(1)}, f32[66,512]{1,0:T(8,128)S(1)}, u32[]{:S(2)}, u32[]{:S(2)}) collective-permute-start(f32[66,512]{1,0:T(8,128)S(1)} %get-tuple-element.11), channel_id=1, source_target_pairs={{1,2},{3,4},{5,6},{7,8},{9,10},{11,12},{13,14},{15,16},{17,18},{19... | collective-permute-start | bytes 405512 | tf_op jit(solution)/shard_map/ppermute | solution.py:38
  15.1 2.1 %collective-permute-start.3 = (f32[66,512]{1,0:T(8,128)S(1)}, f32[66,512]{1,0:T(8,128)S(1)}, u32[]{:S(2)}, u32[]{:S(2)}) collective-permute-start(f32[66,512]{1,0:T(8,128)S(1)} %get-tuple-element.12), channel_id=1, source_target_pairs={{0,1},{2,3},{4,5},{6,7},{8,9},{10,11},{12,13},{14,15},{16,17},{18,... | collective-permute-start | bytes 405512 | tf_op jit(solution)/shard_map/ppermute | solution.py:38
  17.2 3.0 %collective-permute-done.2.outer = f32[66,512]{1,0:T(8,128)S(1)} collective-permute-done((f32[66,512]{1,0:T(8,128)S(1)}, f32[66,512]{1,0:T(8,128)S(1)}, u32[]{:S(2)}, u32[]{:S(2)}) %collective-permute-start.2) | collective-permute-done | bytes 135200 | tf_op jit(solution)/shard_map/ppermute | solution.py:38
  20.2 0.0 collective-permute-done.3.inner
  20.2 2.7 %step.1 = f32[320,128]{1,0:T(8,128)} custom-call(f32[4,8,512]{2,1,0:T(8,128)S(1)} %copy-done, f32[4,8,512]{2,1,0:T(8,128)S(1)} %copy-done.1, f32[4,8,512]{2,1,0:T(8,128)S(1)} %copy-done.2, f32[4,8,512]{2,1,0:T(8,128)S(1)} %copy-done.3, f32[4,8,512]{2,1,0:T(8,128)S(1)} %copy-done.4, f32[7,8,512]{2,1,0:T(8,128)S(1)} %collective-permute-done.low, ...), custom_call_target="tpu_custom_call" | custom-call | tf_op jit(solution)/shard_map/step/pallas_call | solution.py:332
  23.0 31.2 %all-to-all-start = ((f32[32,1,1280]{2,1,0:T(1,128)}), f32[32,1,1280]{2,1,0:T(1,128)S(1)}, u32[]{:S(2)}, u32[]{:S(2)}) async-start(f32[32,1,1280]{2,1,0:T(1,128)} %bitcast), calls=%async_computation | async-start | bytes 327680 | tf_op jit(solution)/shard_map/all_to_all | solution.py:343
  54.1 0.0 copy-done.8
  54.1 0.1 copy.12.tint
  54.2 17.4 %all-to-all-done = f32[32,1,1280]{2,1,0:T(1,128)S(1)} async-done(((f32[32,1,1280]{2,1,0:T(1,128)}), f32[32,1,1280]{2,1,0:T(1,128)S(1)}, u32[]{:S(2)}, u32[]{:S(2)}) %all-to-all-start) | async-done | bytes 163872 | tf_op jit(solution)/shard_map/all_to_all | solution.py:343
  71.6 0.0 copy-done.5
  71.6 2.4 %march.1 = f32[8,4,8,16]{3,2,1,0:T(8,128)} custom-call(f32[8]{0:T(128)S(1)} %copy-done.5, f32[8]{0:T(128)S(1)} %copy-done.6, f32[8]{0:T(128)S(1)} %copy-done.7, f32[8,3]{1,0:T(8,128)S(1)} %copy.12.tint, f32[320,128]{1,0:T(8,128)S(1)} %bitcast.2), custom_call_target="tpu_custom_call" | custom-call | tf_op jit(solution)/shard_map/march/pallas_call | solution.py:352
  (9 shorter events, 0.0 us)
Async XLA Ops:
  0.0 11.5 %copy-start.1 = (f32[4,8,512]{2,1,0:T(8,128)S(1)}, f32[4,8,512]{2,1,0:T(8,128)}, u32[]{:S(2)}) copy-start(f32[4,8,512]{2,1,0:T(8,128)} %heat.5) | copy-start | bytes 196612
  0.0 11.5 %copy-start.2 = (f32[4,8,512]{2,1,0:T(8,128)S(1)}, f32[4,8,512]{2,1,0:T(8,128)}, u32[]{:S(2)}) copy-start(f32[4,8,512]{2,1,0:T(8,128)} %kappa.5) | copy-start | bytes 196612
  0.0 11.5 %copy-start.3 = (f32[4,8,512]{2,1,0:T(8,128)S(1)}, f32[4,8,512]{2,1,0:T(8,128)}, u32[]{:S(2)}) copy-start(f32[4,8,512]{2,1,0:T(8,128)} %vel_z.5) | copy-start | bytes 196612
  0.0 11.5 %copy-start.4 = (f32[4,8,512]{2,1,0:T(8,128)S(1)}, f32[4,8,512]{2,1,0:T(8,128)}, u32[]{:S(2)}) copy-start(f32[4,8,512]{2,1,0:T(8,128)} %vel_y.5) | copy-start | bytes 196612
  0.0 11.5 %copy-start = (f32[4,8,512]{2,1,0:T(8,128)S(1)}, f32[4,8,512]{2,1,0:T(8,128)}, u32[]{:S(2)}) copy-start(f32[4,8,512]{2,1,0:T(8,128)} %fuel.5) | copy-start | bytes 196612
  1.0 6.2 %collective-permute-start = (f32[7,8,512]{2,1,0:T(8,128)S(1)}, f32[7,8,512]{2,1,0:T(8,128)S(1)}, u32[]{:S(2)}, u32[]{:S(2)}) collective-permute-start(f32[7,8,512]{2,1,0:T(8,128)S(1)} %get-tuple-element.9), channel_id=1, source_target_pairs={{0,32},{32,64},{64,96},{96,128},{128,160},{160,192},{192,224},{224... | collective-permute-start | bytes 344072 | tf_op jit(solution)/shard_map/ppermute | solution.py:32
  4.8 6.7 %collective-permute-start.1 = (f32[7,8,512]{2,1,0:T(8,128)S(1)}, f32[7,8,512]{2,1,0:T(8,128)S(1)}, u32[]{:S(2)}, u32[]{:S(2)}) collective-permute-start(f32[7,8,512]{2,1,0:T(8,128)S(1)} %get-tuple-element.10), channel_id=1, source_target_pairs={{32,0},{64,32},{96,64},{128,96},{160,128},{192,160},{224,192},{256... | collective-permute-start | bytes 344072 | tf_op jit(solution)/shard_map/ppermute | solution.py:32
  11.7 8.6 %collective-permute-start.2 = (f32[66,512]{1,0:T(8,128)S(1)}, f32[66,512]{1,0:T(8,128)S(1)}, u32[]{:S(2)}, u32[]{:S(2)}) collective-permute-start(f32[66,512]{1,0:T(8,128)S(1)} %get-tuple-element.11), channel_id=1, source_target_pairs={{1,2},{3,4},{5,6},{7,8},{9,10},{11,12},{13,14},{15,16},{17,18},{19... | collective-permute-start | bytes 405512 | tf_op jit(solution)/shard_map/ppermute | solution.py:38
  15.1 5.2 %collective-permute-start.3 = (f32[66,512]{1,0:T(8,128)S(1)}, f32[66,512]{1,0:T(8,128)S(1)}, u32[]{:S(2)}, u32[]{:S(2)}) collective-permute-start(f32[66,512]{1,0:T(8,128)S(1)} %get-tuple-element.12), channel_id=1, source_target_pairs={{0,1},{2,3},{4,5},{6,7},{8,9},{10,11},{12,13},{14,15},{16,17},{18,... | collective-permute-start | bytes 405512 | tf_op jit(solution)/shard_map/ppermute | solution.py:38
  23.0 31.2 %copy-start.8 = (f32[8,3]{0,1:T(4,128)S(1)}, f32[8,3]{0,1:T(4,128)}, u32[]{:S(2)}) copy-start(f32[8,3]{0,1:T(4,128)} %param.17) | copy-start | bytes 292
  23.0 48.7 %all-to-all-start = ((f32[32,1,1280]{2,1,0:T(1,128)}), f32[32,1,1280]{2,1,0:T(1,128)S(1)}, u32[]{:S(2)}, u32[]{:S(2)}) async-start(f32[32,1,1280]{2,1,0:T(1,128)} %bitcast), calls=%async_computation | async-start | bytes 327680 | tf_op jit(solution)/shard_map/all_to_all | solution.py:343
  54.2 17.4 %copy-start.5 = (f32[8]{0:T(128)S(1)}, f32[8]{0:T(128)}, u32[]{:S(2)}) copy-start(f32[8]{0:T(128)} %centre.1) | copy-start | bytes 100
  54.2 17.4 %copy-start.6 = (f32[8]{0:T(128)S(1)}, f32[8]{0:T(128)}, u32[]{:S(2)}) copy-start(f32[8]{0:T(128)} %width.1) | copy-start | bytes 100
  54.2 17.4 %copy-start.7 = (f32[8]{0:T(128)S(1)}, f32[8]{0:T(128)}, u32[]{:S(2)}) copy-start(f32[8]{0:T(128)} %density.1) | copy-start | bytes 100

commit v6 on v5

--- a/solution.py
+++ b/solution.py
@@ -95,126 +95,146 @@
     pl.when(jnp.logical_not(odd))(lambda: fill(inner, outer))
 
 
-def side(value, step):
-    size = value.shape[1]
-    lane = lax.broadcasted_iota(jnp.int32, value.shape, 1)
-    if step > 0:
-        return jnp.where(lane < size - 1, pltpu.roll(value, size - 1, 1), 0.0)
-    return jnp.where(lane > 0, pltpu.roll(value, 1, 1), 0.0)
-
-
-def above(value):
-    return pltpu.roll(value, value.shape[0] - 1, 0)
-
-
-def below(value):
-    return pltpu.roll(value, 1, 0)
-
-
-def parts(ref, i, vel_z, vel_y):
-    centre = ref[i]
-    ahead, behind = ref[i + 1], ref[i - 1]
-    up, down = above(centre), below(centre)
-    near = (ahead + behind) + (up + down) + (side(centre, 1) + side(centre, -1))
-    transport = 0.5 * (vel_z * (ahead - behind) + vel_y * (up - down))
-    return centre, near - 6.0 * centre, transport
-
-
-def rates(fuel_ref, heat_ref, i, kappa, vel_z, vel_y):
-    fuel_mid, fuel_lap, fuel_adv = parts(fuel_ref, i, vel_z, vel_y)
-    heat_mid, heat_lap, heat_adv = parts(heat_ref, i, vel_z, vel_y)
-    square = heat_mid * heat_mid
-    burning = burn_rate * fuel_mid * square / (1.0 + square)
+def neighbours(blocks, m, lane, rolled):
+    def turned(i, by):
+        if not 0 <= i < len(blocks):
+            return 0.0
+        if (i, by) not in rolled:
+            rolled[i, by] = pltpu.roll(blocks[i], by, 1)
+        return rolled[i, by]
+
+    right = jnp.where(lane < 127, turned(m, 127), turned(m + 1, 127))
+    return right + jnp.where(lane > 0, turned(m, 1), turned(m - 1, 1))
+
+
+def parts(centre, ahead, behind, beside, half_z, half_y):
+    up, down = pltpu.roll(centre, centre.shape[0] - 1, 0), pltpu.roll(centre, 1, 0)
+    near = (ahead + behind) + (up + down) + beside
+    return near - 6.0 * centre, half_z * (ahead - behind) + half_y * (up - down)
+
+
+def rates(fuels, heats, kappa, vel_z, vel_y):
+    half_z, half_y = 0.5 * vel_z, 0.5 * vel_y
+    fuel_lap, fuel_adv = parts(*fuels, half_z, half_y)
+    heat_lap, heat_adv = parts(*heats, half_z, half_y)
+    square = heats[0] * heats[0]
+    burning = burn_rate * fuels[0] * square / (1.0 + square)
     return (
         lewis_ratio * kappa * fuel_lap - fuel_adv - burning,
         kappa * heat_lap - heat_adv + heat_release * burning,
     )
 
 
-def block_transpose(tile):
-    row = lax.broadcasted_iota(jnp.int32, tile.shape, 0)
-    block = lax.broadcasted_iota(jnp.int32, tile.shape, 1) // 16
-    for bit in (1, 2, 4):
-        later = pltpu.roll(pltpu.roll(tile, 8 - bit, 0), 16 * bit, 1)
-        earlier = pltpu.roll(pltpu.roll(tile, bit, 0), 128 - 16 * bit, 1)
+def block_transpose(tiles):
+    shape = (8, 128)
+    row = lax.broadcasted_iota(jnp.int32, shape, 0)
+    block = lax.broadcasted_iota(jnp.int32, shape, 1) // 16
+    for bit in (4, 2, 1):
         row_bit, block_bit = (row & bit) != 0, (block & bit) != 0
-        swapped = jnp.where(block_bit, later, earlier)
-        tile = jnp.where(row_bit == block_bit, tile, swapped)
-    return tile
+        if bit == 4:
+            moved = [pltpu.roll(pltpu.roll(tile, 64, 1), 4, 0) for tile in tiles]
+        else:
+            right = [pltpu.roll(tile, 16 * bit, 1) for tile in tiles]
+            left = [pltpu.roll(tile, 128 - 16 * bit, 1) for tile in tiles]
+            right = [pltpu.roll(tile, 8 - bit, 0) for tile in right]
+            left = [pltpu.roll(tile, bit, 0) for tile in left]
+            moved = [jnp.where(block_bit, r, l) for r, l in zip(right, left)]
+        same = row_bit == block_bit
+        tiles = [jnp.where(same, tile, other) for tile, other in zip(tiles, moved)]
+    return tiles
 
 
 def step_kernel(
     fuel, heat, kappa, vel_z, vel_y, low, high, outer, inner, out,
-    fuel_s, heat_s, kappa_s, vel_z_s, vel_y_s, fuel_one, heat_one, heat_two, fuel_two, edge,
+    halo, fuel_one, heat_one, heat_two, fuel_two, edge,
 ):
     planes, rows, size = fuel.shape
-    tall = fuel_s.shape[1]
-    own = slice(0, rows)
-    whole = (fuel_s, heat_s, kappa_s, vel_z_s, vel_y_s)
     columns = deep_planes((fuel, heat, kappa, vel_z, vel_y), low, high)
-    for target, column in zip(whole, columns):
-        for j, (source, i, width) in enumerate(column):
-            target[j, own] = source[i]
 
     def border(row_low, row_high):
         at = 0
-        for target, column in zip(whole, columns):
-            for j, (source, i, width) in enumerate(column):
-                target[j, tall - width : tall] = row_low[at : at + width]
-                target[j, rows : rows + width] = row_high[at : at + width]
-                at += width
+        for j, (source, i, width) in enumerate(sum(columns, [])):
+            halo[j, rows - width : rows] = row_low[at : at + width]
+            halo[j, 0:width] = row_high[at : at + width]
+            at += width
 
     odd = second_core()
     pl.when(odd)(lambda: border(inner, outer))
     pl.when(jnp.logical_not(odd))(lambda: border(outer, inner))
 
-    def first(j, carry):
-        rate_fuel, rate_heat = rates(
-            fuel_s, heat_s, j + 1, kappa_s[j], vel_z_s[j], vel_y_s[j]
-        )
-        fuel_one[j] = fuel_s[j + 1] + time_step * rate_fuel
-        heat_one[j] = heat_s[j + 1] + time_step * rate_heat
-        return carry
-
-    lax.fori_loop(0, planes + 2, first, 0)
-
-    def second(j, carry):
-        rate_fuel, rate_heat = rates(
-            fuel_one, heat_one, j + 1, kappa_s[j + 1], vel_z_s[j + 1], vel_y_s[j + 1]
-        )
-        fuel_two[j] = 0.5 * (fuel_s[j + 2] + fuel_one[j + 1] + time_step * rate_fuel)
-        heat_two[j] = 0.5 * (heat_s[j + 2] + heat_one[j + 1] + time_step * rate_heat)
-        return carry
-
-    lax.fori_loop(0, planes, second, 0)
+    parts_of = [slice(at, at + 128) for at in range(0, size, 128)]
+    lane = lax.broadcasted_iota(jnp.int32, (2 * rows, 128), 1)
+
+    def plane(field, j, m):
+        source, i, width = columns[field][j]
+        row = sum(len(column) for column in columns[:field]) + j
+        return jnp.concatenate([source[i, :, parts_of[m]], halo[row, :, parts_of[m]]], axis=0)
+
+    for j in range(planes + 2):
+        blocks = [[plane(f, j + 1, m) for m in range(len(parts_of))] for f in (0, 1)]
+        rolled = ({}, {})
+        for m, part in enumerate(parts_of):
+            fuels, heats = (
+                (
+                    blocks[f][m],
+                    plane(f, j + 2, m),
+                    plane(f, j, m),
+                    neighbours(blocks[f], m, lane, rolled[f]),
+                )
+                for f in (0, 1)
+            )
+            rate_fuel, rate_heat = rates(fuels, heats, *(plane(f, j, m) for f in (2, 3, 4)))
+            fuel_one[j, :, part] = fuels[0] + time_step * rate_fuel
+            heat_one[j, :, part] = heats[0] + time_step * rate_heat
+
+    for j in range(planes):
+        ones = (fuel_one, heat_one)
+        blocks = [[ref[j + 1, :, part] for part in parts_of] for ref in ones]
+        rolled = ({}, {})
+        for m, part in enumerate(parts_of):
+            fuels, heats = (
+                (
+                    blocks[f][m],
+                    ones[f][j + 2, :, part],
+                    ones[f][j, :, part],
+                    neighbours(blocks[f], m, lane, rolled[f]),
+                )
+                for f in (0, 1)
+            )
+            rate_fuel, rate_heat = rates(fuels, heats, *(plane(f, j + 1, m) for f in (2, 3, 4)))
+            final = 0.5 * (plane(0, j + 2, m) + fuels[0] + time_step * rate_fuel)
+            fuel_two[j, :, part] = final[:rows]
+            heat_two[j, :, part] = 0.5 * (plane(1, j + 2, m) + heats[0] + time_step * rate_heat)
 
     chunk = 2 * planes + 2
     count = size // 16
 
-    def send(value, at):
-        for m in range(size // 128):
-            tile = block_transpose(value[:, m * 128 : (m + 1) * 128])
+    def send(values, at):
+        groups = size // 128
+        tiles = [value[:, m * 128 : (m + 1) * 128] for value in values for m in range(groups)]
+        for i, tile in enumerate(block_transpose(tiles)):
+            row, m = at + i // groups, i % groups
             place = (8 * m - first_member(count)) % count
             before = min(8, count - place)
-            out[pl.ds(place * chunk + at, before, stride=chunk), :] = tile[:before]
+            out[pl.ds(place * chunk + row, before, stride=chunk), :] = tile[:before]
             if before < 8:
-                out[pl.ds(at, 8 - before, stride=chunk), :] = tile[before:]
+                out[pl.ds(row, 8 - before, stride=chunk), :] = tile[before:]
 
     lane = lax.broadcasted_iota(jnp.int32, (rows, size), 1)
     place = lane % 16
     borders = jnp.zeros((rows, size), jnp.float32)
     for p in range(planes):
-        level = heat_two[p, own]
-        send(level, p)
-        send(fuel_two[p, own], planes + p)
-        edge[p : p + 1] = heat_two[p, tall - 1 : tall]
+        level = heat_two[p, :rows]
+        send([level], p)
+        send([fuel_two[p]], planes + p)
+        edge[p : p + 1] = heat_two[p, 2 * rows - 1 : 2 * rows]
         edge[planes + p : planes + p + 1] = heat_two[p, rows : rows + 1]
         left = (place == p) & (lane >= 16)
         right = (place == planes + p) & (lane < size - 16)
         borders = jnp.where(left, pltpu.roll(level, p + 1, 1), borders)
         borders = jnp.where(right, pltpu.roll(level, size - 16 + planes + p, 1), borders)
-    send(edge[...], 2 * planes)
-    send(borders, 2 * planes + 1)
+    send([edge[...]], 2 * planes)
+    send([borders], 2 * planes + 1)
 
 
 def per_function(ref, *index):
@@ -267,30 +287,30 @@
     thick = per_function(density) * (-log2_e * opacity_scale)
     half = [0.5 * per_function(tint, c) for c in range(3)]
 
-    def one_plane(s, p, state):
+    def one_plane(at, s, p, state):
         passing, total, *colour = state
-        s = lax.rem(s + (count - first_member(count)), count)
-        at = s * chunk + p
-        level, fuel = fields[pl.ds(at, 1), :], fields[pl.ds(at + planes, 1), :]
+        level, fuel = fields[pl.ds(at + p, 1), :], fields[pl.ds(at + planes + p, 1), :]
         offset = level - mid
         survive = jnp.exp2(thick * jnp.exp2(narrow * (offset * offset)))
-        weight = passing * (1.0 - survive) * lights[p, pl.ds(s, 1)]
+        left = passing * survive
+        weight = (passing - left) * lights[p, pl.ds(s, 1)]
         colour = [value + weight * jnp.tanh(half[c] * fuel) for c, value in enumerate(colour)]
-        return (passing * survive, total + weight, *colour)
-
-    joint = 4
+        return (left, total + weight, *colour)
+
+    joint = 8
 
     def segments(i, state):
         for s in range(joint):
+            s = lax.rem(i * joint + s + (count - first_member(count)), count)
             for p in range(planes):
-                state = one_plane(i * joint + s, p, state)
+                state = one_plane(s * chunk, s, p, state)
         return state
 
     zero = jnp.zeros((8, 128), jnp.float32)
     state = lax.fori_loop(0, count // joint, segments, (zero + 1.0, zero, zero, zero, zero))
     passing, total, *colour = state
-    for c, value in enumerate([total + value for value in colour] + [passing]):
-        tile = block_transpose(value)
+    values = [total + value for value in colour] + [passing]
+    for c, tile in enumerate(block_transpose(values)):
         for k in range(8):
             out[k, c] = tile[:, 16 * k : 16 * k + 16]
 
@@ -323,11 +343,13 @@
     )(*fields, low, high)
     outer, inner = swap(outer, "rows", 1), swap(inner, "rows", 0)
 
-    tall = rows + 8
     chunk = 2 * planes + 2
-    scratch = [pltpu.VMEM((planes + 2 * deep, tall, columns), jnp.float32) for deep in depths]
+    tall = 2 * rows
+    deep_count = sum(planes + 2 * deep for deep in depths)
+    scratch = [pltpu.VMEM((deep_count, rows, columns), jnp.float32)]
     scratch += [pltpu.VMEM((planes + 2, tall, columns), jnp.float32)] * 2
-    scratch += [pltpu.VMEM((planes, tall, columns), jnp.float32)] * 2
+    scratch += [pltpu.VMEM((planes, tall, columns), jnp.float32)]
+    scratch += [pltpu.VMEM((planes, rows, columns), jnp.float32)]
     scratch += [pltpu.VMEM((2 * planes, columns), jnp.float32)]
     stepped = pl.pallas_call(
         step_kernel,

time: 74.4 us -> 74 us (level)
  no operation moved by 1% of the time
where the time goes in v6:
time: 74 us; the launch traced here: 73.6 us
  starting transfers between devices  41.8 us (56%)
  waiting for transfers between devices  25.8 us (35%)
  Pallas kernels  5.74 us (8%)
    all_to_all x1, starting transfers between devices, body(): lax.all_to_all(stepped.reshape(depth_count, 1, chunk * 128), 'depth', spl...  31.2 us
    all_to_all x1, waiting for transfers between devices, body(): lax.all_to_all(stepped.reshape(depth_count, 1, chunk * 128), 'depth', spl...  17.4 us
    ppermute x2, starting transfers between devices, swap(): lax.ppermute(block, axis, forward + [(target, source) for source, target...  5.51 us
    ppermute x1, waiting for transfers between devices, exchange(): lax.ppermute(to_prev, axis, backward)  4.31 us
    ppermute x1, starting transfers between devices, exchange(): lax.ppermute(to_next, axis, forward)  3.83 us
    ppermute x2, waiting for transfers between devices, swap(): lax.ppermute(block, axis, forward + [(target, source) for source, target...  3.05 us
    pallas_call x1, Pallas kernels, body(): pl.pallas_call(step_kernel, out_shape=f32((depth_count * chunk, 128)), in...  2.36 us
    pallas_call x1, Pallas kernels, body(): pl.pallas_call(functools.partial(march_kernel, 4.0 / (planes * depth_coun...  2.31 us
  transfers between devices with their start and end apart: 5, of which 4 were waited for; matrix products, arithmetic and copies ran while one was open for 0% of the time, Pallas kernels for 0%

profile of v6, /device:TPU:6, one launch (start us, length us, event | category | flops | bytes accessed | tf_op | source)
XLA Modules:
  0.0 73.6 jit_solution(7194139944718804648)
XLA Ops:
  0.0 0.0 copy-start.4
  0.0 0.0 copy-start
  0.0 0.9 %pack_planes.1 = (f32[7,8,512]{2,1,0:T(8,128)S(1)}, f32[7,8,512]{2,1,0:T(8,128)S(1)}) custom-call(f32[4,8,512]{2,1,0:T(8,128)} %fuel.5, f32[4,8,512]{2,1,0:T(8,128)} %heat.5, f32[4,8,512]{2,1,0:T(8,128)} %kappa.5, f32[4,8,512]{2,1,0:T(8,128)} %vel_z.5, f32[4,8,512]{2,1,0:T(8,128)} %vel_y.5), custom_call_target="tpu_custom_call" | custom-call | tf_op jit(solution)/shard_map/pack_planes/pallas_call | solution.py:326
  1.0 3.8 %collective-permute-start = (f32[7,8,512]{2,1,0:T(8,128)S(1)}, f32[7,8,512]{2,1,0:T(8,128)S(1)}, u32[]{:S(2)}, u32[]{:S(2)}) collective-permute-start(f32[7,8,512]{2,1,0:T(8,128)S(1)} %get-tuple-element.9), channel_id=1, source_target_pairs={{0,32},{32,64},{64,96},{96,128},{128,160},{160,192},{192,224},{224... | collective-permute-start | bytes 344072 | tf_op jit(solution)/shard_map/ppermute | solution.py:32
  4.8 1.3 %collective-permute-start.1 = (f32[7,8,512]{2,1,0:T(8,128)S(1)}, f32[7,8,512]{2,1,0:T(8,128)S(1)}, u32[]{:S(2)}, u32[]{:S(2)}) collective-permute-start(f32[7,8,512]{2,1,0:T(8,128)S(1)} %get-tuple-element.10), channel_id=1, source_target_pairs={{32,0},{64,32},{96,64},{128,96},{160,128},{192,160},{224,192},{256... | collective-permute-start | bytes 344072 | tf_op jit(solution)/shard_map/ppermute | solution.py:32
  6.1 1.1 %collective-permute-done.low = f32[7,8,512]{2,1,0:T(8,128)S(1)} collective-permute-done((f32[7,8,512]{2,1,0:T(8,128)S(1)}, f32[7,8,512]{2,1,0:T(8,128)S(1)}, u32[]{:S(2)}, u32[]{:S(2)}) %collective-permute-start) | collective-permute-done | bytes 114720 | tf_op jit(solution)/shard_map/ppermute | solution.py:32
  7.2 4.3 %collective-permute-done.1.high = f32[7,8,512]{2,1,0:T(8,128)S(1)} collective-permute-done((f32[7,8,512]{2,1,0:T(8,128)S(1)}, f32[7,8,512]{2,1,0:T(8,128)S(1)}, u32[]{:S(2)}, u32[]{:S(2)}) %collective-permute-start.1) | collective-permute-done | bytes 114720 | tf_op jit(solution)/shard_map/ppermute | solution.py:32
  11.5 0.0 copy-done.1
  11.5 0.0 copy-done.2
  11.5 0.0 copy-done.3
  11.5 0.0 copy-done.4
  11.5 0.0 copy-done
  11.5 0.1 pack_rows.1
  11.7 3.4 %collective-permute-start.2 = (f32[66,512]{1,0:T(8,128)S(1)}, f32[66,512]{1,0:T(8,128)S(1)}, u32[]{:S(2)}, u32[]{:S(2)}) collective-permute-start(f32[66,512]{1,0:T(8,128)S(1)} %get-tuple-element.11), channel_id=1, source_target_pairs={{1,2},{3,4},{5,6},{7,8},{9,10},{11,12},{13,14},{15,16},{17,18},{19... | collective-permute-start | bytes 405512 | tf_op jit(solution)/shard_map/ppermute | solution.py:38
  15.1 2.1 %collective-permute-start.3 = (f32[66,512]{1,0:T(8,128)S(1)}, f32[66,512]{1,0:T(8,128)S(1)}, u32[]{:S(2)}, u32[]{:S(2)}) collective-permute-start(f32[66,512]{1,0:T(8,128)S(1)} %get-tuple-element.12), channel_id=1, source_target_pairs={{0,1},{2,3},{4,5},{6,7},{8,9},{10,11},{12,13},{14,15},{16,17},{18,... | collective-permute-start | bytes 405512 | tf_op jit(solution)/shard_map/ppermute | solution.py:38
  17.2 3.0 %collective-permute-done.2.outer = f32[66,512]{1,0:T(8,128)S(1)} collective-permute-done((f32[66,512]{1,0:T(8,128)S(1)}, f32[66,512]{1,0:T(8,128)S(1)}, u32[]{:S(2)}, u32[]{:S(2)}) %collective-permute-start.2) | collective-permute-done | bytes 135200 | tf_op jit(solution)/shard_map/ppermute | solution.py:38
  20.2 0.0 collective-permute-done.3.inner
  20.2 2.4 %step.1 = f32[320,128]{1,0:T(8,128)} custom-call(f32[4,8,512]{2,1,0:T(8,128)S(1)} %copy-done, f32[4,8,512]{2,1,0:T(8,128)S(1)} %copy-done.1, f32[4,8,512]{2,1,0:T(8,128)S(1)} %copy-done.2, f32[4,8,512]{2,1,0:T(8,128)S(1)} %copy-done.3, f32[4,8,512]{2,1,0:T(8,128)S(1)} %copy-done.4, f32[7,8,512]{2,1,0:T(8,128)S(1)} %collective-permute-done.low, ...), custom_call_target="tpu_custom_call" | custom-call | tf_op jit(solution)/shard_map/step/pallas_call | solution.py:354
  22.6 31.2 %all-to-all-start = ((f32[32,1,1280]{2,1,0:T(1,128)}), f32[32,1,1280]{2,1,0:T(1,128)S(1)}, u32[]{:S(2)}, u32[]{:S(2)}) async-start(f32[32,1,1280]{2,1,0:T(1,128)} %bitcast), calls=%async_computation | async-start | bytes 327680 | tf_op jit(solution)/shard_map/all_to_all | solution.py:365
  53.8 0.0 copy-done.8
  53.8 0.1 copy.12.tint
  53.9 17.4 %all-to-all-done = f32[32,1,1280]{2,1,0:T(1,128)S(1)} async-done(((f32[32,1,1280]{2,1,0:T(1,128)}), f32[32,1,1280]{2,1,0:T(1,128)S(1)}, u32[]{:S(2)}, u32[]{:S(2)}) %all-to-all-start) | async-done | bytes 163872 | tf_op jit(solution)/shard_map/all_to_all | solution.py:365
  71.3 0.0 copy-done.7
  71.3 2.3 %march.1 = f32[8,4,8,16]{3,2,1,0:T(8,128)} custom-call(f32[8]{0:T(128)S(1)} %copy-done.5, f32[8]{0:T(128)S(1)} %copy-done.6, f32[8]{0:T(128)S(1)} %copy-done.7, f32[8,3]{1,0:T(8,128)S(1)} %copy.12.tint, f32[320,128]{1,0:T(8,128)S(1)} %bitcast.2), custom_call_target="tpu_custom_call" | custom-call | tf_op jit(solution)/shard_map/march/pallas_call | solution.py:374
  (9 shorter events, 0.0 us)
Async XLA Ops:
  0.0 11.5 %copy-start.1 = (f32[4,8,512]{2,1,0:T(8,128)S(1)}, f32[4,8,512]{2,1,0:T(8,128)}, u32[]{:S(2)}) copy-start(f32[4,8,512]{2,1,0:T(8,128)} %heat.5) | copy-start | bytes 196612
  0.0 11.5 %copy-start.2 = (f32[4,8,512]{2,1,0:T(8,128)S(1)}, f32[4,8,512]{2,1,0:T(8,128)}, u32[]{:S(2)}) copy-start(f32[4,8,512]{2,1,0:T(8,128)} %kappa.5) | copy-start | bytes 196612
  0.0 11.5 %copy-start.3 = (f32[4,8,512]{2,1,0:T(8,128)S(1)}, f32[4,8,512]{2,1,0:T(8,128)}, u32[]{:S(2)}) copy-start(f32[4,8,512]{2,1,0:T(8,128)} %vel_z.5) | copy-start | bytes 196612
  0.0 11.5 %copy-start.4 = (f32[4,8,512]{2,1,0:T(8,128)S(1)}, f32[4,8,512]{2,1,0:T(8,128)}, u32[]{:S(2)}) copy-start(f32[4,8,512]{2,1,0:T(8,128)} %vel_y.5) | copy-start | bytes 196612
  0.0 11.5 %copy-start = (f32[4,8,512]{2,1,0:T(8,128)S(1)}, f32[4,8,512]{2,1,0:T(8,128)}, u32[]{:S(2)}) copy-start(f32[4,8,512]{2,1,0:T(8,128)} %fuel.5) | copy-start | bytes 196612
  1.0 6.2 %collective-permute-start = (f32[7,8,512]{2,1,0:T(8,128)S(1)}, f32[7,8,512]{2,1,0:T(8,128)S(1)}, u32[]{:S(2)}, u32[]{:S(2)}) collective-permute-start(f32[7,8,512]{2,1,0:T(8,128)S(1)} %get-tuple-element.9), channel_id=1, source_target_pairs={{0,32},{32,64},{64,96},{96,128},{128,160},{160,192},{192,224},{224... | collective-permute-start | bytes 344072 | tf_op jit(solution)/shard_map/ppermute | solution.py:32
  4.8 6.7 %collective-permute-start.1 = (f32[7,8,512]{2,1,0:T(8,128)S(1)}, f32[7,8,512]{2,1,0:T(8,128)S(1)}, u32[]{:S(2)}, u32[]{:S(2)}) collective-permute-start(f32[7,8,512]{2,1,0:T(8,128)S(1)} %get-tuple-element.10), channel_id=1, source_target_pairs={{32,0},{64,32},{96,64},{128,96},{160,128},{192,160},{224,192},{256... | collective-permute-start | bytes 344072 | tf_op jit(solution)/shard_map/ppermute | solution.py:32
  11.7 8.6 %collective-permute-start.2 = (f32[66,512]{1,0:T(8,128)S(1)}, f32[66,512]{1,0:T(8,128)S(1)}, u32[]{:S(2)}, u32[]{:S(2)}) collective-permute-start(f32[66,512]{1,0:T(8,128)S(1)} %get-tuple-element.11), channel_id=1, source_target_pairs={{1,2},{3,4},{5,6},{7,8},{9,10},{11,12},{13,14},{15,16},{17,18},{19... | collective-permute-start | bytes 405512 | tf_op jit(solution)/shard_map/ppermute | solution.py:38
  15.1 5.2 %collective-permute-start.3 = (f32[66,512]{1,0:T(8,128)S(1)}, f32[66,512]{1,0:T(8,128)S(1)}, u32[]{:S(2)}, u32[]{:S(2)}) collective-permute-start(f32[66,512]{1,0:T(8,128)S(1)} %get-tuple-element.12), channel_id=1, source_target_pairs={{0,1},{2,3},{4,5},{6,7},{8,9},{10,11},{12,13},{14,15},{16,17},{18,... | collective-permute-start | bytes 405512 | tf_op jit(solution)/shard_map/ppermute | solution.py:38
  22.6 31.2 %copy-start.8 = (f32[8,3]{0,1:T(4,128)S(1)}, f32[8,3]{0,1:T(4,128)}, u32[]{:S(2)}) copy-start(f32[8,3]{0,1:T(4,128)} %param.17) | copy-start | bytes 292
  22.6 48.7 %all-to-all-start = ((f32[32,1,1280]{2,1,0:T(1,128)}), f32[32,1,1280]{2,1,0:T(1,128)S(1)}, u32[]{:S(2)}, u32[]{:S(2)}) async-start(f32[32,1,1280]{2,1,0:T(1,128)} %bitcast), calls=%async_computation | async-start | bytes 327680 | tf_op jit(solution)/shard_map/all_to_all | solution.py:365
  53.9 17.4 %copy-start.5 = (f32[8]{0:T(128)S(1)}, f32[8]{0:T(128)}, u32[]{:S(2)}) copy-start(f32[8]{0:T(128)} %centre.1) | copy-start | bytes 100
  53.9 17.4 %copy-start.6 = (f32[8]{0:T(128)S(1)}, f32[8]{0:T(128)}, u32[]{:S(2)}) copy-start(f32[8]{0:T(128)} %width.1) | copy-start | bytes 100
  53.9 17.4 %copy-start.7 = (f32[8]{0:T(128)S(1)}, f32[8]{0:T(128)}, u32[]{:S(2)}) copy-start(f32[8]{0:T(128)} %density.1) | copy-start | bytes 100

commit v7 on v6

--- a/solution.py
+++ b/solution.py
@@ -13,6 +13,8 @@
 heat_release = 0.6
 burn_rate = 0.5
 
+befores = (3, 3, 2, 2, 2)
+afters = (1, 1, 0, 0, 0)
 depths = (2, 2, 1, 1, 1)
 log2_e = math.log2(math.e)
 
@@ -27,8 +29,8 @@
 
 def exchange(to_next, to_prev, axis):
     count = lax.axis_size(axis)
-    forward = [(i, i + 1) for i in range(count - 1)]
-    backward = [(target, source) for source, target in forward]
+    forward = [(i, (i + 1) % count) for i in range(count)]
+    backward = [(i + 1, i) for i in range(count - 1)]
     return lax.ppermute(to_next, axis, forward), lax.ppermute(to_prev, axis, backward)
 
 
@@ -48,17 +50,19 @@
 
 def planes_kernel(fuel, heat, kappa, vel_z, vel_y, to_next, to_prev, arrived):
     planes = fuel.shape[0]
-    at, copies = 0, []
-    for field, deep in zip((fuel, heat, kappa, vel_z, vel_y), depths):
-        for source, target in ((planes - deep, to_next), (0, to_prev)):
-            copies.append(
-                pltpu.make_async_copy(
-                    field.at[pl.ds(source, deep)],
-                    target.at[pl.ds(at, deep)],
-                    arrived.at[len(copies)],
-                )
-            )
-        at += deep
+    fields = (fuel, heat, kappa, vel_z, vel_y)
+    copies = []
+    for target, widths, last in ((to_next, befores, True), (to_prev, afters, False)):
+        at = 0
+        for field, width in zip(fields, widths):
+            if width:
+                source = field.at[pl.ds(planes - width if last else 0, width)]
+                copies.append((source, target.at[pl.ds(at, width)]))
+            at += width
+    copies = [
+        pltpu.make_async_copy(source, target, arrived.at[i])
+        for i, (source, target) in enumerate(copies)
+    ]
     for copy in copies:
         copy.start()
     for copy in copies:
@@ -67,14 +71,17 @@
 
 def deep_planes(fields, low, high):
     planes = fields[0].shape[0]
-    at = 0
+    at_low = at_high = 0
     columns = []
-    for field, deep in zip(fields, depths):
-        column = [(low, at + i, 1 + i) for i in range(deep)]
-        column += [(field, i, 1 + deep) for i in range(planes)]
-        column += [(high, at + i, deep - i) for i in range(deep)]
-        columns.append(column)
-        at += deep
+    for field, before, after, deep in zip(fields, befores, afters, depths):
+        column = [(low, at_low + i) for i in range(before)]
+        column += [(field, i) for i in range(planes)]
+        column += [(high, at_high + i) for i in range(after)]
+        last = len(column) - 1
+        columns.append(
+            [(*plane, 1 + min(deep, j, last - j)) for j, plane in enumerate(column)]
+        )
+        at_low, at_high = at_low + before, at_high + after
     return columns
 
 
@@ -170,6 +177,8 @@
         row = sum(len(column) for column in columns[:field]) + j
         return jnp.concatenate([source[i, :, parts_of[m]], halo[row, :, parts_of[m]]], axis=0)
 
+    coupled = jnp.where(lax.axis_index("depth") > 0, 1.0, 0.0)
+
     for j in range(planes + 2):
         blocks = [[plane(f, j + 1, m) for m in range(len(parts_of))] for f in (0, 1)]
         rolled = ({}, {})
@@ -177,8 +186,8 @@
             fuels, heats = (
                 (
                     blocks[f][m],
-                    plane(f, j + 2, m),
-                    plane(f, j, m),
+                    plane(f, j + 2, m) * (coupled if j == 1 else 1.0),
+                    plane(f, j, m) * (coupled if j == 2 else 1.0),
                     neighbours(blocks[f], m, lane, rolled[f]),
                 )
                 for f in (0, 1)
@@ -195,8 +204,8 @@
             fuels, heats = (
                 (
                     blocks[f][m],
-                    ones[f][j + 2, :, part],
-                    ones[f][j, :, part],
+                    ones[f][j + 2, :, part] * (coupled if j == 0 else 1.0),
+                    ones[f][j, :, part] * (coupled if j == 1 else 1.0),
                     neighbours(blocks[f], m, lane, rolled[f]),
                 )
                 for f in (0, 1)
@@ -245,15 +254,6 @@
     return value
 
 
-def shift_rows(value, step):
-    size = value.shape[0]
-    row = lax.broadcasted_iota(jnp.int32, value.shape, 0)
-    start = (size - first_member(size)) % size
-    if step > 0:
-        return jnp.where(row != (start - 1) % size, pltpu.roll(value, size - 1, 0), 0.0)
-    return jnp.where(row != start, pltpu.roll(value, 1, 0), 0.0)
-
-
 def march_kernel(opacity_scale, planes, centre, width, density, tint, fields, out, lights):
     chunk = 2 * planes + 2
     count = fields.shape[0] // chunk
@@ -263,10 +263,16 @@
     )
     lane = lax.broadcasted_iota(jnp.int32, (count, 128), 1)
     place = lane % 16
+    row = lax.broadcasted_iota(jnp.int32, (count, 128), 0)
+    coupled = row != (count - first_member(count)) % count
     for p in range(planes):
         level = columns[p]
-        ahead = columns[p + 1] if p + 1 < planes else shift_rows(columns[0], 1)
-        behind = columns[p - 1] if p > 0 else shift_rows(columns[planes - 1], -1)
+        ahead = columns[p + 1] if p + 1 < planes else pltpu.roll(columns[0], count - 1, 0)
+        behind = columns[p - 1] if p > 0 else pltpu.roll(columns[planes - 1], 1, 0)
+        if p == 0:
+            ahead = jnp.where(coupled, ahead, 0.0)
+        if p == 1:
+            behind = jnp.where(coupled, behind, 0.0)
 
         def moved(value, by):
             by = by % 128
@@ -301,9 +307,11 @@
 
     def segments(i, state):
         for s in range(joint):
-            s = lax.rem(i * joint + s + (count - first_member(count)), count)
-            for p in range(planes):
-                state = one_plane(s * chunk, s, p, state)
+            s = i * joint + s + (count - first_member(count))
+            now, after = lax.rem(s, count), lax.rem(s + 1, count)
+            for p in range(1, planes):
+                state = one_plane(now * chunk, now, p, state)
+            state = one_plane(after * chunk, after, 0, state)
         return state
 
     zero = jnp.zeros((8, 128), jnp.float32)
@@ -320,12 +328,11 @@
     depth_count = lax.axis_size("depth")
     fields = (fuel, heat, kappa, vel_z, vel_y)
     f32 = functools.partial(jax.ShapeDtypeStruct, dtype=jnp.float32)
-    sent_planes = sum(depths)
     sent_rows = sum(planes * (1 + deep) + deep * (1 + deep) for deep in depths)
 
     to_next, to_prev = pl.pallas_call(
         planes_kernel,
-        out_shape=[f32((sent_planes, rows, columns))] * 2,
+        out_shape=[f32((sum(widths), rows, columns)) for widths in (befores, afters)],
         in_specs=[hbm] * 5,
         out_specs=[vmem] * 2,
         scratch_shapes=[pltpu.SemaphoreType.DMA((2 * len(depths),))],

time: 74 us -> 73.3 us (level)
  starting transfers between devices: 41.8 us -> 28.3 us
  waiting for transfers between devices: 25.8 us -> 38.5 us
    all_to_all x1, starting transfers between devices: 31.2 us -> 17.2 us  [body(): lax.all_to_all(stepped.reshape(depth_count, 1, chunk * 128), 'depth', spl...]
    ppermute x1, waiting for transfers between devices: 1.08 us -> 13.9 us  [exchange(): lax.ppermute(to_next, axis, forward)]
where the time goes in v7:
time: 73.3 us; the launch traced here: 72.9 us
  waiting for transfers between devices  38.5 us (53%)
  starting transfers between devices  28.3 us (39%)
  Pallas kernels  5.77 us (8%)
    all_to_all x1, waiting for transfers between devices, body(): lax.all_to_all(stepped.reshape(depth_count, 1, chunk * 128), 'depth', spl...  17.5 us
    all_to_all x1, starting transfers between devices, body(): lax.all_to_all(stepped.reshape(depth_count, 1, chunk * 128), 'depth', spl...  17.2 us
    ppermute x1, waiting for transfers between devices, exchange(): lax.ppermute(to_next, axis, forward)  13.9 us
    ppermute x2, starting transfers between devices, swap(): lax.ppermute(block, axis, forward + [(target, source) for source, target...  5.97 us
    ppermute x1, waiting for transfers between devices, exchange(): lax.ppermute(to_prev, axis, backward)  4.51 us
    ppermute x1, starting transfers between devices, exchange(): lax.ppermute(to_next, axis, forward)  3.83 us
    ppermute x2, waiting for transfers between devices, swap(): lax.ppermute(block, axis, forward + [(target, source) for source, target...  2.59 us
    pallas_call x1, Pallas kernels, body(): pl.pallas_call(step_kernel, out_shape=f32((depth_count * chunk, 128)), in...  2.37 us
  transfers between devices with their start and end apart: 5, of which 4 were waited for; matrix products, arithmetic and copies ran while one was open for 0% of the time, Pallas kernels for 0%

profile of v7, /device:TPU:6, one launch (start us, length us, event | category | flops | bytes accessed | tf_op | source)
XLA Modules:
  0.0 72.9 jit_solution(10755267232921349578)
XLA Ops:
  0.0 0.0 copy-start.4
  0.0 0.0 copy-start
  0.0 1.0 %pack_planes.1 = (f32[12,8,512]{2,1,0:T(8,128)S(1)}, f32[2,8,512]{2,1,0:T(8,128)S(1)}) custom-call(f32[4,8,512]{2,1,0:T(8,128)} %fuel.5, f32[4,8,512]{2,1,0:T(8,128)} %heat.5, f32[4,8,512]{2,1,0:T(8,128)} %kappa.5, f32[4,8,512]{2,1,0:T(8,128)} %vel_z.5, f32[4,8,512]{2,1,0:T(8,128)} %vel_y.5), custom_call_target="tpu_custom_call" | custom-call | tf_op jit(solution)/shard_map/pack_planes/pallas_call | solution.py:333
  1.0 3.8 %collective-permute-start = (f32[12,8,512]{2,1,0:T(8,128)S(1)}, f32[12,8,512]{2,1,0:T(8,128)S(1)}, u32[]{:S(2)}, u32[]{:S(2)}) collective-permute-start(f32[12,8,512]{2,1,0:T(8,128)S(1)} %get-tuple-element.9), channel_id=1, source_target_pairs={{0,32},{32,64},{64,96},{96,128},{128,160},{160,192},{192,224},{224... | collective-permute-start | bytes 589832 | tf_op jit(solution)/shard_map/ppermute | solution.py:34
  4.8 1.3 %collective-permute-start.1 = (f32[2,8,512]{2,1,0:T(8,128)S(1)}, f32[2,8,512]{2,1,0:T(8,128)S(1)}, u32[]{:S(2)}, u32[]{:S(2)}) collective-permute-start(f32[2,8,512]{2,1,0:T(8,128)S(1)} %get-tuple-element.10), channel_id=1, source_target_pairs={{32,0},{64,32},{96,64},{128,96},{160,128},{192,160},{224,192},{256... | collective-permute-start | bytes 98312 | tf_op jit(solution)/shard_map/ppermute | solution.py:34
  6.1 4.5 %collective-permute-done.1.high = f32[2,8,512]{2,1,0:T(8,128)S(1)} collective-permute-done((f32[2,8,512]{2,1,0:T(8,128)S(1)}, f32[2,8,512]{2,1,0:T(8,128)S(1)}, u32[]{:S(2)}, u32[]{:S(2)}) %collective-permute-start.1) | collective-permute-done | bytes 32800 | tf_op jit(solution)/shard_map/ppermute | solution.py:34
  10.7 13.9 %collective-permute-done.low = f32[12,8,512]{2,1,0:T(8,128)S(1)} collective-permute-done((f32[12,8,512]{2,1,0:T(8,128)S(1)}, f32[12,8,512]{2,1,0:T(8,128)S(1)}, u32[]{:S(2)}, u32[]{:S(2)}) %collective-permute-start) | collective-permute-done | bytes 196640 | tf_op jit(solution)/shard_map/ppermute | solution.py:34
  24.6 0.0 copy-done.1
  24.6 0.0 copy-done.2
  24.6 0.0 copy-done.3
  24.6 0.0 copy-done.4
  24.6 0.0 copy-done
  24.6 0.1 pack_rows.1
  24.7 4.1 %collective-permute-start.2 = (f32[66,512]{1,0:T(8,128)S(1)}, f32[66,512]{1,0:T(8,128)S(1)}, u32[]{:S(2)}, u32[]{:S(2)}) collective-permute-start(f32[66,512]{1,0:T(8,128)S(1)} %get-tuple-element.11), channel_id=1, source_target_pairs={{1,2},{3,4},{5,6},{7,8},{9,10},{11,12},{13,14},{15,16},{17,18},{19... | collective-permute-start | bytes 405512 | tf_op jit(solution)/shard_map/ppermute | solution.py:40
  28.8 1.9 %collective-permute-start.3 = (f32[66,512]{1,0:T(8,128)S(1)}, f32[66,512]{1,0:T(8,128)S(1)}, u32[]{:S(2)}, u32[]{:S(2)}) collective-permute-start(f32[66,512]{1,0:T(8,128)S(1)} %get-tuple-element.12), channel_id=1, source_target_pairs={{0,1},{2,3},{4,5},{6,7},{8,9},{10,11},{12,13},{14,15},{16,17},{18,... | collective-permute-start | bytes 405512 | tf_op jit(solution)/shard_map/ppermute | solution.py:40
  30.7 2.6 %collective-permute-done.2.outer = f32[66,512]{1,0:T(8,128)S(1)} collective-permute-done((f32[66,512]{1,0:T(8,128)S(1)}, f32[66,512]{1,0:T(8,128)S(1)}, u32[]{:S(2)}, u32[]{:S(2)}) %collective-permute-start.2) | collective-permute-done | bytes 135200 | tf_op jit(solution)/shard_map/ppermute | solution.py:40
  33.3 0.0 collective-permute-done.3.inner
  33.3 2.4 %step.1 = f32[320,128]{1,0:T(8,128)} custom-call(f32[4,8,512]{2,1,0:T(8,128)S(1)} %copy-done, f32[4,8,512]{2,1,0:T(8,128)S(1)} %copy-done.1, f32[4,8,512]{2,1,0:T(8,128)S(1)} %copy-done.2, f32[4,8,512]{2,1,0:T(8,128)S(1)} %copy-done.3, f32[4,8,512]{2,1,0:T(8,128)S(1)} %copy-done.4, f32[12,8,512]{2,1,0:T(8,128)S(1)} %collective-permute-done.low, ...), custom_call_target="tpu_custom_call" | custom-call | tf_op jit(solution)/shard_map/step/pallas_call | solution.py:361
  35.7 17.2 %all-to-all-start = ((f32[32,1,1280]{2,1,0:T(1,128)}), f32[32,1,1280]{2,1,0:T(1,128)S(1)}, u32[]{:S(2)}, u32[]{:S(2)}) async-start(f32[32,1,1280]{2,1,0:T(1,128)} %bitcast), calls=%async_computation | async-start | bytes 327680 | tf_op jit(solution)/shard_map/all_to_all | solution.py:372
  52.9 0.0 copy-done.8
  53.0 0.1 copy.12.tint
  53.0 17.5 %all-to-all-done = f32[32,1,1280]{2,1,0:T(1,128)S(1)} async-done(((f32[32,1,1280]{2,1,0:T(1,128)}), f32[32,1,1280]{2,1,0:T(1,128)S(1)}, u32[]{:S(2)}, u32[]{:S(2)}) %all-to-all-start) | async-done | bytes 163872 | tf_op jit(solution)/shard_map/all_to_all | solution.py:372
  70.6 0.0 copy-done.5
  70.6 2.3 %march.1 = f32[8,4,8,16]{3,2,1,0:T(8,128)} custom-call(f32[8]{0:T(128)S(1)} %copy-done.5, f32[8]{0:T(128)S(1)} %copy-done.6, f32[8]{0:T(128)S(1)} %copy-done.7, f32[8,3]{1,0:T(8,128)S(1)} %copy.12.tint, f32[320,128]{1,0:T(8,128)S(1)} %bitcast.2), custom_call_target="tpu_custom_call" | custom-call | tf_op jit(solution)/shard_map/march/pallas_call | solution.py:381
  (9 shorter events, 0.0 us)
Async XLA Ops:
  0.0 24.6 %copy-start.1 = (f32[4,8,512]{2,1,0:T(8,128)S(1)}, f32[4,8,512]{2,1,0:T(8,128)}, u32[]{:S(2)}) copy-start(f32[4,8,512]{2,1,0:T(8,128)} %heat.5) | copy-start | bytes 196612
  0.0 24.6 %copy-start.2 = (f32[4,8,512]{2,1,0:T(8,128)S(1)}, f32[4,8,512]{2,1,0:T(8,128)}, u32[]{:S(2)}) copy-start(f32[4,8,512]{2,1,0:T(8,128)} %kappa.5) | copy-start | bytes 196612
  0.0 24.6 %copy-start.3 = (f32[4,8,512]{2,1,0:T(8,128)S(1)}, f32[4,8,512]{2,1,0:T(8,128)}, u32[]{:S(2)}) copy-start(f32[4,8,512]{2,1,0:T(8,128)} %vel_z.5) | copy-start | bytes 196612
  0.0 24.6 %copy-start.4 = (f32[4,8,512]{2,1,0:T(8,128)S(1)}, f32[4,8,512]{2,1,0:T(8,128)}, u32[]{:S(2)}) copy-start(f32[4,8,512]{2,1,0:T(8,128)} %vel_y.5) | copy-start | bytes 196612
  0.0 24.6 %copy-start = (f32[4,8,512]{2,1,0:T(8,128)S(1)}, f32[4,8,512]{2,1,0:T(8,128)}, u32[]{:S(2)}) copy-start(f32[4,8,512]{2,1,0:T(8,128)} %fuel.5) | copy-start | bytes 196612
  1.0 23.6 %collective-permute-start = (f32[12,8,512]{2,1,0:T(8,128)S(1)}, f32[12,8,512]{2,1,0:T(8,128)S(1)}, u32[]{:S(2)}, u32[]{:S(2)}) collective-permute-start(f32[12,8,512]{2,1,0:T(8,128)S(1)} %get-tuple-element.9), channel_id=1, source_target_pairs={{0,32},{32,64},{64,96},{96,128},{128,160},{160,192},{192,224},{224... | collective-permute-start | bytes 589832 | tf_op jit(solution)/shard_map/ppermute | solution.py:34
  4.8 5.8 %collective-permute-start.1 = (f32[2,8,512]{2,1,0:T(8,128)S(1)}, f32[2,8,512]{2,1,0:T(8,128)S(1)}, u32[]{:S(2)}, u32[]{:S(2)}) collective-permute-start(f32[2,8,512]{2,1,0:T(8,128)S(1)} %get-tuple-element.10), channel_id=1, source_target_pairs={{32,0},{64,32},{96,64},{128,96},{160,128},{192,160},{224,192},{256... | collective-permute-start | bytes 98312 | tf_op jit(solution)/shard_map/ppermute | solution.py:34
  24.7 8.6 %collective-permute-start.2 = (f32[66,512]{1,0:T(8,128)S(1)}, f32[66,512]{1,0:T(8,128)S(1)}, u32[]{:S(2)}, u32[]{:S(2)}) collective-permute-start(f32[66,512]{1,0:T(8,128)S(1)} %get-tuple-element.11), channel_id=1, source_target_pairs={{1,2},{3,4},{5,6},{7,8},{9,10},{11,12},{13,14},{15,16},{17,18},{19... | collective-permute-start | bytes 405512 | tf_op jit(solution)/shard_map/ppermute | solution.py:40
  28.8 4.5 %collective-permute-start.3 = (f32[66,512]{1,0:T(8,128)S(1)}, f32[66,512]{1,0:T(8,128)S(1)}, u32[]{:S(2)}, u32[]{:S(2)}) collective-permute-start(f32[66,512]{1,0:T(8,128)S(1)} %get-tuple-element.12), channel_id=1, source_target_pairs={{0,1},{2,3},{4,5},{6,7},{8,9},{10,11},{12,13},{14,15},{16,17},{18,... | collective-permute-start | bytes 405512 | tf_op jit(solution)/shard_map/ppermute | solution.py:40
  35.7 17.3 %copy-start.8 = (f32[8,3]{0,1:T(4,128)S(1)}, f32[8,3]{0,1:T(4,128)}, u32[]{:S(2)}) copy-start(f32[8,3]{0,1:T(4,128)} %param.17) | copy-start | bytes 292
  35.7 34.9 %all-to-all-start = ((f32[32,1,1280]{2,1,0:T(1,128)}), f32[32,1,1280]{2,1,0:T(1,128)S(1)}, u32[]{:S(2)}, u32[]{:S(2)}) async-start(f32[32,1,1280]{2,1,0:T(1,128)} %bitcast), calls=%async_computation | async-start | bytes 327680 | tf_op jit(solution)/shard_map/all_to_all | solution.py:372
  53.0 17.5 %copy-start.5 = (f32[8]{0:T(128)S(1)}, f32[8]{0:T(128)}, u32[]{:S(2)}) copy-start(f32[8]{0:T(128)} %centre.1) | copy-start | bytes 100
  53.0 17.5 %copy-start.6 = (f32[8]{0:T(128)S(1)}, f32[8]{0:T(128)}, u32[]{:S(2)}) copy-start(f32[8]{0:T(128)} %width.1) | copy-start | bytes 100
  53.0 17.5 %copy-start.7 = (f32[8]{0:T(128)S(1)}, f32[8]{0:T(128)}, u32[]{:S(2)}) copy-start(f32[8]{0:T(128)} %density.1) | copy-start | bytes 100

commit v8 on v7

--- a/solution.py
+++ b/solution.py
@@ -254,7 +254,16 @@
     return value
 
 
-def march_kernel(opacity_scale, planes, centre, width, density, tint, fields, out, lights):
+def functions_kernel(opacity_scale, centre, width, density, tint, out):
+    spread = per_function(width)
+    out[0] = per_function(centre)
+    out[1] = -log2_e / (spread * spread)
+    out[2] = per_function(density) * (-log2_e * opacity_scale)
+    for c in range(3):
+        out[3 + c] = 0.5 * per_function(tint, c)
+
+
+def march_kernel(planes, functions, fields, out, lights):
     chunk = 2 * planes + 2
     count = fields.shape[0] // chunk
     columns = [fields[pl.ds(i, count, stride=chunk), :] for i in range(planes)]
@@ -287,11 +296,7 @@
         facing = 0.48 * grad_z + 0.6 * grad_y + 0.64 * grad_x
         lights[p] = 0.5 * (0.35 + 0.65 * (facing * facing) / norm_sq)
 
-    mid = per_function(centre)
-    spread = per_function(width)
-    narrow = -log2_e / (spread * spread)
-    thick = per_function(density) * (-log2_e * opacity_scale)
-    half = [0.5 * per_function(tint, c) for c in range(3)]
+    mid, narrow, thick, *half = (functions[i] for i in range(6))
 
     def one_plane(at, s, p, state):
         passing, total, *colour = state
@@ -378,15 +383,24 @@
         tiled=True,
     ).reshape(depth_count * chunk, 128)
 
+    functions = pl.pallas_call(
+        functools.partial(functions_kernel, 4.0 / (planes * depth_count)),
+        out_shape=f32((6, 8, 128)),
+        in_specs=[smem] * 4,
+        out_specs=vmem,
+        compiler_params=params(),
+        name="functions",
+    )(tf_centre, tf_width, tf_density, tf_tint)
+
     return pl.pallas_call(
-        functools.partial(march_kernel, 4.0 / (planes * depth_count), planes),
+        functools.partial(march_kernel, planes),
         out_shape=f32((8, 4, rows, columns // depth_count)),
-        in_specs=[smem] * 4 + [vmem],
+        in_specs=[vmem] * 2,
         out_specs=vmem,
         scratch_shapes=[pltpu.VMEM((planes, depth_count, 128), jnp.float32)],
         compiler_params=params(),
         name="march",
-    )(tf_centre, tf_width, tf_density, tf_tint, gathered)
+    )(functions, gathered)
 
 
 def solution(mesh):

time: 73.3 us -> 72.7 us (level)
  waiting for transfers between devices: 38.5 us -> 37.3 us
    all_to_all x1, waiting for transfers between devices: 17.5 us -> 16.3 us  [body(): lax.all_to_all(stepped.reshape(depth_count, 1, chunk * 128), 'depth', spl...]
    pallas_call x1 -> x2, Pallas kernels: 2.31 us -> 2.31 us  [the longest x1 1.67 us: body(): pl.pallas_call(functools.partial(march_kernel, planes), out_shape=f32((8,...]
  transfers between devices with their start and end apart: 5 -> 5, of which waited for: 4 -> 4; matrix products, arithmetic and copies ran while one was open for 0% -> 0% of each run, Pallas kernels for 0% -> 1%
where the time goes in v8:
time: 72.7 us; the launch traced here: 72.2 us
  waiting for transfers between devices  37.3 us (51%)
  starting transfers between devices  28.3 us (39%)
  Pallas kernels  5.77 us (8%)
    all_to_all x1, starting transfers between devices, body(): lax.all_to_all(stepped.reshape(depth_count, 1, chunk * 128), 'depth', spl...  17.2 us
    all_to_all x1, waiting for transfers between devices, body(): lax.all_to_all(stepped.reshape(depth_count, 1, chunk * 128), 'depth', spl...  16.3 us
    ppermute x1, waiting for transfers between devices, exchange(): lax.ppermute(to_next, axis, forward)  13.9 us
    ppermute x2, starting transfers between devices, swap(): lax.ppermute(block, axis, forward + [(target, source) for source, target...  5.97 us
    ppermute x1, waiting for transfers between devices, exchange(): lax.ppermute(to_prev, axis, backward)  4.51 us
    ppermute x1, starting transfers between devices, exchange(): lax.ppermute(to_next, axis, forward)  3.83 us
    ppermute x2, waiting for transfers between devices, swap(): lax.ppermute(block, axis, forward + [(target, source) for source, target...  2.59 us
    pallas_call x1, Pallas kernels, body(): pl.pallas_call(step_kernel, out_shape=f32((depth_count * chunk, 128)), in...  2.37 us
  transfers between devices with their start and end apart: 5, of which 4 were waited for; matrix products, arithmetic and copies ran while one was open for 0% of the time, Pallas kernels for 1%

profile of v8, /device:TPU:6, one launch (start us, length us, event | category | flops | bytes accessed | tf_op | source)
XLA Modules:
  0.0 72.2 jit_solution(6351896824477977827)
XLA Ops:
  0.0 0.0 copy-start.4
  0.0 1.0 %pack_planes.1 = (f32[12,8,512]{2,1,0:T(8,128)S(1)}, f32[2,8,512]{2,1,0:T(8,128)S(1)}) custom-call(f32[4,8,512]{2,1,0:T(8,128)} %fuel.5, f32[4,8,512]{2,1,0:T(8,128)} %heat.5, f32[4,8,512]{2,1,0:T(8,128)} %kappa.5, f32[4,8,512]{2,1,0:T(8,128)} %vel_z.5, f32[4,8,512]{2,1,0:T(8,128)} %vel_y.5), custom_call_target="tpu_custom_call" | custom-call | tf_op jit(solution)/shard_map/pack_planes/pallas_call | solution.py:338
  1.0 3.8 %collective-permute-start = (f32[12,8,512]{2,1,0:T(8,128)S(1)}, f32[12,8,512]{2,1,0:T(8,128)S(1)}, u32[]{:S(2)}, u32[]{:S(2)}) collective-permute-start(f32[12,8,512]{2,1,0:T(8,128)S(1)} %get-tuple-element.9), channel_id=1, source_target_pairs={{0,32},{32,64},{64,96},{96,128},{128,160},{160,192},{192,224},{224... | collective-permute-start | bytes 589832 | tf_op jit(solution)/shard_map/ppermute | solution.py:34
  4.8 1.3 %collective-permute-start.1 = (f32[2,8,512]{2,1,0:T(8,128)S(1)}, f32[2,8,512]{2,1,0:T(8,128)S(1)}, u32[]{:S(2)}, u32[]{:S(2)}) collective-permute-start(f32[2,8,512]{2,1,0:T(8,128)S(1)} %get-tuple-element.10), channel_id=1, source_target_pairs={{32,0},{64,32},{96,64},{128,96},{160,128},{192,160},{224,192},{256... | collective-permute-start | bytes 98312 | tf_op jit(solution)/shard_map/ppermute | solution.py:34
  6.1 4.5 %collective-permute-done.1.high = f32[2,8,512]{2,1,0:T(8,128)S(1)} collective-permute-done((f32[2,8,512]{2,1,0:T(8,128)S(1)}, f32[2,8,512]{2,1,0:T(8,128)S(1)}, u32[]{:S(2)}, u32[]{:S(2)}) %collective-permute-start.1) | collective-permute-done | bytes 32800 | tf_op jit(solution)/shard_map/ppermute | solution.py:34
  10.7 13.9 %collective-permute-done.low = f32[12,8,512]{2,1,0:T(8,128)S(1)} collective-permute-done((f32[12,8,512]{2,1,0:T(8,128)S(1)}, f32[12,8,512]{2,1,0:T(8,128)S(1)}, u32[]{:S(2)}, u32[]{:S(2)}) %collective-permute-start) | collective-permute-done | bytes 196640 | tf_op jit(solution)/shard_map/ppermute | solution.py:34
  24.6 0.0 copy-done.2
  24.6 0.1 pack_rows.1
  24.7 4.1 %collective-permute-start.2 = (f32[66,512]{1,0:T(8,128)S(1)}, f32[66,512]{1,0:T(8,128)S(1)}, u32[]{:S(2)}, u32[]{:S(2)}) collective-permute-start(f32[66,512]{1,0:T(8,128)S(1)} %get-tuple-element.11), channel_id=1, source_target_pairs={{1,2},{3,4},{5,6},{7,8},{9,10},{11,12},{13,14},{15,16},{17,18},{19... | collective-permute-start | bytes 405512 | tf_op jit(solution)/shard_map/ppermute | solution.py:40
  28.8 1.9 %collective-permute-start.3 = (f32[66,512]{1,0:T(8,128)S(1)}, f32[66,512]{1,0:T(8,128)S(1)}, u32[]{:S(2)}, u32[]{:S(2)}) collective-permute-start(f32[66,512]{1,0:T(8,128)S(1)} %get-tuple-element.12), channel_id=1, source_target_pairs={{0,1},{2,3},{4,5},{6,7},{8,9},{10,11},{12,13},{14,15},{16,17},{18,... | collective-permute-start | bytes 405512 | tf_op jit(solution)/shard_map/ppermute | solution.py:40
  30.7 2.6 %collective-permute-done.2.outer = f32[66,512]{1,0:T(8,128)S(1)} collective-permute-done((f32[66,512]{1,0:T(8,128)S(1)}, f32[66,512]{1,0:T(8,128)S(1)}, u32[]{:S(2)}, u32[]{:S(2)}) %collective-permute-start.2) | collective-permute-done | bytes 135200 | tf_op jit(solution)/shard_map/ppermute | solution.py:40
  33.3 0.0 collective-permute-done.3.inner
  33.3 2.4 %step.1 = f32[320,128]{1,0:T(8,128)} custom-call(f32[4,8,512]{2,1,0:T(8,128)S(1)} %copy-done, f32[4,8,512]{2,1,0:T(8,128)S(1)} %copy-done.1, f32[4,8,512]{2,1,0:T(8,128)S(1)} %copy-done.2, f32[4,8,512]{2,1,0:T(8,128)S(1)} %copy-done.3, f32[4,8,512]{2,1,0:T(8,128)S(1)} %copy-done.4, f32[12,8,512]{2,1,0:T(8,128)S(1)} %collective-permute-done.low, ...), custom_call_target="tpu_custom_call" | custom-call | tf_op jit(solution)/shard_map/step/pallas_call | solution.py:366
  35.7 17.2 %all-to-all-start = ((f32[32,1,1280]{2,1,0:T(1,128)}), f32[32,1,1280]{2,1,0:T(1,128)S(1)}, u32[]{:S(2)}, u32[]{:S(2)}) async-start(f32[32,1,1280]{2,1,0:T(1,128)} %bitcast), calls=%async_computation | async-start | bytes 327680 | tf_op jit(solution)/shard_map/all_to_all | solution.py:377
  53.0 0.0 copy-start.5
  53.0 0.0 copy-start.6
  53.0 0.0 copy-start.7
  53.0 0.1 copy.11.tint
  53.1 0.5 copy-done.5
  53.6 0.0 copy-done.6
  53.6 0.0 copy-done.7
  53.6 0.6 functions.1
  54.3 16.3 %all-to-all-done = f32[32,1,1280]{2,1,0:T(1,128)S(1)} async-done(((f32[32,1,1280]{2,1,0:T(1,128)}), f32[32,1,1280]{2,1,0:T(1,128)S(1)}, u32[]{:S(2)}, u32[]{:S(2)}) %all-to-all-start) | async-done | bytes 163872 | tf_op jit(solution)/shard_map/all_to_all | solution.py:377
  70.6 1.7 %march.1 = f32[8,4,8,16]{3,2,1,0:T(8,128)} custom-call(f32[6,8,128]{2,1,0:T(8,128)S(1)} %functions.1, f32[320,128]{1,0:T(8,128)S(1)} %bitcast.2), custom_call_target="tpu_custom_call" | custom-call | tf_op jit(solution)/shard_map/march/pallas_call | solution.py:395
  (10 shorter events, 0.0 us)
Async XLA Ops:
  0.0 24.6 %copy-start.1 = (f32[4,8,512]{2,1,0:T(8,128)S(1)}, f32[4,8,512]{2,1,0:T(8,128)}, u32[]{:S(2)}) copy-start(f32[4,8,512]{2,1,0:T(8,128)} %heat.5) | copy-start | bytes 196612
  0.0 24.6 %copy-start.2 = (f32[4,8,512]{2,1,0:T(8,128)S(1)}, f32[4,8,512]{2,1,0:T(8,128)}, u32[]{:S(2)}) copy-start(f32[4,8,512]{2,1,0:T(8,128)} %kappa.5) | copy-start | bytes 196612
  0.0 24.6 %copy-start.3 = (f32[4,8,512]{2,1,0:T(8,128)S(1)}, f32[4,8,512]{2,1,0:T(8,128)}, u32[]{:S(2)}) copy-start(f32[4,8,512]{2,1,0:T(8,128)} %vel_z.5) | copy-start | bytes 196612
  0.0 24.6 %copy-start.4 = (f32[4,8,512]{2,1,0:T(8,128)S(1)}, f32[4,8,512]{2,1,0:T(8,128)}, u32[]{:S(2)}) copy-start(f32[4,8,512]{2,1,0:T(8,128)} %vel_y.5) | copy-start | bytes 196612
  0.0 24.6 %copy-start = (f32[4,8,512]{2,1,0:T(8,128)S(1)}, f32[4,8,512]{2,1,0:T(8,128)}, u32[]{:S(2)}) copy-start(f32[4,8,512]{2,1,0:T(8,128)} %fuel.5) | copy-start | bytes 196612
  1.0 23.6 %collective-permute-start = (f32[12,8,512]{2,1,0:T(8,128)S(1)}, f32[12,8,512]{2,1,0:T(8,128)S(1)}, u32[]{:S(2)}, u32[]{:S(2)}) collective-permute-start(f32[12,8,512]{2,1,0:T(8,128)S(1)} %get-tuple-element.9), channel_id=1, source_target_pairs={{0,32},{32,64},{64,96},{96,128},{128,160},{160,192},{192,224},{224... | collective-permute-start | bytes 589832 | tf_op jit(solution)/shard_map/ppermute | solution.py:34
  4.8 5.8 %collective-permute-start.1 = (f32[2,8,512]{2,1,0:T(8,128)S(1)}, f32[2,8,512]{2,1,0:T(8,128)S(1)}, u32[]{:S(2)}, u32[]{:S(2)}) collective-permute-start(f32[2,8,512]{2,1,0:T(8,128)S(1)} %get-tuple-element.10), channel_id=1, source_target_pairs={{32,0},{64,32},{96,64},{128,96},{160,128},{192,160},{224,192},{256... | collective-permute-start | bytes 98312 | tf_op jit(solution)/shard_map/ppermute | solution.py:34
  24.7 8.6 %collective-permute-start.2 = (f32[66,512]{1,0:T(8,128)S(1)}, f32[66,512]{1,0:T(8,128)S(1)}, u32[]{:S(2)}, u32[]{:S(2)}) collective-permute-start(f32[66,512]{1,0:T(8,128)S(1)} %get-tuple-element.11), channel_id=1, source_target_pairs={{1,2},{3,4},{5,6},{7,8},{9,10},{11,12},{13,14},{15,16},{17,18},{19... | collective-permute-start | bytes 405512 | tf_op jit(solution)/shard_map/ppermute | solution.py:40
  28.8 4.5 %collective-permute-start.3 = (f32[66,512]{1,0:T(8,128)S(1)}, f32[66,512]{1,0:T(8,128)S(1)}, u32[]{:S(2)}, u32[]{:S(2)}) collective-permute-start(f32[66,512]{1,0:T(8,128)S(1)} %get-tuple-element.12), channel_id=1, source_target_pairs={{0,1},{2,3},{4,5},{6,7},{8,9},{10,11},{12,13},{14,15},{16,17},{18,... | collective-permute-start | bytes 405512 | tf_op jit(solution)/shard_map/ppermute | solution.py:40
  35.7 17.3 %copy-start.8 = (f32[8,3]{0,1:T(4,128)S(1)}, f32[8,3]{0,1:T(4,128)}, u32[]{:S(2)}) copy-start(f32[8,3]{0,1:T(4,128)} %param.17) | copy-start | bytes 292
  35.7 34.9 %all-to-all-start = ((f32[32,1,1280]{2,1,0:T(1,128)}), f32[32,1,1280]{2,1,0:T(1,128)S(1)}, u32[]{:S(2)}, u32[]{:S(2)}) async-start(f32[32,1,1280]{2,1,0:T(1,128)} %bitcast), calls=%async_computation | async-start | bytes 327680 | tf_op jit(solution)/shard_map/all_to_all | solution.py:377
  53.0 0.7 copy-start.5
  53.0 0.7 copy-start.6
  53.0 0.7 copy-start.7
